TPU v7x, 128 devices: a whole 4x4x4 slice. The times are simulated.
128 devices in a mesh: panel: 8 (over y, core), blk: 16 (over z, x).
Axes of the slice: x: 4, y: 4, z: 4, core: 2. Of those that a mesh axis runs over, the one named last changes fastest.
Arguments:
- source_flux: bfloat16 [72, 512, 2048], P(None, 'panel', 'blk'), may hold values from -6 to 6
- gauss_weight: float32 [4, 2048, 512], P(None, ('panel', 'blk')), may hold values from 0.02 to 0.2
- gauss_offset: float32 [2, 4, 2048, 512], P(None, None, ('panel', 'blk')), may hold values from -0.5 to 0.5
- slot_count: int32 [2048], P(('panel', 'blk')), may hold values from 1 to 512, as said below
- source_cell: int32 [2048, 512], P(('panel', 'blk')), may hold values from 0 to 8191, as said below
- target_cell: int32 [2048, 512], P(('panel', 'blk')), may hold values from 0 to 4095, as said below
- target_area: float32 [524288], P(('panel', 'blk')), may hold values from 0.25 to 1
Outputs:
- remapped: bfloat16 [72, 524288], P(None, ('panel', 'blk'))
Inputs may be any that keep to these rules, and one draw needn't show every extreme that they name: `slot_count`: live slots from source s to owner k of its band at entry s * size of blk + k; in every draw some owner receives 512 live slots from every source device of its band. `source_cell`: Row-major index of a cell in the sender's block of 64 x 128; slots past the count hold arbitrary cells. `target_cell`: cell index within owner d's 4096 cells; row d * size of blk + k lists the slots from source k of d's band.
All inputs are finite; a program needn't handle non-finite values.
Results may differ from a plain program's by a relative error of at most 0.0044.
The roundings to bfloat16 on the way count: a program that leaves them out, or rounds other values in their place, can miss the bound.
Values may be sent and summed in bfloat16 or wider, within the bound.
No kernel may reach another device: no remote copies, remote signals or barrier semaphores. Data moves between devices by JAX's collectives and lax.ppermute only.
A program may use at most 192 MiB of HBM per device.

v0:
```python
import jax
import jax.numpy as jnp
from jax import lax
from jax.sharding import PartitionSpec as P


def padded(x, sides, width, wrap):
    for axis, dim in sides:
        size, length = (lax.axis_size(axis), x.shape[dim])
        up = [(i, (i + 1) % size) for i in range(size if wrap else size - 1)]
        down = [(j, i) for i, j in up]
        last = lax.slice_in_dim(x, length - width, length, axis=dim)
        first = lax.slice_in_dim(x, 0, width, axis=dim)
        before = lax.ppermute(last, axis, up)
        after = lax.ppermute(first, axis, down)
        x = jnp.concatenate([before, x, after], axis=dim)
    return x


def on_device(
    source_flux, gauss_weight, gauss_offset, slot_count, source_cell, target_cell, target_area
):
    fields, height, breadth = source_flux.shape
    members = lax.axis_size("blk")
    capacity = source_cell.shape[1]
    ocean_cells = target_area.shape[0]
    row_rim = padded(source_flux, (("panel", 1),), 2, False)
    col_rim = padded(source_flux, (("blk", 2),), 2, True)
    center = source_flux.astype(jnp.float32)
    row_parts = [
        row_rim[:, 2 + shift : 2 + shift + height, :].astype(jnp.float32)
        for shift in (-2, -1, 1, 2)
    ]
    col_parts = [
        col_rim[:, :, 2 + shift : 2 + shift + breadth].astype(jnp.float32)
        for shift in (-2, -1, 1, 2)
    ]
    slope_x = (row_parts[0] - 8.0 * row_parts[1] + 8.0 * row_parts[2] - row_parts[3]) / 12.0
    curve_x = (
        -row_parts[0] + 16.0 * row_parts[1] - 30.0 * center + 16.0 * row_parts[2] - row_parts[3]
    ) / 12.0
    slope_y = (col_parts[0] - 8.0 * col_parts[1] + 8.0 * col_parts[2] - col_parts[3]) / 12.0
    curve_y = (
        -col_parts[0] + 16.0 * col_parts[1] - 30.0 * center + 16.0 * col_parts[2] - col_parts[3]
    ) / 12.0
    recon = jnp.stack([center, slope_x, slope_y, curve_x, curve_y]).reshape(
        5, fields, height * breadth
    )
    offset_x = gauss_offset[0]
    offset_y = gauss_offset[1]
    slots = lax.broadcasted_iota(jnp.int32, (members, capacity), 1)
    live_mask = (slots < slot_count[:, None]).astype(jnp.float32)
    moments = (
        jnp.stack(
            [
                jnp.sum(gauss_weight, axis=0),
                jnp.sum(gauss_weight * offset_x, axis=0),
                jnp.sum(gauss_weight * offset_y, axis=0),
                0.5 * jnp.sum(gauss_weight * offset_x * offset_x, axis=0),
                0.5 * jnp.sum(gauss_weight * offset_y * offset_y, axis=0),
            ]
        )
        * live_mask[None]
    )
    picked = jnp.take(recon, source_cell.reshape(-1), axis=2).reshape(5, fields, members, capacity)
    records = jnp.sum(picked * moments[:, None], axis=0).astype(jnp.bfloat16)
    arrived = lax.all_to_all(records, "blk", split_axis=1, concat_axis=1, tiled=True)
    subset = arrived.shape[0]
    by_source = jnp.transpose(arrived, (1, 0, 2))

    def deposit(total, pair):
        values, targets_here = pair
        spread_table = (
            targets_here[:, None] == lax.broadcasted_iota(jnp.int32, (capacity, ocean_cells), 1)
        ).astype(jnp.bfloat16)
        return (total + jnp.dot(values, spread_table, preferred_element_type=jnp.float32), None)

    start = jnp.zeros((subset, ocean_cells), jnp.float32)
    summed, unused = lax.scan(deposit, start, (by_source, target_cell))
    return (summed / target_area[None, :]).astype(jnp.bfloat16)


def solution(mesh):
    placed = (
        P(None, "panel", "blk"),
        P(None, ("panel", "blk"), None),
        P(None, None, ("panel", "blk"), None),
        P(("panel", "blk")),
        P(("panel", "blk"), None),
        P(("panel", "blk"), None),
        P(("panel", "blk")),
    )
    return jax.shard_map(
        on_device, mesh=mesh, in_specs=placed, out_specs=P(None, ("panel", "blk")), check_vma=False
    )
```

profile of v0, /device:TPU:0, one launch (start us, length us, event | category | flops | bytes accessed | tf_op | source)
XLA Modules:
  0.0 346.0 jit_solution(6626236770152206769)
XLA Ops:
  0.0 1.7 fusion.27
  1.7 1.3 collective-permute-start.1
  3.0 3.6 %collective-permute-start = (bf16[72,2,128]{2,1,0:T(2,128)(2,1)}, bf16[72,2,128]{2,1,0:T(2,128)(2,1)}, u32[]{:S(2)}, u32[]{:S(2)}) collective-permute-start(bf16[72,2,128]{2,1,0:T(2,128)(2,1)} %get-tuple-element.70), channel_id=1, source_target_pairs={{0,16},{16,32},{32,48},{48,64},{64,80},{80,96},{96,112},{1,17},{17... | collective-permute-start | bytes 110600 | tf_op jit(solution)/shard_map/ppermute | solution.py:14
  6.6 2.2 fusion.26
  8.8 2.0 copy.37
  10.8 1.6 collective-permute-start.2
  12.4 2.0 copy.38
  14.3 4.7 %collective-permute-start.3 = (bf16[72,64,2]{0,1,2:T(8,128)(2,1)}, bf16[72,64,2]{0,1,2:T(8,128)(2,1)}, u32[]{:S(2)}, u32[]{:S(2)}) collective-permute-start(bf16[72,64,2]{0,1,2:T(8,128)(2,1)} %copy.38), channel_id=1, source_target_pairs={{1,0},{2,1},{3,2},{4,3},{5,4},{6,5},{7,6},{8,7},{9,8},{10,9},{11,1... | collective-permute-start | bytes 55304 | tf_op jit(solution)/shard_map/ppermute | solution.py:15
  19.6 1.5 constant_dynamic-update-slice_fusion.6
  22.6 2.9 copy.34
  25.5 3.6 %copy.30 = bf16[72,64,2]{2,1,0:T(8,128)(2,1)} copy(bf16[72,64,2]{0,1,2:T(8,128)(2,1)} %collective-permute-done.2) | data formatting | bytes 36864 | tf_op jit(solution)/shard_map/ppermute | solution.py:14
  29.1 3.6 %copy.32 = bf16[72,64,2]{2,1,0:T(8,128)(2,1)} copy(bf16[72,64,2]{0,1,2:T(8,128)(2,1)} %collective-permute-done.3) | data formatting | bytes 36864 | tf_op jit(solution)/shard_map/ppermute | solution.py:15
  32.8 9.0 %fusion.18 = (f32[72,64,128]{2,1,0:T(8,128)}, f32[72,64,128]{2,1,0:T(8,128)}) fusion(bf16[72,64,128]{2,1,0:T(8,128)(2,1)S(1)} %copy-done, bf16[72,64,2]{2,1,0:T(8,128)(2,1)} %copy.30, bf16[72,64,2]{2,1,0:T(8,128)(2,1)} %copy.32), kind=kLoop, calls=%fused_computation.38 | loop fusion | flops 23592960 | bytes 5935104 | tf_op jit(solution)/shard_map/div | solution.py:43
  41.8 3.4 stack.34
  45.2 3.4 stack.36
  48.6 0.8 constant_dynamic-update-slice_fusion
  49.4 1.1 copy-done.1
  50.5 5.4 %fusion.12 = (f32[72,64,128]{2,1,0:T(8,128)S(1)}, f32[72,64,128]{2,1,0:T(8,128)}) fusion(bf16[72,64,128]{2,1,0:T(8,128)(2,1)S(1)} %copy-done, bf16[72,66,128]{2,1,0:T(8,128)(2,1)} %copy-done.1, bf16[72,2,128]{2,1,0:T(2,128)(2,1)} %collective-permute-done), kind=kLoop, calls=%fused_computation.32 | loop fusion | flops 17694720 | bytes 8294400 | tf_op jit(solution)/shard_map/div | solution.py:39
  55.9 3.4 stack.33
  59.3 1.8 stack.35
  61.1 3.4 constant_dynamic-update-slice_fusion.5
  64.5 1.6 constant_dynamic-update-slice_fusion.4
  66.1 1.0 copy-done.4
  67.1 1.6 constant_dynamic-update-slice_fusion.3
  68.6 0.9 copy-done.2
  69.6 1.6 constant_dynamic-update-slice_fusion.2
  71.2 21.2 %copy.33 = f32[5,72,8192]{1,0,2:T(8,128)} copy(f32[5,72,8192]{2,1,0:T(8,128)} %constant_dynamic-update-slice_fusion.2) | data formatting | bytes 23592960 | tf_op jit(solution)/shard_map/stack | solution.py:46
  92.3 132.6 %gather_fusion = f32[8192,5,72]{2,1,0:T(8,128)} fusion(f32[5,72,8192]{1,0,2:T(8,128)} %copy.33, s32[8192]{0:T(1024)S(1)} %copy-done.6), kind=kCustom, calls=%fused_computation | custom fusion | bytes 23625728 | tf_op jit(solution)/shard_map/jit(_take)/gather | solution.py:65
  224.9 50.1 %fusion.6 = bf16[72,8192]{0,1:T(8,128)(2,1)S(1)} fusion(f32[8192,5,72]{2,1,0:T(8,128)} %gather_fusion, f32[5,8192]{0,1:T(8,128)} %copy.34, pred[8192]{0:T(1024)(128)(4,1)S(1)} %compare_and_fusion), kind=kLoop, calls=%fused_computation.10 | loop fusion | flops 8257536 | bytes 13148160 | tf_op jit(solution)/shard_map/reduce_sum | solution.py:66
  275.0 1.8 copy.35
  276.8 1.1 copy.49
  277.9 3.7 %all-to-all-start = ((bf16[72,16,512]{2,0,1:T(8,128)(2,1)}), bf16[72,16,512]{2,0,1:T(8,128)(2,1)S(1)}, u32[]{:S(2)}, u32[]{:S(2)}) async-start(bf16[72,16,512]{2,0,1:T(8,128)(2,1)} %bitcast.57), calls=%async_computation | async-start | bytes 2359296 | tf_op jit(solution)/shard_map/all_to_all | solution.py:67
  281.6 20.9 %all-to-all-done = bf16[72,16,512]{2,0,1:T(8,128)(2,1)S(1)} async-done(((bf16[72,16,512]{2,0,1:T(8,128)(2,1)}), bf16[72,16,512]{2,0,1:T(8,128)(2,1)S(1)}, u32[]{:S(2)}, u32[]{:S(2)}) %all-to-all-start) | async-done | bytes 1179680 | tf_op jit(solution)/shard_map/all_to_all | solution.py:67
  302.5 42.6 %while.11 = (s32[]{:T(128)}, f32[72,4096]{1,0:T(8,128)S(1)}, bf16[16,72,512]{2,1,0:T(8,128)(2,1)S(1)}, s32[16,512]{1,0:T(8,128)}, s32[]{:T(128)}, /*index=5*/s32[]{:T(128)}) while((s32[]{:T(128)}, f32[72,4096]{1,0:T(8,128)S(1)}, bf16[16,72,512]{2,1,0:T(8,128)(2,1)S(1)}, s32[16,512]{1,0:T(8,128)}, s32[]{:T(128)}, ...), condition=%wide.region_7.8_spmd.clone, body=%wide.region_6.7_spmd.clone.sunk | while | flops 304676864 | bytes 2439263 | solution.py:79
  302.5 0.7 constant_dynamic-slice_fusion.2
  303.2 1.9 fusion.31
  305.2 0.7 constant_dynamic-slice_fusion.2
  305.9 1.9 fusion.31
  307.8 0.7 constant_dynamic-slice_fusion.2
  308.6 1.9 fusion.31
  310.5 0.7 constant_dynamic-slice_fusion.2
  311.2 1.9 fusion.31
  313.2 0.7 constant_dynamic-slice_fusion.2
  313.9 1.9 fusion.31
  315.8 0.7 constant_dynamic-slice_fusion.2
  316.5 1.9 fusion.31
  318.5 0.7 constant_dynamic-slice_fusion.2
  319.2 1.9 fusion.31
  321.1 0.7 constant_dynamic-slice_fusion.2
  321.9 1.9 fusion.31
  323.8 0.7 constant_dynamic-slice_fusion.2
  324.5 1.9 fusion.31
  326.5 0.7 constant_dynamic-slice_fusion.2
  327.2 1.9 fusion.31
  329.1 0.7 constant_dynamic-slice_fusion.2
  329.9 1.9 fusion.31
  331.8 0.7 constant_dynamic-slice_fusion.2
  332.5 1.9 fusion.31
  334.4 0.7 constant_dynamic-slice_fusion.2
  335.2 1.9 fusion.31
  337.8 1.9 fusion.31
  340.5 1.9 fusion.31
  343.2 1.9 fusion.31
  345.1 0.9 divide_convert_fusion
  (45 shorter events, 4.1 us)
Async XLA Ops:
  1.7 46.9 %collective-permute-start.1 = (bf16[72,2,128]{2,1,0:T(2,128)(2,1)}, bf16[72,2,128]{2,1,0:T(2,128)(2,1)}, u32[]{:S(2)}, u32[]{:S(2)}) collective-permute-start(bf16[72,2,128]{2,1,0:T(2,128)(2,1)} %get-tuple-element.71), channel_id=1, source_target_pairs={{16,0},{32,16},{48,32},{64,48},{80,64},{96,80},{112,96},{17,1},{33... | collective-permute-start | bytes 110600 | tf_op jit(solution)/shard_map/ppermute | solution.py:15
  3.0 47.5 %collective-permute-start = (bf16[72,2,128]{2,1,0:T(2,128)(2,1)}, bf16[72,2,128]{2,1,0:T(2,128)(2,1)}, u32[]{:S(2)}, u32[]{:S(2)}) collective-permute-start(bf16[72,2,128]{2,1,0:T(2,128)(2,1)} %get-tuple-element.70), channel_id=1, source_target_pairs={{0,16},{16,32},{32,48},{48,64},{64,80},{80,96},{96,112},{1,17},{17... | collective-permute-start | bytes 110600 | tf_op jit(solution)/shard_map/ppermute | solution.py:14
  8.8 10.3 %copy-start = (bf16[72,64,128]{2,1,0:T(8,128)(2,1)S(1)}, bf16[72,64,128]{2,1,0:T(8,128)(2,1)}, u32[]{:S(2)}) copy-start(bf16[72,64,128]{2,1,0:T(8,128)(2,1)} %param.9) | copy-start | bytes 3538948
  10.8 14.7 %collective-permute-start.2 = (bf16[72,64,2]{0,1,2:T(8,128)(2,1)}, bf16[72,64,2]{0,1,2:T(8,128)(2,1)}, u32[]{:S(2)}, u32[]{:S(2)}) collective-permute-start(bf16[72,64,2]{0,1,2:T(8,128)(2,1)} %copy.37), channel_id=1, source_target_pairs={{0,1},{1,2},{2,3},{3,4},{4,5},{5,6},{6,7},{7,8},{8,9},{9,10},{10,1... | collective-permute-start | bytes 55304 | tf_op jit(solution)/shard_map/ppermute | solution.py:14
  14.3 14.8 %collective-permute-start.3 = (bf16[72,64,2]{0,1,2:T(8,128)(2,1)}, bf16[72,64,2]{0,1,2:T(8,128)(2,1)}, u32[]{:S(2)}, u32[]{:S(2)}) collective-permute-start(bf16[72,64,2]{0,1,2:T(8,128)(2,1)} %copy.38), channel_id=1, source_target_pairs={{1,0},{2,1},{3,2},{4,3},{5,4},{6,5},{7,6},{8,7},{9,8},{10,9},{11,1... | collective-permute-start | bytes 55304 | tf_op jit(solution)/shard_map/ppermute | solution.py:15
  19.5 1.6 copy-start.8
  19.6 2.3 copy-start.5
  19.6 2.3 copy-start.7
  19.6 2.5 copy-start.10
  49.4 1.1 copy-start.1
  61.1 3.4 copy-start.3
  64.5 2.5 copy-start.4
  67.1 2.5 copy-start.2
  71.2 21.2 %copy-start.6 = (s32[8192]{0:T(1024)S(1)}, s32[8192]{0:T(1024)}, u32[]{:S(2)}) copy-start(s32[8192]{0:T(1024)} %broadcast_clamp_fusion) | copy-start | bytes 98308
  277.9 24.6 %all-to-all-start = ((bf16[72,16,512]{2,0,1:T(8,128)(2,1)}), bf16[72,16,512]{2,0,1:T(8,128)(2,1)S(1)}, u32[]{:S(2)}, u32[]{:S(2)}) async-start(bf16[72,16,512]{2,0,1:T(8,128)(2,1)} %bitcast.57), calls=%async_computation | async-start | bytes 2359296 | tf_op jit(solution)/shard_map/all_to_all | solution.py:67
  302.5 42.6 %copy-start.9 = (f32[4096]{0:T(1024)S(1)}, f32[4096]{0:T(1024)}, u32[]{:S(2)}) copy-start(f32[4096]{0:T(1024)} %param.15) | copy-start | bytes 49156
where the time goes:
time: 352 us; the launch traced here: 346 us
  local copies, waits for them, and re-layouts  213 us (61%)
  other arithmetic  66.3 us (19%)
  matrix products  30.6 us (9%)
  waiting for transfers between devices  20.9 us (6%)
  starting transfers between devices  14.9 us (4%)
    gather x1, local copies, waits for them, and re-layouts, on_device(): jnp.take(recon, source_cell.reshape(-1), axis=2)  133 us
    reduce_sum x1, other arithmetic, on_device(): records = jnp.sum(picked * moments[:, None], axis=0).astype(jnp.bfloat16)  50.1 us
    another operation x7, local copies, waits for them, and re-layouts, on_device(): jnp.stack([center, slope_x, slope_y, curve_x, curve_y])  35.1 us
    dot_general x16, matrix products, deposit(): jnp.dot(values, spread_table, preferred_element_type=jnp.float32)  30.6 us
    all_to_all x1, waiting for transfers between devices, on_device(): lax.all_to_all(records, 'blk', split_axis=1, concat_axis=1, tiled=True)  20.9 us
    unnamed x37, local copies, waits for them, and re-layouts  15.4 us
    dynamic_slice x16, local copies, waits for them, and re-layouts, on_device(): summed, unused = lax.scan(deposit, start, (by_source, target_cell))  11.6 us
    div x1, other arithmetic, on_device(): (-col_parts[0] + 16.0 * col_parts[1] - 30.0 * center + 16.0 * col_parts[2...  9.05 us
  transfers between devices with their start and end apart: 5, of which 1 were waited for; matrix products, arithmetic and copies ran while one was open for 10% of the time, Pallas kernels for 0%

commit v1 on v0

v1 whole, which is shorter than its diff:
```python
import functools

import jax
import jax.numpy as jnp
from jax import lax
from jax.experimental import pallas as pl
from jax.experimental.pallas import tpu as pltpu
from jax.sharding import PartitionSpec as P

GROUP = 8
REACH = 2
LOW = 256
TERMS = 16


def record_body(window_ref, rim_ref, term_ref, out_ref, *, fields, height, breadth):
    groups = height // GROUP
    span = GROUP + 2 * REACH
    terms = term_ref[0]
    slots = terms.shape[1]
    scale = terms[0:1]
    row_taps = [terms[1 + i : 2 + i] for i in range(4)]
    col_taps = [terms[5 + i : 6 + i] for i in range(4)]
    row = terms[9:10].astype(jnp.int32)
    col = terms[10:11].astype(jnp.int32)
    shifts = (-2, -1, 1, 2)
    group = row // GROUP
    local = row - group * GROUP + REACH
    gap = lax.broadcasted_iota(jnp.int32, (breadth, slots), 0) - col
    here = jnp.where(gap == 0, 1.0, 0.0).astype(jnp.bfloat16)
    beside = jnp.zeros((breadth, slots), jnp.float32)
    for shift, tap in zip(shifts, col_taps):
        beside = jnp.where(gap == shift, tap, beside)
    beside = beside.astype(jnp.bfloat16)
    pieces = []
    for j in range(span):
        centre = jnp.where(local == j, 1.0, 0.0)
        weight = centre
        for shift, tap in zip(shifts, row_taps):
            weight = jnp.where(local + shift == j, tap, weight)
        pieces.append(
            here * weight.astype(jnp.bfloat16) + beside * centre.astype(jnp.bfloat16)
        )
    table = jnp.concatenate(pieces, axis=0)
    product = jnp.dot(window_ref[...], table, preferred_element_type=jnp.float32)
    same_row = jnp.where(
        lax.broadcasted_iota(jnp.int32, (height, slots), 0) == row, 1.0, 0.0
    ).astype(jnp.bfloat16)
    rim_pieces = []
    for place in (-2, -1, breadth, breadth + 1):
        weight = jnp.zeros((1, slots), jnp.float32)
        for shift, tap in zip(shifts, col_taps):
            weight = jnp.where(col + shift == place, tap, weight)
        rim_pieces.append(same_row * weight.astype(jnp.bfloat16))
    total = jnp.dot(
        rim_ref[...], jnp.concatenate(rim_pieces, axis=0), preferred_element_type=jnp.float32
    )
    for g in range(groups):
        total = total + jnp.where(group == g, product[g * fields : (g + 1) * fields], 0.0)
    out_ref[0] = (total * scale).astype(jnp.bfloat16)


def deposit_body(record_ref, target_ref, area_ref, out_ref, total_ref, *, fields, cells):
    step = pl.program_id(0)
    highs = cells // LOW
    target = target_ref[0]
    capacity = target.shape[1]
    high = target // LOW
    low = target - high * LOW
    values = record_ref[0].astype(jnp.float32)
    spread = jnp.concatenate(
        [jnp.where(high == h, values, 0.0) for h in range(highs)], axis=0
    ).astype(jnp.bfloat16)
    place = jnp.where(
        lax.broadcasted_iota(jnp.int32, (LOW, capacity), 0) == low, 1.0, 0.0
    ).astype(jnp.bfloat16)
    part = lax.dot_general(
        spread, place, (((1,), (1,)), ((), ())), preferred_element_type=jnp.float32
    )

    @pl.when(step == 0)
    def first():
        total_ref[...] = part

    @pl.when(step > 0)
    def later():
        total_ref[...] = total_ref[...] + part

    @pl.when(step == pl.num_programs(0) - 1)
    def finish():
        for h in range(highs):
            area = area_ref[:, h * LOW : (h + 1) * LOW]
            out_ref[:, h * LOW : (h + 1) * LOW] = (
                total_ref[h * fields : (h + 1) * fields, :] / area
            ).astype(jnp.bfloat16)


def neighbours(first, last, axis, wrap):
    size = lax.axis_size(axis)
    up = [(i, (i + 1) % size) for i in range(size if wrap else size - 1)]
    down = [(j, i) for i, j in up]
    return (lax.ppermute(last, axis, up), lax.ppermute(first, axis, down))


def on_device(
    source_flux, gauss_weight, gauss_offset, slot_count, source_cell, target_cell, target_area
):
    fields, height, breadth = source_flux.shape
    members = lax.axis_size("blk")
    capacity = source_cell.shape[1]
    cells = target_area.shape[0]
    groups = height // GROUP
    span = GROUP + 2 * REACH
    above, below = neighbours(
        source_flux[:, :REACH], source_flux[:, height - REACH :], "panel", False
    )
    flat = lambda part: jnp.swapaxes(part, 1, 2).reshape(fields, REACH * height)
    before, after = neighbours(
        flat(source_flux[:, :, :REACH]), flat(source_flux[:, :, breadth - REACH :]), "blk", True
    )
    rim = jnp.concatenate([before, after], axis=1)
    tall = jnp.concatenate([above, source_flux, below], axis=1)
    window = jnp.stack([tall[:, g * GROUP : g * GROUP + span] for g in range(groups)]).reshape(
        groups * fields, span * breadth
    )
    offset_x = gauss_offset[0]
    offset_y = gauss_offset[1]
    slots = lax.broadcasted_iota(jnp.int32, (members, capacity), 1)
    live = (slots < slot_count[:, None]).astype(jnp.float32)
    area = jnp.sum(gauss_weight, axis=0)
    first_x = jnp.sum(gauss_weight * offset_x, axis=0)
    first_y = jnp.sum(gauss_weight * offset_y, axis=0)
    second_x = 0.5 * jnp.sum(gauss_weight * offset_x * offset_x, axis=0)
    second_y = 0.5 * jnp.sum(gauss_weight * offset_y * offset_y, axis=0)
    centre = area - 2.5 * (second_x + second_y)
    inverse = 1.0 / (12.0 * centre)
    taps = []
    for one, two in ((first_x, second_x), (first_y, second_y)):
        taps += [
            (one - two) * inverse,
            (16.0 * two - 8.0 * one) * inverse,
            (16.0 * two + 8.0 * one) * inverse,
            (-one - two) * inverse,
        ]
    row = source_cell // breadth
    col = source_cell - row * breadth
    terms = [centre * live] + taps + [row.astype(jnp.float32), col.astype(jnp.float32)]
    terms += [jnp.zeros_like(area)] * (TERMS - len(terms))
    terms = jnp.stack(terms, axis=1)
    records = pl.pallas_call(
        functools.partial(record_body, fields=fields, height=height, breadth=breadth),
        grid=(members,),
        in_specs=[
            pl.BlockSpec((groups * fields, span * breadth), lambda i: (0, 0)),
            pl.BlockSpec((fields, 2 * REACH * height), lambda i: (0, 0)),
            pl.BlockSpec((1, TERMS, capacity), lambda i: (i, 0, 0)),
        ],
        out_specs=pl.BlockSpec((1, fields, capacity), lambda i: (i, 0, 0)),
        out_shape=jax.ShapeDtypeStruct((members, fields, capacity), jnp.bfloat16),
        name="records",
    )(window, rim, terms)
    arrived = lax.all_to_all(records, "blk", split_axis=0, concat_axis=0, tiled=True)
    return pl.pallas_call(
        functools.partial(deposit_body, fields=fields, cells=cells),
        grid=(members,),
        in_specs=[
            pl.BlockSpec((1, fields, capacity), lambda i: (i, 0, 0)),
            pl.BlockSpec((1, 1, capacity), lambda i: (i, 0, 0)),
            pl.BlockSpec((1, cells), lambda i: (0, 0)),
        ],
        out_specs=pl.BlockSpec((fields, cells), lambda i: (0, 0)),
        out_shape=jax.ShapeDtypeStruct((fields, cells), jnp.bfloat16),
        scratch_shapes=[pltpu.VMEM((cells // LOW * fields, LOW), jnp.float32)],
        name="deposit",
    )(arrived, target_cell.reshape(members, 1, capacity), target_area.reshape(1, cells))


def solution(mesh):
    placed = (
        P(None, "panel", "blk"),
        P(None, ("panel", "blk"), None),
        P(None, None, ("panel", "blk"), None),
        P(("panel", "blk")),
        P(("panel", "blk"), None),
        P(("panel", "blk"), None),
        P(("panel", "blk")),
    )
    return jax.shard_map(
        on_device, mesh=mesh, in_specs=placed, out_specs=P(None, ("panel", "blk")), check_vma=False
    )
```

time: 352 us -> 91.8 us (0.26)
  the two profiles are of different devices: /device:TPU:0 before, /device:TPU:1 now
where the time goes in v1:
time: 91.8 us; the launch traced here: 90.9 us
  Pallas kernels  37.8 us (41%)
  waiting for transfers between devices  24.1 us (26%)
  starting transfers between devices  16.3 us (18%)
  local copies, waits for them, and re-layouts  11.1 us (12%)
  other arithmetic  1.31 us (1%)
    pallas_call x1, Pallas kernels, on_device(): pl.pallas_call(functools.partial(record_body, fields=fields, height=heigh...  23.8 us
    all_to_all x1, waiting for transfers between devices, on_device(): lax.all_to_all(records, 'blk', split_axis=0, concat_axis=0, tiled=True)  21 us
    pallas_call x1, Pallas kernels, on_device(): pl.pallas_call(functools.partial(deposit_body, fields=fields, cells=cells...  14 us
    ppermute x4, starting transfers between devices, neighbours(): return (lax.ppermute(last, axis, up), lax.ppermute(first, axis, down))  12.6 us
    all_to_all x1, starting transfers between devices, on_device(): lax.all_to_all(records, 'blk', split_axis=0, concat_axis=0, tiled=True)  3.7 us
    unnamed x21, local copies, waits for them, and re-layouts  3.56 us
    transpose x3, local copies, waits for them, and re-layouts, on_device(): flat = lambda part: jnp.swapaxes(part, 1, 2).reshape(fields, REACH * height)  3.37 us
    ppermute x4, waiting for transfers between devices, neighbours(): return (lax.ppermute(last, axis, up), lax.ppermute(first, axis, down))  3.11 us
  transfers between devices with their start and end apart: 5, of which 2 were waited for; matrix products, arithmetic and copies ran while one was open for 9% of the time, Pallas kernels for 0%

profile of v1, /device:TPU:1, one launch (start us, length us, event | category | flops | bytes accessed | tf_op | source)
XLA Modules:
  0.0 90.9 jit_solution(7140507897404750511)
XLA Ops:
  0.0 1.0 %fusion.19 = (bf16[72,2,128]{2,1,0:T(2,128)(2,1)S(1)}, bf16[72,2,128]{2,1,0:T(2,128)(2,1)S(1)}) fusion(bf16[72,64,128]{2,1,0:T(8,128)(2,1)} %param.7), kind=kLoop, calls=%fused_computation.57 | loop fusion | bytes 147456 | tf_op jit(solution)/shard_map/slice | solution.py:115
  1.0 4.6 %collective-permute-start = (bf16[72,2,128]{2,1,0:T(2,128)(2,1)S(1)}, bf16[72,2,128]{2,1,0:T(2,128)(2,1)S(1)}, u32[]{:S(2)}, u32[]{:S(2)}) collective-permute-start(bf16[72,2,128]{2,1,0:T(2,128)(2,1)S(1)} %get-tuple-element.17), channel_id=1, source_target_pairs={{0,16},{16,32},{32,48},{48,64},{64,80},{80,96},{96,112},{1,17},{17... | collective-permute-start | bytes 110600 | tf_op jit(solution)/shard_map/ppermute | solution.py:102
  5.7 1.9 %collective-permute-start.1 = (bf16[72,2,128]{2,1,0:T(2,128)(2,1)S(1)}, bf16[72,2,128]{2,1,0:T(2,128)(2,1)S(1)}, u32[]{:S(2)}, u32[]{:S(2)}) collective-permute-start(bf16[72,2,128]{2,1,0:T(2,128)(2,1)S(1)} %get-tuple-element.16), channel_id=1, source_target_pairs={{16,0},{32,16},{48,32},{64,48},{80,64},{96,80},{112,96},{17,1},{33... | collective-permute-start | bytes 110600 | tf_op jit(solution)/shard_map/ppermute | solution.py:102
  7.6 2.4 %slice_bitcast_fusion.1 = (bf16[72,2,64]{1,2,0:T(8,128)(2,1)S(1)}, bf16[72,2,64]{1,2,0:T(8,128)(2,1)S(1)}) fusion(bf16[72,64,128]{2,1,0:T(8,128)(2,1)} %param.7), kind=kLoop, calls=%fused_computation.2 | loop fusion | bytes 73728 | tf_op jit(solution)/shard_map/transpose | solution.py:117
  10.0 0.0 copy-start.2
  10.0 0.0 copy-start.3
  10.0 0.0 copy-start.6
  10.0 0.0 copy-start.4
  10.0 0.5 copy.37
  10.5 0.1 reshape.280
  10.6 0.0 copy-start
  10.6 6.0 %collective-permute-start.3 = (bf16[72,128]{1,0:T(8,128)(2,1)S(1)}, bf16[72,128]{1,0:T(8,128)(2,1)S(1)}, u32[]{:S(2)}, u32[]{:S(2)}) collective-permute-start(bf16[72,128]{1,0:T(8,128)(2,1)S(1)} %reshape.280), channel_id=1, source_target_pairs={{1,0},{2,1},{3,2},{4,3},{5,4},{6,5},{7,6},{8,7},{9,8},{10,9},{11,1... | collective-permute-start | bytes 55304 | tf_op jit(solution)/shard_map/ppermute | solution.py:102
  16.6 0.5 copy.36
  17.1 0.1 reshape.279
  17.2 0.1 collective-permute-start.2
  17.3 0.0 copy-done.2
  17.3 0.0 copy-done.3
  17.4 0.0 copy-done.6
  17.4 0.1 compare_select_fusion
  17.5 0.1 copy_multiply_fusion
  17.6 0.1 add_multiply_fusion
  17.7 0.0 copy-done.4
  18.1 2.0 %stack.60.term_ref = f32[16,16,512]{2,1,0:T(8,128)} concatenate(f32[16,1,512]{2,1,0:T(1,128)S(1)} %compare_select_fusion, f32[16,1,512]{2,1,0:T(1,128)S(1)} %copy.48, f32[16,1,512]{2,1,0:T(1,128)S(1)} %copy.49, f32[16,1,512]{2,1,0:T(1,128)S(1)} %copy.50, f32[16,1,512]{2,1,0:T(1,128)S(1)} %copy.51, f32[16,1,512]{2,1,0:T(1,128)S(1)} %copy.52, f32[16,1,512]{2,1,0:T(1,128)S(1)} %get-tuple-element.19, ...), dimensions={1} | concatenate | bytes 1048576 | tf_op jit(solution)/shard_map/stack | solution.py:149
  20.1 0.0 collective-permute-done.3
  20.1 3.1 %collective-permute-done.2 = bf16[72,128]{1,0:T(8,128)(2,1)S(1)} collective-permute-done((bf16[72,128]{1,0:T(8,128)(2,1)S(1)}, bf16[72,128]{1,0:T(8,128)(2,1)S(1)}, u32[]{:S(2)}, u32[]{:S(2)}) %collective-permute-start.2) | collective-permute-done | bytes 18464 | tf_op jit(solution)/shard_map/ppermute | solution.py:102
  23.2 0.6 pad_maximum_fusion.2.rim_ref
  23.9 0.0 collective-permute-done
  23.9 0.0 copy-done
  23.9 0.1 fusion.3
  24.0 0.1 bitcast_dynamic-update-slice_fusion.5
  24.1 0.1 bitcast_dynamic-update-slice_fusion.4
  24.3 0.1 bitcast_dynamic-update-slice_fusion.3
  24.4 0.1 bitcast_dynamic-update-slice_fusion.2
  24.5 0.1 bitcast_dynamic-update-slice_fusion.1
  24.7 0.1 bitcast_dynamic-update-slice_fusion
  24.8 0.0 collective-permute-done.1
  24.8 0.2 fusion.1
  25.0 1.7 %copy.70 = bf16[72,8,12,128]{3,1,2,0:T(8,128)(2,1)} copy(bf16[72,8,12,128]{3,2,1,0:T(8,128)(2,1)S(1)} %bitcast.94) | data formatting | bytes 3538944
  26.7 0.0 copy-start.5
  26.7 23.8 %records.1 = bf16[16,72,512]{2,1,0:T(8,128)(2,1)} custom-call(bf16[576,1536]{1,0:T(8,128)(2,1)} %bitcast.93, bf16[72,256]{1,0:T(8,128)(2,1)} %pad_maximum_fusion.2.rim_ref, f32[16,16,512]{2,1,0:T(8,128)} %stack.60.term_ref), custom_call_target="tpu_custom_call" | custom-call | tf_op jit(solution)/shard_map/records/pallas_call | solution.py:150
  50.6 3.7 %all-to-all-start = ((bf16[16,72,512]{2,1,0:T(8,128)(2,1)}), bf16[16,72,512]{2,1,0:T(8,128)(2,1)S(1)}, u32[]{:S(2)}, u32[]{:S(2)}) async-start(bf16[16,72,512]{2,1,0:T(8,128)(2,1)} %records.1), calls=%async_computation | async-start | bytes 2359296 | tf_op jit(solution)/shard_map/all_to_all | solution.py:162
  54.3 0.0 copy-done.5
  54.3 0.6 reshape.281.target_ref
  54.9 21.0 %all-to-all-done.record_ref = bf16[16,72,512]{2,1,0:T(8,128)(2,1)S(1)} async-done(((bf16[16,72,512]{2,1,0:T(8,128)(2,1)}), bf16[16,72,512]{2,1,0:T(8,128)(2,1)S(1)}, u32[]{:S(2)}, u32[]{:S(2)}) %all-to-all-start) | async-done | bytes 1179680 | tf_op jit(solution)/shard_map/all_to_all | solution.py:162
  75.9 0.0 copy-start.1
  75.9 1.0 %copy-done.1 = bf16[16,72,512]{2,1,0:T(8,128)(2,1)} copy-done((bf16[16,72,512]{2,1,0:T(8,128)(2,1)}, bf16[16,72,512]{2,1,0:T(8,128)(2,1)S(1)}, u32[]{:S(2)}) %copy-start.1) | copy-done | bytes 1179672
  76.9 14.0 %deposit.1 = bf16[72,4096]{1,0:T(8,128)(2,1)} custom-call(bf16[16,72,512]{2,1,0:T(8,128)(2,1)} %copy-done.1, s32[16,1,512]{2,1,0:T(1,128)} %reshape.281.target_ref, f32[1,4096]{1,0:T(1,128)} %bitcast.96), custom_call_target="tpu_custom_call" | custom-call | tf_op jit(solution)/shard_map/deposit/pallas_call | solution.py:163
  (14 shorter events, 0.4 us)
Async XLA Ops:
  1.0 22.8 %collective-permute-start = (bf16[72,2,128]{2,1,0:T(2,128)(2,1)S(1)}, bf16[72,2,128]{2,1,0:T(2,128)(2,1)S(1)}, u32[]{:S(2)}, u32[]{:S(2)}) collective-permute-start(bf16[72,2,128]{2,1,0:T(2,128)(2,1)S(1)} %get-tuple-element.17), channel_id=1, source_target_pairs={{0,16},{16,32},{32,48},{48,64},{64,80},{80,96},{96,112},{1,17},{17... | collective-permute-start | bytes 110600 | tf_op jit(solution)/shard_map/ppermute | solution.py:102
  5.7 19.1 %collective-permute-start.1 = (bf16[72,2,128]{2,1,0:T(2,128)(2,1)S(1)}, bf16[72,2,128]{2,1,0:T(2,128)(2,1)S(1)}, u32[]{:S(2)}, u32[]{:S(2)}) collective-permute-start(bf16[72,2,128]{2,1,0:T(2,128)(2,1)S(1)} %get-tuple-element.16), channel_id=1, source_target_pairs={{16,0},{32,16},{48,32},{64,48},{80,64},{96,80},{112,96},{17,1},{33... | collective-permute-start | bytes 110600 | tf_op jit(solution)/shard_map/ppermute | solution.py:102
  10.0 7.4 %copy-start.2 = (f32[2,4,16,512]{3,2,1,0:T(8,128)S(1)}, f32[2,4,16,512]{3,2,1,0:T(8,128)}, u32[]{:S(2)}) copy-start(f32[2,4,16,512]{3,2,1,0:T(8,128)} %param.9) | copy-start | bytes 786436
  10.0 7.4 %copy-start.3 = (f32[4,16,512]{2,1,0:T(8,128)S(1)}, f32[4,16,512]{2,1,0:T(8,128)}, u32[]{:S(2)}) copy-start(f32[4,16,512]{2,1,0:T(8,128)} %param.8) | copy-start | bytes 393220
  10.0 7.4 %copy-start.6 = (s32[16]{0:T(128)S(1)}, s32[16]{0:T(128)}, u32[]{:S(2)}) copy-start(s32[16]{0:T(128)} %param.10) | copy-start | bytes 196
  10.0 7.7 %copy-start.4 = (s32[16,512]{1,0:T(8,128)S(1)}, s32[16,512]{1,0:T(8,128)}, u32[]{:S(2)}) copy-start(s32[16,512]{1,0:T(8,128)} %param.11) | copy-start | bytes 98308
  10.6 13.3 %copy-start = (bf16[72,64,128]{2,1,0:T(8,128)(2,1)S(1)}, bf16[72,64,128]{2,1,0:T(8,128)(2,1)}, u32[]{:S(2)}) copy-start(bf16[72,64,128]{2,1,0:T(8,128)(2,1)} %param.7) | copy-start | bytes 3538948
  10.6 9.5 %collective-permute-start.3 = (bf16[72,128]{1,0:T(8,128)(2,1)S(1)}, bf16[72,128]{1,0:T(8,128)(2,1)S(1)}, u32[]{:S(2)}, u32[]{:S(2)}) collective-permute-start(bf16[72,128]{1,0:T(8,128)(2,1)S(1)} %reshape.280), channel_id=1, source_target_pairs={{1,0},{2,1},{3,2},{4,3},{5,4},{6,5},{7,6},{8,7},{9,8},{10,9},{11,1... | collective-permute-start | bytes 55304 | tf_op jit(solution)/shard_map/ppermute | solution.py:102
  17.2 6.0 %collective-permute-start.2 = (bf16[72,128]{1,0:T(8,128)(2,1)S(1)}, bf16[72,128]{1,0:T(8,128)(2,1)S(1)}, u32[]{:S(2)}, u32[]{:S(2)}) collective-permute-start(bf16[72,128]{1,0:T(8,128)(2,1)S(1)} %reshape.279), channel_id=1, source_target_pairs={{0,1},{1,2},{2,3},{3,4},{4,5},{5,6},{6,7},{7,8},{8,9},{9,10},{10,1... | collective-permute-start | bytes 55304 | tf_op jit(solution)/shard_map/ppermute | solution.py:102
  26.7 27.6 %copy-start.5 = (s32[16,512]{1,0:T(8,128)S(1)}, s32[16,512]{1,0:T(8,128)}, u32[]{:S(2)}) copy-start(s32[16,512]{1,0:T(8,128)} %param.12) | copy-start | bytes 98308
  50.6 25.4 %all-to-all-start = ((bf16[16,72,512]{2,1,0:T(8,128)(2,1)}), bf16[16,72,512]{2,1,0:T(8,128)(2,1)S(1)}, u32[]{:S(2)}, u32[]{:S(2)}) async-start(bf16[16,72,512]{2,1,0:T(8,128)(2,1)} %records.1), calls=%async_computation | async-start | bytes 2359296 | tf_op jit(solution)/shard_map/all_to_all | solution.py:162
  75.9 1.0 %copy-start.1 = (bf16[16,72,512]{2,1,0:T(8,128)(2,1)}, bf16[16,72,512]{2,1,0:T(8,128)(2,1)S(1)}, u32[]{:S(2)}) copy-start(bf16[16,72,512]{2,1,0:T(8,128)(2,1)S(1)} %all-to-all-done.record_ref) | copy-start | bytes 3538948

commit v2 on v1

v2 whole, which is shorter than its diff:
```python
import functools

import jax
import jax.numpy as jnp
from jax import lax
from jax.experimental import pallas as pl
from jax.experimental.pallas import tpu as pltpu
from jax.sharding import PartitionSpec as P

GROUP = 8
REACH = 2
LOW = 256
TERMS = 16
BATCH = 8


def record_body(
    count_ref, window_ref, rim_ref, term_ref, out_ref, *, fields, height, breadth, start
):
    groups = height // GROUP
    span = GROUP + 2 * REACH
    alive = count_ref[pl.program_id(0)] > start

    @pl.when(alive)
    def compute():
        terms = term_ref[0]
        slots = terms.shape[1]
        scale = terms[0:1]
        row_taps = [terms[1 + i : 2 + i] for i in range(4)]
        col_taps = [terms[5 + i : 6 + i] for i in range(4)]
        row = terms[9:10].astype(jnp.int32)
        col = terms[10:11].astype(jnp.int32)
        shifts = (-2, -1, 1, 2)
        group = row // GROUP
        local = row - group * GROUP + REACH
        gap = lax.broadcasted_iota(jnp.int32, (breadth, slots), 0) - col
        here = jnp.where(gap == 0, 1.0, 0.0).astype(jnp.bfloat16)
        beside = jnp.zeros((breadth, slots), jnp.float32)
        for shift, tap in zip(shifts, col_taps):
            beside = jnp.where(gap == shift, tap, beside)
        beside = beside.astype(jnp.bfloat16)
        pieces = []
        for j in range(span):
            centre = jnp.where(local == j, 1.0, 0.0)
            weight = centre
            for shift, tap in zip(shifts, row_taps):
                weight = jnp.where(local + shift == j, tap, weight)
            pieces.append(
                here * weight.astype(jnp.bfloat16) + beside * centre.astype(jnp.bfloat16)
            )
        table = jnp.concatenate(pieces, axis=0)
        product = jnp.dot(window_ref[...], table, preferred_element_type=jnp.float32)
        same_row = jnp.where(
            lax.broadcasted_iota(jnp.int32, (height, slots), 0) == row, 1.0, 0.0
        ).astype(jnp.bfloat16)
        rim_pieces = []
        for place in (-2, -1, breadth, breadth + 1):
            weight = jnp.zeros((1, slots), jnp.float32)
            for shift, tap in zip(shifts, col_taps):
                weight = jnp.where(col + shift == place, tap, weight)
            rim_pieces.append(same_row * weight.astype(jnp.bfloat16))
        total = jnp.dot(
            rim_ref[...], jnp.concatenate(rim_pieces, axis=0), preferred_element_type=jnp.float32
        )
        for g in range(groups):
            total = total + jnp.where(group == g, product[g * fields : (g + 1) * fields], 0.0)
        out_ref[0] = (total * scale).astype(jnp.bfloat16)

    @pl.when(jnp.logical_not(alive))
    def clear():
        out_ref[...] = jnp.zeros(out_ref.shape, out_ref.dtype)


def deposit_part(record_ref, target_ref, *, highs, padded):
    batch, fields, _ = record_ref.shape
    target = jnp.concatenate([target_ref[b] for b in range(batch)], axis=1)
    values = jnp.concatenate([record_ref[b] for b in range(batch)], axis=1).astype(jnp.float32)
    slots = target.shape[1]
    values = jnp.concatenate(
        [values, jnp.zeros((padded - fields, slots), jnp.float32)], axis=0
    ).astype(jnp.bfloat16)
    high = target // LOW
    low = target - high * LOW
    spread = jnp.concatenate(
        [values * jnp.where(high == h, 1.0, 0.0).astype(jnp.bfloat16) for h in range(highs)],
        axis=0,
    )
    place = jnp.where(
        lax.broadcasted_iota(jnp.int32, (LOW, slots), 0) == low, 1.0, 0.0
    ).astype(jnp.bfloat16)
    return lax.dot_general(
        spread, place, (((1,), (1,)), ((), ())), preferred_element_type=jnp.float32
    )


def deposit_first_body(record_ref, target_ref, total_ref, *, highs, padded):
    part = deposit_part(record_ref, target_ref, highs=highs, padded=padded)

    @pl.when(pl.program_id(0) == 0)
    def first():
        total_ref[...] = part

    @pl.when(pl.program_id(0) > 0)
    def later():
        total_ref[...] = total_ref[...] + part


def deposit_last_body(
    record_ref, target_ref, before_ref, area_ref, out_ref, total_ref, *, highs, padded
):
    step = pl.program_id(0)
    fields = out_ref.shape[0]
    part = deposit_part(record_ref, target_ref, highs=highs, padded=padded)

    @pl.when(step == 0)
    def first():
        total_ref[...] = before_ref[...] + part

    @pl.when(step > 0)
    def later():
        total_ref[...] = total_ref[...] + part

    @pl.when(step == pl.num_programs(0) - 1)
    def finish():
        for h in range(highs):
            area = area_ref[:, h * LOW : (h + 1) * LOW]
            out_ref[:, h * LOW : (h + 1) * LOW] = (
                total_ref[h * padded : h * padded + fields, :] / area
            ).astype(jnp.bfloat16)


def neighbours(first, last, axis, wrap):
    size = lax.axis_size(axis)
    up = [(i, (i + 1) % size) for i in range(size if wrap else size - 1)]
    down = [(j, i) for i, j in up]
    return (lax.ppermute(last, axis, up), lax.ppermute(first, axis, down))


def on_device(
    source_flux, gauss_weight, gauss_offset, slot_count, source_cell, target_cell, target_area
):
    fields, height, breadth = source_flux.shape
    members = lax.axis_size("blk")
    capacity = source_cell.shape[1]
    cells = target_area.shape[0]
    groups = height // GROUP
    span = GROUP + 2 * REACH
    above, below = neighbours(
        source_flux[:, :REACH], source_flux[:, height - REACH :], "panel", False
    )
    flat = lambda part: jnp.swapaxes(part, 1, 2).reshape(fields, REACH * height)
    before, after = neighbours(
        flat(source_flux[:, :, :REACH]), flat(source_flux[:, :, breadth - REACH :]), "blk", True
    )
    rim = jnp.concatenate([before, after], axis=1)
    tall = jnp.concatenate([above, source_flux, below], axis=1)
    window = jnp.stack([tall[:, g * GROUP : g * GROUP + span] for g in range(groups)]).reshape(
        groups * fields, span * breadth
    )
    offset_x = gauss_offset[0]
    offset_y = gauss_offset[1]
    slots = lax.broadcasted_iota(jnp.int32, (members, capacity), 1)
    live = (slots < slot_count[:, None]).astype(jnp.float32)
    area = jnp.sum(gauss_weight, axis=0)
    first_x = jnp.sum(gauss_weight * offset_x, axis=0)
    first_y = jnp.sum(gauss_weight * offset_y, axis=0)
    second_x = 0.5 * jnp.sum(gauss_weight * offset_x * offset_x, axis=0)
    second_y = 0.5 * jnp.sum(gauss_weight * offset_y * offset_y, axis=0)
    centre = area - 2.5 * (second_x + second_y)
    inverse = 1.0 / (12.0 * centre)
    taps = []
    for one, two in ((first_x, second_x), (first_y, second_y)):
        taps += [
            (one - two) * inverse,
            (16.0 * two - 8.0 * one) * inverse,
            (16.0 * two + 8.0 * one) * inverse,
            (-one - two) * inverse,
        ]
    row = source_cell // breadth
    col = source_cell - row * breadth
    terms = [centre * live] + taps + [row.astype(jnp.float32), col.astype(jnp.float32)]
    terms += [jnp.zeros_like(area)] * (TERMS - len(terms))
    terms = jnp.stack(terms, axis=1)
    half = capacity // 2
    arrived = []
    for part in range(2):
        records = pl.pallas_call(
            functools.partial(
                record_body, fields=fields, height=height, breadth=breadth, start=part * half
            ),
            grid_spec=pltpu.PrefetchScalarGridSpec(
                num_scalar_prefetch=1,
                grid=(members,),
                in_specs=[
                    pl.BlockSpec((groups * fields, span * breadth), lambda i, n: (0, 0)),
                    pl.BlockSpec((fields, 2 * REACH * height), lambda i, n: (0, 0)),
                    pl.BlockSpec((1, TERMS, half), lambda i, n, part=part: (i, 0, part)),
                ],
                out_specs=pl.BlockSpec((1, fields, half), lambda i, n: (i, 0, 0)),
            ),
            out_shape=jax.ShapeDtypeStruct((members, fields, half), jnp.bfloat16),
            name=f"records_{part}",
        )(slot_count, window, rim, terms)
        arrived.append(lax.all_to_all(records, "blk", split_axis=0, concat_axis=0, tiled=True))
    highs = cells // LOW
    padded = -(-fields // 16) * 16
    targets = target_cell.reshape(members, 1, capacity)
    record_spec = pl.BlockSpec((BATCH, fields, half), lambda i: (i, 0, 0))
    total_spec = pl.BlockSpec((highs * padded, LOW), lambda i: (0, 0))
    before = pl.pallas_call(
        functools.partial(deposit_first_body, highs=highs, padded=padded),
        grid=(members // BATCH,),
        in_specs=[record_spec, pl.BlockSpec((BATCH, 1, half), lambda i: (i, 0, 0))],
        out_specs=total_spec,
        out_shape=jax.ShapeDtypeStruct((highs * padded, LOW), jnp.float32),
        name="deposit_0",
    )(arrived[0], targets)
    return pl.pallas_call(
        functools.partial(deposit_last_body, highs=highs, padded=padded),
        grid=(members // BATCH,),
        in_specs=[
            record_spec,
            pl.BlockSpec((BATCH, 1, half), lambda i: (i, 0, 1)),
            total_spec,
            pl.BlockSpec((1, cells), lambda i: (0, 0)),
        ],
        out_specs=pl.BlockSpec((fields, cells), lambda i: (0, 0)),
        out_shape=jax.ShapeDtypeStruct((fields, cells), jnp.bfloat16),
        scratch_shapes=[pltpu.VMEM((highs * padded, LOW), jnp.float32)],
        name="deposit_1",
    )(arrived[1], targets, before, target_area.reshape(1, cells))


def solution(mesh):
    placed = (
        P(None, "panel", "blk"),
        P(None, ("panel", "blk"), None),
        P(None, None, ("panel", "blk"), None),
        P(("panel", "blk")),
        P(("panel", "blk"), None),
        P(("panel", "blk"), None),
        P(("panel", "blk")),
    )
    return jax.shard_map(
        on_device, mesh=mesh, in_specs=placed, out_specs=P(None, ("panel", "blk")), check_vma=False
    )
```

time: 91.8 us -> 83.3 us (0.907)
  the two profiles are of different devices: /device:TPU:1 before, /device:TPU:16 now
where the time goes in v2:
time: 83.3 us; the launch traced here: 81.6 us
  Pallas kernels  40.2 us (48%)
  starting transfers between devices  25 us (30%)
  local copies, waits for them, and re-layouts  11 us (13%)
  waiting for transfers between devices  4.43 us (5%)
    pallas_call x2, Pallas kernels, on_device(): pl.pallas_call(functools.partial(record_body, fields=fields, height=heigh...  29 us
    all_to_all x2, starting transfers between devices, on_device(): lax.all_to_all(records, 'blk', split_axis=0, concat_axis=0, tiled=True)  13.1 us
    ppermute x4, starting transfers between devices, neighbours(): return (lax.ppermute(last, axis, up), lax.ppermute(first, axis, down))  11.9 us
    pallas_call x1, Pallas kernels, on_device(): pl.pallas_call(functools.partial(deposit_last_body, highs=highs, padded=p...  5.77 us
    pallas_call x1, Pallas kernels, on_device(): pl.pallas_call(functools.partial(deposit_first_body, highs=highs, padded=...  5.43 us
    all_to_all x2, waiting for transfers between devices, on_device(): lax.all_to_all(records, 'blk', split_axis=0, concat_axis=0, tiled=True)  4.42 us
    unnamed x26, local copies, waits for them, and re-layouts  3.39 us
    transpose x3, local copies, waits for them, and re-layouts, on_device(): flat = lambda part: jnp.swapaxes(part, 1, 2).reshape(fields, REACH * height)  3.37 us
  transfers between devices with their start and end apart: 6, of which 1 were waited for; matrix products, arithmetic and copies ran while one was open for 10% of the time, Pallas kernels for 23%

profile of v2, /device:TPU:16, one launch (start us, length us, event | category | flops | bytes accessed | tf_op | source)
XLA Modules:
  0.0 81.6 jit_solution(7159974407636200957)
XLA Ops:
  0.0 1.0 %fusion.19 = (bf16[72,2,128]{2,1,0:T(2,128)(2,1)S(1)}, bf16[72,2,128]{2,1,0:T(2,128)(2,1)S(1)}) fusion(bf16[72,64,128]{2,1,0:T(8,128)(2,1)} %param.7), kind=kLoop, calls=%fused_computation.58 | loop fusion | bytes 147456 | tf_op jit(solution)/shard_map/slice | solution.py:149
  1.0 1.9 %collective-permute-start = (bf16[72,2,128]{2,1,0:T(2,128)(2,1)S(1)}, bf16[72,2,128]{2,1,0:T(2,128)(2,1)S(1)}, u32[]{:S(2)}, u32[]{:S(2)}) collective-permute-start(bf16[72,2,128]{2,1,0:T(2,128)(2,1)S(1)} %get-tuple-element.17), channel_id=1, source_target_pairs={{0,16},{16,32},{32,48},{48,64},{64,80},{80,96},{96,112},{1,17},{17... | collective-permute-start | bytes 110600 | tf_op jit(solution)/shard_map/ppermute | solution.py:136
  3.0 3.6 %collective-permute-start.1 = (bf16[72,2,128]{2,1,0:T(2,128)(2,1)S(1)}, bf16[72,2,128]{2,1,0:T(2,128)(2,1)S(1)}, u32[]{:S(2)}, u32[]{:S(2)}) collective-permute-start(bf16[72,2,128]{2,1,0:T(2,128)(2,1)S(1)} %get-tuple-element.16), channel_id=1, source_target_pairs={{16,0},{32,16},{48,32},{64,48},{80,64},{96,80},{112,96},{17,1},{33... | collective-permute-start | bytes 110600 | tf_op jit(solution)/shard_map/ppermute | solution.py:136
  6.6 2.4 %slice_bitcast_fusion = (bf16[72,2,64]{1,2,0:T(8,128)(2,1)S(1)}, bf16[72,2,64]{1,2,0:T(8,128)(2,1)S(1)}) fusion(bf16[72,64,128]{2,1,0:T(8,128)(2,1)} %param.7), kind=kLoop, calls=%fused_computation.1 | loop fusion | bytes 73728 | tf_op jit(solution)/shard_map/transpose | solution.py:151
  9.0 0.0 copy-start.3
  9.0 0.0 copy-start.5
  9.0 0.0 copy-start.8
  9.0 0.0 copy-start.6
  9.0 0.5 copy.36
  9.6 0.1 reshape.279
  9.6 0.0 copy-start
  9.7 1.6 %collective-permute-start.2 = (bf16[72,128]{1,0:T(8,128)(2,1)S(1)}, bf16[72,128]{1,0:T(8,128)(2,1)S(1)}, u32[]{:S(2)}, u32[]{:S(2)}) collective-permute-start(bf16[72,128]{1,0:T(8,128)(2,1)S(1)} %reshape.279), channel_id=1, source_target_pairs={{0,1},{1,2},{2,3},{3,4},{4,5},{5,6},{6,7},{7,8},{8,9},{9,10},{10,1... | collective-permute-start | bytes 55304 | tf_op jit(solution)/shard_map/ppermute | solution.py:136
  11.2 0.5 copy.37
  11.7 0.1 reshape.280
  11.8 4.8 %collective-permute-start.3 = (bf16[72,128]{1,0:T(8,128)(2,1)S(1)}, bf16[72,128]{1,0:T(8,128)(2,1)S(1)}, u32[]{:S(2)}, u32[]{:S(2)}) collective-permute-start(bf16[72,128]{1,0:T(8,128)(2,1)S(1)} %reshape.280), channel_id=1, source_target_pairs={{1,0},{2,1},{3,2},{4,3},{5,4},{6,5},{7,6},{8,7},{9,8},{10,9},{11,1... | collective-permute-start | bytes 55304 | tf_op jit(solution)/shard_map/ppermute | solution.py:136
  16.6 0.0 copy-done.3
  16.6 0.0 copy-done.5
  16.7 0.0 copy-done.8
  16.7 0.1 compare_select_fusion
  16.8 0.1 copy_multiply_fusion
  17.0 0.1 add_multiply_fusion
  17.0 0.0 copy-done.6
  17.4 2.1 %stack.60.term_ref = f32[16,16,512]{2,1,0:T(8,128)} concatenate(f32[16,1,512]{2,1,0:T(1,128)S(1)} %compare_select_fusion, f32[16,1,512]{2,1,0:T(1,128)S(1)} %copy.48, f32[16,1,512]{2,1,0:T(1,128)S(1)} %copy.49, f32[16,1,512]{2,1,0:T(1,128)S(1)} %copy.50, f32[16,1,512]{2,1,0:T(1,128)S(1)} %copy.51, f32[16,1,512]{2,1,0:T(1,128)S(1)} %copy.52, f32[16,1,512]{2,1,0:T(1,128)S(1)} %get-tuple-element.19, ...), dimensions={1} | concatenate | bytes 1048576 | tf_op jit(solution)/shard_map/stack | solution.py:183
  19.5 0.0 collective-permute-done.2
  19.5 0.0 collective-permute-done.3
  19.5 0.0 copy-start.4
  19.5 0.0 collective-permute-done
  19.5 0.0 copy-done
  19.6 0.1 fusion.3
  19.7 0.1 bitcast_dynamic-update-slice_fusion.5
  19.8 0.1 bitcast_dynamic-update-slice_fusion.4
  20.0 0.1 bitcast_dynamic-update-slice_fusion.3
  20.1 0.1 bitcast_dynamic-update-slice_fusion.2
  20.2 0.1 bitcast_dynamic-update-slice_fusion.1
  20.4 0.1 bitcast_dynamic-update-slice_fusion
  20.5 0.0 copy-done.4
  20.5 0.0 collective-permute-done.1
  20.5 0.2 fusion.1
  20.7 1.7 %copy.70 = bf16[72,8,12,128]{3,1,2,0:T(8,128)(2,1)} copy(bf16[72,8,12,128]{3,2,1,0:T(8,128)(2,1)S(1)} %bitcast.95) | data formatting | bytes 3538944
  22.4 15.6 %records_0.1 = bf16[16,72,256]{2,1,0:T(8,128)(2,1)} custom-call(s32[16]{0:T(128)} %count_ref.3, bf16[576,1536]{1,0:T(8,128)(2,1)} %bitcast.93, bf16[72,256]{1,0:T(8,128)(2,1)} %copy-done.4, f32[16,16,512]{2,1,0:T(8,128)} %stack.60.term_ref), custom_call_target="tpu_custom_call" | custom-call | tf_op jit(solution)/shard_map/records_0/pallas_call | solution.py:187
  38.0 0.0 copy-start.7
  38.0 5.9 %all-to-all-start.1 = ((bf16[16,72,256]{2,1,0:T(8,128)(2,1)}), bf16[16,72,256]{2,1,0:T(8,128)(2,1)S(1)}, u32[]{:S(2)}, u32[]{:S(2)}) async-start(bf16[16,72,256]{2,1,0:T(8,128)(2,1)} %records_0.1), calls=%async_computation.1 | async-start | bytes 1179648 | tf_op jit(solution)/shard_map/all_to_all | solution.py:204
  43.8 13.4 %records_1.1 = bf16[16,72,256]{2,1,0:T(8,128)(2,1)} custom-call(s32[16]{0:T(128)} %count_ref.3, bf16[576,1536]{1,0:T(8,128)(2,1)} %bitcast.94, bf16[72,256]{1,0:T(8,128)(2,1)} %copy-done.4, f32[16,16,512]{2,1,0:T(8,128)} %stack.60.term_ref), custom_call_target="tpu_custom_call" | custom-call | tf_op jit(solution)/shard_map/records_1/pallas_call | solution.py:187
  57.3 0.0 all-to-all-done.1.record_ref
  57.3 0.0 copy-start.2
  57.3 7.2 %all-to-all-start = ((bf16[16,72,256]{2,1,0:T(8,128)(2,1)}), bf16[16,72,256]{2,1,0:T(8,128)(2,1)S(1)}, u32[]{:S(2)}, u32[]{:S(2)}) async-start(bf16[16,72,256]{2,1,0:T(8,128)(2,1)} %records_1.1), calls=%async_computation | async-start | bytes 1179648 | tf_op jit(solution)/shard_map/all_to_all | solution.py:204
  64.5 0.0 copy-done.7
  64.5 0.6 reshape.281.target_ref
  65.1 0.0 copy-done.2
  65.1 5.4 %deposit_0.1.before_ref = f32[1280,256]{1,0:T(8,128)} custom-call(bf16[16,72,256]{2,1,0:T(8,128)(2,1)} %copy-done.2, s32[16,1,512]{2,1,0:T(1,128)} %reshape.281.target_ref), custom_call_target="tpu_custom_call" | custom-call | tf_op jit(solution)/shard_map/deposit_0/pallas_call | solution.py:210
  70.6 4.4 %all-to-all-done.record_ref = bf16[16,72,256]{2,1,0:T(8,128)(2,1)S(1)} async-done(((bf16[16,72,256]{2,1,0:T(8,128)(2,1)}), bf16[16,72,256]{2,1,0:T(8,128)(2,1)S(1)}, u32[]{:S(2)}, u32[]{:S(2)}) %all-to-all-start) | async-done | bytes 589856 | tf_op jit(solution)/shard_map/all_to_all | solution.py:204
  75.0 0.0 copy-start.1
  75.0 0.9 %copy-done.1 = bf16[16,72,256]{2,1,0:T(8,128)(2,1)} copy-done((bf16[16,72,256]{2,1,0:T(8,128)(2,1)}, bf16[16,72,256]{2,1,0:T(8,128)(2,1)S(1)}, u32[]{:S(2)}) %copy-start.1) | copy-done | bytes 589848
  75.8 5.8 %deposit_1.1 = bf16[72,4096]{1,0:T(8,128)(2,1)} custom-call(bf16[16,72,256]{2,1,0:T(8,128)(2,1)} %copy-done.1, s32[16,1,512]{2,1,0:T(1,128)} %reshape.281.target_ref, f32[1280,256]{1,0:T(8,128)} %deposit_0.1.before_ref, f32[1,4096]{1,0:T(1,128)} %bitcast.97), custom_call_target="tpu_custom_call" | custom-call | tf_op jit(solution)/shard_map/deposit_1/pallas_call | solution.py:218
  (16 shorter events, 0.4 us)
Async XLA Ops:
  1.0 18.5 %collective-permute-start = (bf16[72,2,128]{2,1,0:T(2,128)(2,1)S(1)}, bf16[72,2,128]{2,1,0:T(2,128)(2,1)S(1)}, u32[]{:S(2)}, u32[]{:S(2)}) collective-permute-start(bf16[72,2,128]{2,1,0:T(2,128)(2,1)S(1)} %get-tuple-element.17), channel_id=1, source_target_pairs={{0,16},{16,32},{32,48},{48,64},{64,80},{80,96},{96,112},{1,17},{17... | collective-permute-start | bytes 110600 | tf_op jit(solution)/shard_map/ppermute | solution.py:136
  3.0 17.5 %collective-permute-start.1 = (bf16[72,2,128]{2,1,0:T(2,128)(2,1)S(1)}, bf16[72,2,128]{2,1,0:T(2,128)(2,1)S(1)}, u32[]{:S(2)}, u32[]{:S(2)}) collective-permute-start(bf16[72,2,128]{2,1,0:T(2,128)(2,1)S(1)} %get-tuple-element.16), channel_id=1, source_target_pairs={{16,0},{32,16},{48,32},{64,48},{80,64},{96,80},{112,96},{17,1},{33... | collective-permute-start | bytes 110600 | tf_op jit(solution)/shard_map/ppermute | solution.py:136
  9.0 7.6 %copy-start.3 = (f32[2,4,16,512]{3,2,1,0:T(8,128)S(1)}, f32[2,4,16,512]{3,2,1,0:T(8,128)}, u32[]{:S(2)}) copy-start(f32[2,4,16,512]{3,2,1,0:T(8,128)} %param.9) | copy-start | bytes 786436
  9.0 7.6 %copy-start.5 = (f32[4,16,512]{2,1,0:T(8,128)S(1)}, f32[4,16,512]{2,1,0:T(8,128)}, u32[]{:S(2)}) copy-start(f32[4,16,512]{2,1,0:T(8,128)} %param.8) | copy-start | bytes 393220
  9.0 7.7 %copy-start.8 = (s32[16]{0:T(128)S(1)}, s32[16]{0:T(128)}, u32[]{:S(2)}) copy-start(s32[16]{0:T(128)} %count_ref.3) | copy-start | bytes 196
  9.0 8.0 %copy-start.6 = (s32[16,512]{1,0:T(8,128)S(1)}, s32[16,512]{1,0:T(8,128)}, u32[]{:S(2)}) copy-start(s32[16,512]{1,0:T(8,128)} %param.11) | copy-start | bytes 98308
  9.6 9.9 %copy-start = (bf16[72,64,128]{2,1,0:T(8,128)(2,1)S(1)}, bf16[72,64,128]{2,1,0:T(8,128)(2,1)}, u32[]{:S(2)}) copy-start(bf16[72,64,128]{2,1,0:T(8,128)(2,1)} %param.7) | copy-start | bytes 3538948
  9.7 9.8 %collective-permute-start.2 = (bf16[72,128]{1,0:T(8,128)(2,1)S(1)}, bf16[72,128]{1,0:T(8,128)(2,1)S(1)}, u32[]{:S(2)}, u32[]{:S(2)}) collective-permute-start(bf16[72,128]{1,0:T(8,128)(2,1)S(1)} %reshape.279), channel_id=1, source_target_pairs={{0,1},{1,2},{2,3},{3,4},{4,5},{5,6},{6,7},{7,8},{8,9},{9,10},{10,1... | collective-permute-start | bytes 55304 | tf_op jit(solution)/shard_map/ppermute | solution.py:136
  11.8 7.7 %collective-permute-start.3 = (bf16[72,128]{1,0:T(8,128)(2,1)S(1)}, bf16[72,128]{1,0:T(8,128)(2,1)S(1)}, u32[]{:S(2)}, u32[]{:S(2)}) collective-permute-start(bf16[72,128]{1,0:T(8,128)(2,1)S(1)} %reshape.280), channel_id=1, source_target_pairs={{1,0},{2,1},{3,2},{4,3},{5,4},{6,5},{7,6},{8,7},{9,8},{10,9},{11,1... | collective-permute-start | bytes 55304 | tf_op jit(solution)/shard_map/ppermute | solution.py:136
  19.5 1.0 %copy-start.4 = (bf16[72,256]{1,0:T(8,128)(2,1)}, bf16[72,256]{1,0:T(8,128)(2,1)S(1)}, u32[]{:S(2)}) copy-start(bf16[72,256]{1,0:T(8,128)(2,1)S(1)} %constant_dynamic-update-slice_fusion.rim_ref) | copy-start | bytes 110596
  38.0 26.5 %copy-start.7 = (s32[16,512]{1,0:T(8,128)S(1)}, s32[16,512]{1,0:T(8,128)}, u32[]{:S(2)}) copy-start(s32[16,512]{1,0:T(8,128)} %param.12) | copy-start | bytes 98308
  38.0 19.3 %all-to-all-start.1 = ((bf16[16,72,256]{2,1,0:T(8,128)(2,1)}), bf16[16,72,256]{2,1,0:T(8,128)(2,1)S(1)}, u32[]{:S(2)}, u32[]{:S(2)}) async-start(bf16[16,72,256]{2,1,0:T(8,128)(2,1)} %records_0.1), calls=%async_computation.1 | async-start | bytes 1179648 | tf_op jit(solution)/shard_map/all_to_all | solution.py:204
  57.3 7.9 %copy-start.2 = (bf16[16,72,256]{2,1,0:T(8,128)(2,1)}, bf16[16,72,256]{2,1,0:T(8,128)(2,1)S(1)}, u32[]{:S(2)}) copy-start(bf16[16,72,256]{2,1,0:T(8,128)(2,1)S(1)} %all-to-all-done.1.record_ref) | copy-start | bytes 1769476
  57.3 17.7 %all-to-all-start = ((bf16[16,72,256]{2,1,0:T(8,128)(2,1)}), bf16[16,72,256]{2,1,0:T(8,128)(2,1)S(1)}, u32[]{:S(2)}, u32[]{:S(2)}) async-start(bf16[16,72,256]{2,1,0:T(8,128)(2,1)} %records_1.1), calls=%async_computation | async-start | bytes 1179648 | tf_op jit(solution)/shard_map/all_to_all | solution.py:204
  75.0 0.9 %copy-start.1 = (bf16[16,72,256]{2,1,0:T(8,128)(2,1)}, bf16[16,72,256]{2,1,0:T(8,128)(2,1)S(1)}, u32[]{:S(2)}) copy-start(bf16[16,72,256]{2,1,0:T(8,128)(2,1)S(1)} %all-to-all-done.record_ref) | copy-start | bytes 1769476

commit v3 on v2

--- a/solution.py
+++ b/solution.py
@@ -12,63 +12,95 @@
 LOW = 256
 TERMS = 16
 BATCH = 8
-
-
-def record_body(
-    count_ref, window_ref, rim_ref, term_ref, out_ref, *, fields, height, breadth, start
-):
+OWNERS = 4
+
+
+def slot_records(terms, window_ref, rim, *, fields, height, breadth):
     groups = height // GROUP
     span = GROUP + 2 * REACH
-    alive = count_ref[pl.program_id(0)] > start
-
-    @pl.when(alive)
-    def compute():
-        terms = term_ref[0]
-        slots = terms.shape[1]
-        scale = terms[0:1]
-        row_taps = [terms[1 + i : 2 + i] for i in range(4)]
-        col_taps = [terms[5 + i : 6 + i] for i in range(4)]
-        row = terms[9:10].astype(jnp.int32)
-        col = terms[10:11].astype(jnp.int32)
-        shifts = (-2, -1, 1, 2)
-        group = row // GROUP
-        local = row - group * GROUP + REACH
-        gap = lax.broadcasted_iota(jnp.int32, (breadth, slots), 0) - col
-        here = jnp.where(gap == 0, 1.0, 0.0).astype(jnp.bfloat16)
-        beside = jnp.zeros((breadth, slots), jnp.float32)
+    slots = terms.shape[1]
+    scale = terms[0:1]
+    row_taps = [terms[1 + i : 2 + i] for i in range(4)]
+    col_taps = [terms[5 + i : 6 + i] for i in range(4)]
+    row = terms[9:10].astype(jnp.int32)
+    col = terms[10:11].astype(jnp.int32)
+    shifts = (-2, -1, 1, 2)
+    group = row // GROUP
+    local = row - group * GROUP + REACH
+    gap = lax.broadcasted_iota(jnp.int32, (breadth, slots), 0) - col
+    here = jnp.where(gap == 0, 1.0, 0.0).astype(jnp.bfloat16)
+    beside = jnp.zeros((breadth, slots), jnp.float32)
+    for shift, tap in zip(shifts, col_taps):
+        beside = jnp.where(gap == shift, tap, beside)
+    beside = beside.astype(jnp.bfloat16)
+    pieces = []
+    for j in range(span):
+        centre = jnp.where(local == j, 1.0, 0.0)
+        weight = centre
+        for shift, tap in zip(shifts, row_taps):
+            weight = jnp.where(local + shift == j, tap, weight)
+        pieces.append(here * weight.astype(jnp.bfloat16) + beside * centre.astype(jnp.bfloat16))
+    table = jnp.concatenate(pieces, axis=0)
+    product = jnp.dot(window_ref[...], table, preferred_element_type=jnp.float32)
+    same_row = jnp.where(
+        lax.broadcasted_iota(jnp.int32, (height, slots), 0) == row, 1.0, 0.0
+    ).astype(jnp.bfloat16)
+    rim_pieces = []
+    for place in (-2, -1, breadth, breadth + 1):
+        weight = jnp.zeros((1, slots), jnp.float32)
         for shift, tap in zip(shifts, col_taps):
-            beside = jnp.where(gap == shift, tap, beside)
-        beside = beside.astype(jnp.bfloat16)
-        pieces = []
-        for j in range(span):
-            centre = jnp.where(local == j, 1.0, 0.0)
-            weight = centre
-            for shift, tap in zip(shifts, row_taps):
-                weight = jnp.where(local + shift == j, tap, weight)
-            pieces.append(
-                here * weight.astype(jnp.bfloat16) + beside * centre.astype(jnp.bfloat16)
-            )
-        table = jnp.concatenate(pieces, axis=0)
-        product = jnp.dot(window_ref[...], table, preferred_element_type=jnp.float32)
-        same_row = jnp.where(
-            lax.broadcasted_iota(jnp.int32, (height, slots), 0) == row, 1.0, 0.0
-        ).astype(jnp.bfloat16)
-        rim_pieces = []
-        for place in (-2, -1, breadth, breadth + 1):
-            weight = jnp.zeros((1, slots), jnp.float32)
-            for shift, tap in zip(shifts, col_taps):
-                weight = jnp.where(col + shift == place, tap, weight)
-            rim_pieces.append(same_row * weight.astype(jnp.bfloat16))
-        total = jnp.dot(
-            rim_ref[...], jnp.concatenate(rim_pieces, axis=0), preferred_element_type=jnp.float32
-        )
-        for g in range(groups):
-            total = total + jnp.where(group == g, product[g * fields : (g + 1) * fields], 0.0)
-        out_ref[0] = (total * scale).astype(jnp.bfloat16)
-
-    @pl.when(jnp.logical_not(alive))
-    def clear():
-        out_ref[...] = jnp.zeros(out_ref.shape, out_ref.dtype)
+            weight = jnp.where(col + shift == place, tap, weight)
+        rim_pieces.append(same_row * weight.astype(jnp.bfloat16))
+    total = jnp.dot(rim, jnp.concatenate(rim_pieces, axis=0), preferred_element_type=jnp.float32)
+    for g in range(groups):
+        total = total + jnp.where(group == g, product[g * fields : (g + 1) * fields], 0.0)
+    return (total * scale).astype(jnp.bfloat16)
+
+
+def record_body(
+    count_ref,
+    window_ref,
+    above_ref,
+    below_ref,
+    before_ref,
+    after_ref,
+    term_ref,
+    out_ref,
+    full_ref,
+    *,
+    fields,
+    height,
+    breadth,
+    start,
+):
+    step = pl.program_id(0)
+    batch, _, slots = term_ref.shape
+    edge = REACH * breadth
+
+    @pl.when(step == 0)
+    def fill():
+        full_ref[...] = window_ref[...]
+        full_ref[:fields, :edge] = above_ref[...]
+        full_ref[-fields:, -edge:] = below_ref[...]
+
+    rim = jnp.concatenate([before_ref[...], after_ref[...]], axis=1)
+    make = functools.partial(slot_records, fields=fields, height=height, breadth=breadth)
+    if start == 0:
+        terms = jnp.concatenate([term_ref[b] for b in range(batch)], axis=1)
+        made = make(terms, full_ref, rim)
+        for b in range(batch):
+            out_ref[b] = made[:, b * slots : (b + 1) * slots]
+    else:
+        for b in range(batch):
+            alive = count_ref[step * batch + b] > start
+
+            @pl.when(alive)
+            def compute():
+                out_ref[b] = make(term_ref[b], full_ref, rim)
+
+            @pl.when(jnp.logical_not(alive))
+            def clear():
+                out_ref[b] = jnp.zeros((fields, slots), out_ref.dtype)
 
 
 def deposit_part(record_ref, target_ref, *, highs, padded):
@@ -145,15 +177,21 @@
     cells = target_area.shape[0]
     groups = height // GROUP
     span = GROUP + 2 * REACH
+    flat_rows = lambda part: part.reshape(fields, REACH * breadth)
+    flat_cols = lambda part: jnp.swapaxes(part, 1, 2).reshape(fields, REACH * height)
     above, below = neighbours(
-        source_flux[:, :REACH], source_flux[:, height - REACH :], "panel", False
-    )
-    flat = lambda part: jnp.swapaxes(part, 1, 2).reshape(fields, REACH * height)
+        flat_rows(source_flux[:, :REACH]),
+        flat_rows(source_flux[:, height - REACH :]),
+        "panel",
+        False,
+    )
     before, after = neighbours(
-        flat(source_flux[:, :, :REACH]), flat(source_flux[:, :, breadth - REACH :]), "blk", True
-    )
-    rim = jnp.concatenate([before, after], axis=1)
-    tall = jnp.concatenate([above, source_flux, below], axis=1)
+        flat_cols(source_flux[:, :, :REACH]),
+        flat_cols(source_flux[:, :, breadth - REACH :]),
+        "blk",
+        True,
+    )
+    tall = jnp.pad(source_flux, ((0, 0), (REACH, REACH), (0, 0)))
     window = jnp.stack([tall[:, g * GROUP : g * GROUP + span] for g in range(groups)]).reshape(
         groups * fields, span * breadth
     )
@@ -190,17 +228,23 @@
             ),
             grid_spec=pltpu.PrefetchScalarGridSpec(
                 num_scalar_prefetch=1,
-                grid=(members,),
+                grid=(members // OWNERS,),
                 in_specs=[
                     pl.BlockSpec((groups * fields, span * breadth), lambda i, n: (0, 0)),
-                    pl.BlockSpec((fields, 2 * REACH * height), lambda i, n: (0, 0)),
-                    pl.BlockSpec((1, TERMS, half), lambda i, n, part=part: (i, 0, part)),
+                    pl.BlockSpec((fields, REACH * breadth), lambda i, n: (0, 0)),
+                    pl.BlockSpec((fields, REACH * breadth), lambda i, n: (0, 0)),
+                    pl.BlockSpec((fields, REACH * height), lambda i, n: (0, 0)),
+                    pl.BlockSpec((fields, REACH * height), lambda i, n: (0, 0)),
+                    pl.BlockSpec((OWNERS, TERMS, half), lambda i, n, part=part: (i, 0, part)),
                 ],
-                out_specs=pl.BlockSpec((1, fields, half), lambda i, n: (i, 0, 0)),
+                out_specs=pl.BlockSpec((OWNERS, fields, half), lambda i, n: (i, 0, 0)),
+                scratch_shapes=[
+                    pltpu.VMEM((groups * fields, span * breadth), jnp.bfloat16)
+                ],
             ),
             out_shape=jax.ShapeDtypeStruct((members, fields, half), jnp.bfloat16),
             name=f"records_{part}",
-        )(slot_count, window, rim, terms)
+        )(slot_count, window, above, below, before, after, terms)
         arrived.append(lax.all_to_all(records, "blk", split_axis=0, concat_axis=0, tiled=True))
     highs = cells // LOW
     padded = -(-fields // 16) * 16

time: 83.3 us -> 78.2 us (0.939)
  the two profiles are of different devices: /device:TPU:16 before, /device:TPU:0 now
where the time goes in v3:
time: 78.2 us; the launch traced here: 78.3 us
  Pallas kernels  36.3 us (46%)
  starting transfers between devices  20.1 us (26%)
  local copies, waits for them, and re-layouts  14.4 us (18%)
  waiting for transfers between devices  6.97 us (9%)
    pallas_call x2, Pallas kernels, on_device(): pl.pallas_call(functools.partial(record_body, fields=fields, height=heigh...  25.1 us
    ppermute x4, starting transfers between devices, neighbours(): return (lax.ppermute(last, axis, up), lax.ppermute(first, axis, down))  10.1 us
    all_to_all x2, starting transfers between devices, on_device(): lax.all_to_all(records, 'blk', split_axis=0, concat_axis=0, tiled=True)  9.97 us
    all_to_all x2, waiting for transfers between devices, on_device(): lax.all_to_all(records, 'blk', split_axis=0, concat_axis=0, tiled=True)  6.96 us
    pallas_call x1, Pallas kernels, on_device(): pl.pallas_call(functools.partial(deposit_last_body, highs=highs, padded=p...  5.77 us
    pallas_call x1, Pallas kernels, on_device(): pl.pallas_call(functools.partial(deposit_first_body, highs=highs, padded=...  5.43 us
    unnamed x30, local copies, waits for them, and re-layouts  5.27 us
    transpose x3, local copies, waits for them, and re-layouts, on_device(): jnp.swapaxes(part, 1, 2).reshape(fields, REACH * height)  3.99 us
  transfers between devices with their start and end apart: 6, of which 2 were waited for; matrix products, arithmetic and copies ran while one was open for 15% of the time, Pallas kernels for 23%

profile of v3, /device:TPU:0, one launch (start us, length us, event | category | flops | bytes accessed | tf_op | source)
XLA Modules:
  0.0 78.3 jit_solution(5436407850698008087)
XLA Ops:
  0.0 1.0 %fusion.19 = (bf16[72,2,128]{2,1,0:T(2,128)(2,1)S(1)}, bf16[72,2,128]{2,1,0:T(2,128)(2,1)S(1)}) fusion(bf16[72,64,128]{2,1,0:T(8,128)(2,1)} %param.7), kind=kLoop, calls=%fused_computation.58 | loop fusion | bytes 147456 | tf_op jit(solution)/shard_map/slice | solution.py:183
  1.0 0.6 copy.76
  1.7 1.9 %collective-permute-start = (bf16[72,256]{1,0:T(8,128)(2,1)}, bf16[72,256]{1,0:T(8,128)(2,1)}, u32[]{:S(2)}, u32[]{:S(2)}) collective-permute-start(bf16[72,256]{1,0:T(8,128)(2,1)} %bitcast.100), channel_id=1, source_target_pairs={{0,16},{16,32},{32,48},{48,64},{64,80},{80,96},{96,112},{1,17},{17... | collective-permute-start | bytes 110600 | tf_op jit(solution)/shard_map/ppermute | solution.py:168
  3.6 0.6 copy.75
  4.2 1.3 %collective-permute-start.1 = (bf16[72,256]{1,0:T(8,128)(2,1)}, bf16[72,256]{1,0:T(8,128)(2,1)}, u32[]{:S(2)}, u32[]{:S(2)}) collective-permute-start(bf16[72,256]{1,0:T(8,128)(2,1)} %bitcast.99), channel_id=1, source_target_pairs={{16,0},{32,16},{48,32},{64,48},{80,64},{96,80},{112,96},{17,1},{33... | collective-permute-start | bytes 110600 | tf_op jit(solution)/shard_map/ppermute | solution.py:168
  5.5 2.4 %slice_bitcast_fusion = (bf16[72,2,64]{1,2,0:T(8,128)(2,1)S(1)}, bf16[72,2,64]{1,2,0:T(8,128)(2,1)S(1)}) fusion(bf16[72,64,128]{2,1,0:T(8,128)(2,1)} %param.7), kind=kLoop, calls=%fused_computation.3 | loop fusion | bytes 73728 | tf_op jit(solution)/shard_map/transpose | solution.py:181
  7.8 0.0 copy-start
  7.8 1.1 %copy.36 = bf16[72,2,64]{2,1,0:T(2,128)(2,1)} copy(bf16[72,2,64]{1,2,0:T(8,128)(2,1)S(1)} %get-tuple-element.15) | data formatting | bytes 36864 | tf_op jit(solution)/shard_map/transpose | solution.py:181
  9.0 0.9 %reshape.287 = bf16[72,128]{1,0:T(8,128)(2,1)S(1)} reshape(bf16[72,2,64]{2,1,0:T(2,128)(2,1)} %copy.36) | data formatting | bytes 36864 | tf_op jit(solution)/shard_map/reshape | solution.py:181
  9.8 2.1 %collective-permute-start.2 = (bf16[72,128]{1,0:T(8,128)(2,1)S(1)}, bf16[72,128]{1,0:T(8,128)(2,1)S(1)}, u32[]{:S(2)}, u32[]{:S(2)}) collective-permute-start(bf16[72,128]{1,0:T(8,128)(2,1)S(1)} %reshape.287), channel_id=1, source_target_pairs={{0,1},{1,2},{2,3},{3,4},{4,5},{5,6},{6,7},{7,8},{8,9},{9,10},{10,1... | collective-permute-start | bytes 55304 | tf_op jit(solution)/shard_map/ppermute | solution.py:168
  11.9 0.5 copy.37
  12.4 0.1 reshape.288
  12.5 0.0 copy-start.3
  12.5 0.0 copy-start.4
  12.5 4.8 %collective-permute-start.3 = (bf16[72,128]{1,0:T(8,128)(2,1)S(1)}, bf16[72,128]{1,0:T(8,128)(2,1)S(1)}, u32[]{:S(2)}, u32[]{:S(2)}) collective-permute-start(bf16[72,128]{1,0:T(8,128)(2,1)S(1)} %reshape.288), channel_id=1, source_target_pairs={{1,0},{2,1},{3,2},{4,3},{5,4},{6,5},{7,6},{8,7},{9,8},{10,9},{11,1... | collective-permute-start | bytes 55304 | tf_op jit(solution)/shard_map/ppermute | solution.py:168
  17.4 0.0 copy-done
  17.4 0.1 fusion.1
  17.5 0.0 copy-start.7
  17.5 0.0 copy-start.9
  17.5 0.1 bitcast_dynamic-update-slice_fusion.5
  17.6 0.1 bitcast_dynamic-update-slice_fusion.4
  17.8 0.1 bitcast_dynamic-update-slice_fusion.3
  17.9 0.1 bitcast_dynamic-update-slice_fusion.2
  18.0 0.1 bitcast_dynamic-update-slice_fusion.1
  18.2 0.1 bitcast_dynamic-update-slice_fusion
  18.3 0.0 copy-done.3
  18.3 0.0 copy-done.4
  18.4 0.0 copy-done.7
  18.5 0.0 copy-done.9
  18.5 0.1 compare_select_fusion
  18.6 0.1 copy_multiply_fusion
  18.7 0.1 add_multiply_fusion
  18.8 0.1 fusion.3
  18.9 1.7 %copy.74 = bf16[72,8,12,128]{3,1,2,0:T(8,128)(2,1)} copy(bf16[72,8,12,128]{3,2,1,0:T(8,128)(2,1)S(1)} %bitcast.103) | data formatting | bytes 3538944
  20.9 2.1 %stack.60.term_ref = f32[16,16,512]{2,1,0:T(8,128)} concatenate(f32[16,1,512]{2,1,0:T(1,128)S(1)} %compare_select_fusion, f32[16,1,512]{2,1,0:T(1,128)S(1)} %copy.48, f32[16,1,512]{2,1,0:T(1,128)S(1)} %copy.49, f32[16,1,512]{2,1,0:T(1,128)S(1)} %copy.50, f32[16,1,512]{2,1,0:T(1,128)S(1)} %copy.51, f32[16,1,512]{2,1,0:T(1,128)S(1)} %copy.52, f32[16,1,512]{2,1,0:T(1,128)S(1)} %get-tuple-element.19, ...), dimensions={1} | concatenate | bytes 1048576 | tf_op jit(solution)/shard_map/stack | solution.py:221
  23.0 0.0 collective-permute-done.2.before_ref
  23.0 0.0 copy-start.5
  23.0 0.0 collective-permute-done.3.after_ref
  23.0 0.0 copy-start.6
  23.0 0.0 collective-permute-done.above_ref
  23.0 0.0 collective-permute-done.1.below_ref
  23.0 0.6 copy-done.5
  23.6 0.0 copy-done.6
  23.6 12.6 %records_0.1 = bf16[16,72,256]{2,1,0:T(8,128)(2,1)} custom-call(s32[16]{0:T(128)} %count_ref.3, bf16[576,1536]{1,0:T(8,128)(2,1)} %bitcast.101, bf16[72,256]{1,0:T(8,128)(2,1)} %collective-permute-done.above_ref, bf16[72,256]{1,0:T(8,128)(2,1)} %collective-permute-done.1.below_ref, bf16[72,128]{1,0:T(8,128)(2,1)} %copy-done.5, bf16[72,128]{1,0:T(8,128)(2,1)} %copy-done.6, ...), custom_call_target="tpu_custom_call" | custom-call | tf_op jit(solution)/shard_map/records_0/pallas_call | solution.py:225
  36.2 3.7 %all-to-all-start.1 = ((bf16[16,72,256]{2,1,0:T(8,128)(2,1)}), bf16[16,72,256]{2,1,0:T(8,128)(2,1)S(1)}, u32[]{:S(2)}, u32[]{:S(2)}) async-start(bf16[16,72,256]{2,1,0:T(8,128)(2,1)} %records_0.1), calls=%async_computation.1 | async-start | bytes 1179648 | tf_op jit(solution)/shard_map/all_to_all | solution.py:248
  39.9 0.0 copy-start.8
  39.9 12.5 %records_1.1 = bf16[16,72,256]{2,1,0:T(8,128)(2,1)} custom-call(s32[16]{0:T(128)} %count_ref.3, bf16[576,1536]{1,0:T(8,128)(2,1)} %bitcast.102, bf16[72,256]{1,0:T(8,128)(2,1)} %collective-permute-done.above_ref, bf16[72,256]{1,0:T(8,128)(2,1)} %collective-permute-done.1.below_ref, bf16[72,128]{1,0:T(8,128)(2,1)} %copy-done.5, bf16[72,128]{1,0:T(8,128)(2,1)} %copy-done.6, ...), custom_call_target="tpu_custom_call" | custom-call | tf_op jit(solution)/shard_map/records_1/pallas_call | solution.py:225
  52.4 0.6 all-to-all-done.1.record_ref
  53.0 0.0 copy-start.2
  53.0 6.3 %all-to-all-start = ((bf16[16,72,256]{2,1,0:T(8,128)(2,1)}), bf16[16,72,256]{2,1,0:T(8,128)(2,1)S(1)}, u32[]{:S(2)}, u32[]{:S(2)}) async-start(bf16[16,72,256]{2,1,0:T(8,128)(2,1)} %records_1.1), calls=%async_computation | async-start | bytes 1179648 | tf_op jit(solution)/shard_map/all_to_all | solution.py:248
  59.4 0.0 copy-done.8
  59.4 0.6 reshape.289.target_ref
  60.0 0.0 copy-done.2
  60.0 5.4 %deposit_0.1.before_ref = f32[1280,256]{1,0:T(8,128)} custom-call(bf16[16,72,256]{2,1,0:T(8,128)(2,1)} %copy-done.2, s32[16,1,512]{2,1,0:T(1,128)} %reshape.289.target_ref), custom_call_target="tpu_custom_call" | custom-call | tf_op jit(solution)/shard_map/deposit_0/pallas_call | solution.py:254
  65.4 6.3 %all-to-all-done.record_ref = bf16[16,72,256]{2,1,0:T(8,128)(2,1)S(1)} async-done(((bf16[16,72,256]{2,1,0:T(8,128)(2,1)}), bf16[16,72,256]{2,1,0:T(8,128)(2,1)S(1)}, u32[]{:S(2)}, u32[]{:S(2)}) %all-to-all-start) | async-done | bytes 589856 | tf_op jit(solution)/shard_map/all_to_all | solution.py:248
  71.7 0.0 copy-start.1
  71.7 0.8 %copy-done.1 = bf16[16,72,256]{2,1,0:T(8,128)(2,1)} copy-done((bf16[16,72,256]{2,1,0:T(8,128)(2,1)}, bf16[16,72,256]{2,1,0:T(8,128)(2,1)S(1)}, u32[]{:S(2)}) %copy-start.1) | copy-done | bytes 589848
  72.6 5.8 %deposit_1.1 = bf16[72,4096]{1,0:T(8,128)(2,1)} custom-call(bf16[16,72,256]{2,1,0:T(8,128)(2,1)} %copy-done.1, s32[16,1,512]{2,1,0:T(1,128)} %reshape.289.target_ref, f32[1280,256]{1,0:T(8,128)} %deposit_0.1.before_ref, f32[1,4096]{1,0:T(1,128)} %bitcast.107), custom_call_target="tpu_custom_call" | custom-call | tf_op jit(solution)/shard_map/deposit_1/pallas_call | solution.py:262
  (14 shorter events, 0.4 us)
Async XLA Ops:
  1.7 21.3 %collective-permute-start = (bf16[72,256]{1,0:T(8,128)(2,1)}, bf16[72,256]{1,0:T(8,128)(2,1)}, u32[]{:S(2)}, u32[]{:S(2)}) collective-permute-start(bf16[72,256]{1,0:T(8,128)(2,1)} %bitcast.100), channel_id=1, source_target_pairs={{0,16},{16,32},{32,48},{48,64},{64,80},{80,96},{96,112},{1,17},{17... | collective-permute-start | bytes 110600 | tf_op jit(solution)/shard_map/ppermute | solution.py:168
  4.2 18.8 %collective-permute-start.1 = (bf16[72,256]{1,0:T(8,128)(2,1)}, bf16[72,256]{1,0:T(8,128)(2,1)}, u32[]{:S(2)}, u32[]{:S(2)}) collective-permute-start(bf16[72,256]{1,0:T(8,128)(2,1)} %bitcast.99), channel_id=1, source_target_pairs={{16,0},{32,16},{48,32},{64,48},{80,64},{96,80},{112,96},{17,1},{33... | collective-permute-start | bytes 110600 | tf_op jit(solution)/shard_map/ppermute | solution.py:168
  7.8 9.5 %copy-start = (bf16[72,64,128]{2,1,0:T(8,128)(2,1)S(1)}, bf16[72,64,128]{2,1,0:T(8,128)(2,1)}, u32[]{:S(2)}) copy-start(bf16[72,64,128]{2,1,0:T(8,128)(2,1)} %param.7) | copy-start | bytes 3538948
  9.8 13.2 %collective-permute-start.2 = (bf16[72,128]{1,0:T(8,128)(2,1)S(1)}, bf16[72,128]{1,0:T(8,128)(2,1)S(1)}, u32[]{:S(2)}, u32[]{:S(2)}) collective-permute-start(bf16[72,128]{1,0:T(8,128)(2,1)S(1)} %reshape.287), channel_id=1, source_target_pairs={{0,1},{1,2},{2,3},{3,4},{4,5},{5,6},{6,7},{7,8},{8,9},{9,10},{10,1... | collective-permute-start | bytes 55304 | tf_op jit(solution)/shard_map/ppermute | solution.py:168
  12.5 5.8 %copy-start.3 = (f32[2,4,16,512]{3,2,1,0:T(8,128)S(1)}, f32[2,4,16,512]{3,2,1,0:T(8,128)}, u32[]{:S(2)}) copy-start(f32[2,4,16,512]{3,2,1,0:T(8,128)} %param.9) | copy-start | bytes 786436
  12.5 5.8 %copy-start.4 = (f32[4,16,512]{2,1,0:T(8,128)S(1)}, f32[4,16,512]{2,1,0:T(8,128)}, u32[]{:S(2)}) copy-start(f32[4,16,512]{2,1,0:T(8,128)} %param.8) | copy-start | bytes 393220
  12.5 10.4 %collective-permute-start.3 = (bf16[72,128]{1,0:T(8,128)(2,1)S(1)}, bf16[72,128]{1,0:T(8,128)(2,1)S(1)}, u32[]{:S(2)}, u32[]{:S(2)}) collective-permute-start(bf16[72,128]{1,0:T(8,128)(2,1)S(1)} %reshape.288), channel_id=1, source_target_pairs={{1,0},{2,1},{3,2},{4,3},{5,4},{6,5},{7,6},{8,7},{9,8},{10,9},{11,1... | collective-permute-start | bytes 55304 | tf_op jit(solution)/shard_map/ppermute | solution.py:168
  17.5 0.9 %copy-start.7 = (s32[16,512]{1,0:T(8,128)S(1)}, s32[16,512]{1,0:T(8,128)}, u32[]{:S(2)}) copy-start(s32[16,512]{1,0:T(8,128)} %param.11) | copy-start | bytes 98308
  17.5 1.0 %copy-start.9 = (s32[16]{0:T(128)S(1)}, s32[16]{0:T(128)}, u32[]{:S(2)}) copy-start(s32[16]{0:T(128)} %count_ref.3) | copy-start | bytes 196
  23.0 0.6 copy-start.5
  23.0 0.6 copy-start.6
  36.2 16.9 %all-to-all-start.1 = ((bf16[16,72,256]{2,1,0:T(8,128)(2,1)}), bf16[16,72,256]{2,1,0:T(8,128)(2,1)S(1)}, u32[]{:S(2)}, u32[]{:S(2)}) async-start(bf16[16,72,256]{2,1,0:T(8,128)(2,1)} %records_0.1), calls=%async_computation.1 | async-start | bytes 1179648 | tf_op jit(solution)/shard_map/all_to_all | solution.py:248
  39.9 19.5 %copy-start.8 = (s32[16,512]{1,0:T(8,128)S(1)}, s32[16,512]{1,0:T(8,128)}, u32[]{:S(2)}) copy-start(s32[16,512]{1,0:T(8,128)} %param.12) | copy-start | bytes 98308
  53.0 7.0 %copy-start.2 = (bf16[16,72,256]{2,1,0:T(8,128)(2,1)}, bf16[16,72,256]{2,1,0:T(8,128)(2,1)S(1)}, u32[]{:S(2)}) copy-start(bf16[16,72,256]{2,1,0:T(8,128)(2,1)S(1)} %all-to-all-done.1.record_ref) | copy-start | bytes 1769476
  53.0 18.7 %all-to-all-start = ((bf16[16,72,256]{2,1,0:T(8,128)(2,1)}), bf16[16,72,256]{2,1,0:T(8,128)(2,1)S(1)}, u32[]{:S(2)}, u32[]{:S(2)}) async-start(bf16[16,72,256]{2,1,0:T(8,128)(2,1)} %records_1.1), calls=%async_computation | async-start | bytes 1179648 | tf_op jit(solution)/shard_map/all_to_all | solution.py:248
  71.7 0.8 %copy-start.1 = (bf16[16,72,256]{2,1,0:T(8,128)(2,1)}, bf16[16,72,256]{2,1,0:T(8,128)(2,1)S(1)}, u32[]{:S(2)}) copy-start(bf16[16,72,256]{2,1,0:T(8,128)(2,1)S(1)} %all-to-all-done.record_ref) | copy-start | bytes 1769476

commit v4 on v3

--- a/solution.py
+++ b/solution.py
@@ -2,6 +2,7 @@
 
 import jax
 import jax.numpy as jnp
+import numpy as np
 from jax import lax
 from jax.experimental import pallas as pl
 from jax.experimental.pallas import tpu as pltpu
@@ -10,7 +11,7 @@
 GROUP = 8
 REACH = 2
 LOW = 256
-TERMS = 16
+TERMS = 11
 BATCH = 8
 OWNERS = 4
 
@@ -18,12 +19,12 @@
 def slot_records(terms, window_ref, rim, *, fields, height, breadth):
     groups = height // GROUP
     span = GROUP + 2 * REACH
-    slots = terms.shape[1]
-    scale = terms[0:1]
-    row_taps = [terms[1 + i : 2 + i] for i in range(4)]
-    col_taps = [terms[5 + i : 6 + i] for i in range(4)]
-    row = terms[9:10].astype(jnp.int32)
-    col = terms[10:11].astype(jnp.int32)
+    slots = terms[0].shape[1]
+    scale = terms[0]
+    row_taps = terms[1:5]
+    col_taps = terms[5:9]
+    row = terms[9].astype(jnp.int32)
+    col = terms[10].astype(jnp.int32)
     shifts = (-2, -1, 1, 2)
     group = row // GROUP
     local = row - group * GROUP + REACH
@@ -57,36 +58,86 @@
     return (total * scale).astype(jnp.bfloat16)
 
 
+def slot_terms(weight, offset, cell, count, *, start, breadth):
+    offset_x = offset[0]
+    offset_y = offset[1]
+    slots = lax.broadcasted_iota(jnp.int32, cell.shape, 1) + start
+    live = jnp.where(slots < count, 1.0, 0.0)
+    area = jnp.sum(weight, axis=0)
+    first_x = jnp.sum(weight * offset_x, axis=0)
+    first_y = jnp.sum(weight * offset_y, axis=0)
+    second_x = 0.5 * jnp.sum(weight * offset_x * offset_x, axis=0)
+    second_y = 0.5 * jnp.sum(weight * offset_y * offset_y, axis=0)
+    centre = area - 2.5 * (second_x + second_y)
+    inverse = 1.0 / (12.0 * centre)
+    terms = [centre * live]
+    for one, two in ((first_x, second_x), (first_y, second_y)):
+        terms += [
+            (one - two) * inverse,
+            (16.0 * two - 8.0 * one) * inverse,
+            (16.0 * two + 8.0 * one) * inverse,
+            (-one - two) * inverse,
+        ]
+    row = cell // breadth
+    col = cell - row * breadth
+    return terms + [row.astype(jnp.float32), col.astype(jnp.float32)]
+
+
 def record_body(
     count_ref,
-    window_ref,
+    rows_ref,
     above_ref,
     below_ref,
     before_ref,
     after_ref,
-    term_ref,
+    weight_ref,
+    offset_ref,
+    cell_ref,
+    counts_ref,
     out_ref,
     full_ref,
+    rim_ref,
+    term_ref,
     *,
-    fields,
-    height,
-    breadth,
     start,
 ):
     step = pl.program_id(0)
-    batch, _, slots = term_ref.shape
-    edge = REACH * breadth
+    height, fields, breadth = rows_ref.shape
+    batch, _, slots = out_ref.shape
 
     @pl.when(step == 0)
     def fill():
-        full_ref[...] = window_ref[...]
-        full_ref[:fields, :edge] = above_ref[...]
-        full_ref[-fields:, -edge:] = below_ref[...]
-
-    rim = jnp.concatenate([before_ref[...], after_ref[...]], axis=1)
+        for g in range(height // GROUP):
+            for j in range(GROUP + 2 * REACH):
+                r = g * GROUP + j - REACH
+                if r < 0:
+                    part = above_ref[r + REACH]
+                elif r >= height:
+                    part = below_ref[r - height]
+                else:
+                    part = rows_ref[r]
+                full_ref[g * fields : (g + 1) * fields, j * breadth : (j + 1) * breadth] = part
+        rim_ref[...] = jnp.concatenate(
+            [side[i] for side in (before_ref, after_ref) for i in range(REACH)], axis=1
+        )
+        terms = slot_terms(
+            weight_ref[...],
+            offset_ref[...],
+            cell_ref[...],
+            counts_ref[...],
+            start=start,
+            breadth=breadth,
+        )
+        for k, term in enumerate(terms):
+            term_ref[k] = term
+
+    rim = rim_ref[...]
     make = functools.partial(slot_records, fields=fields, height=height, breadth=breadth)
+    take = lambda k, b: term_ref[k, pl.ds(step * batch + b, 1), :]
     if start == 0:
-        terms = jnp.concatenate([term_ref[b] for b in range(batch)], axis=1)
+        terms = [
+            jnp.concatenate([take(k, b) for b in range(batch)], axis=1) for k in range(TERMS)
+        ]
         made = make(terms, full_ref, rim)
         for b in range(batch):
             out_ref[b] = made[:, b * slots : (b + 1) * slots]
@@ -96,7 +147,7 @@
 
             @pl.when(alive)
             def compute():
-                out_ref[b] = make(term_ref[b], full_ref, rim)
+                out_ref[b] = make([take(k, b) for k in range(TERMS)], full_ref, rim)
 
             @pl.when(jnp.logical_not(alive))
             def clear():
@@ -177,74 +228,62 @@
     cells = target_area.shape[0]
     groups = height // GROUP
     span = GROUP + 2 * REACH
-    flat_rows = lambda part: part.reshape(fields, REACH * breadth)
-    flat_cols = lambda part: jnp.swapaxes(part, 1, 2).reshape(fields, REACH * height)
-    above, below = neighbours(
-        flat_rows(source_flux[:, :REACH]),
-        flat_rows(source_flux[:, height - REACH :]),
-        "panel",
-        False,
-    )
-    before, after = neighbours(
-        flat_cols(source_flux[:, :, :REACH]),
-        flat_cols(source_flux[:, :, breadth - REACH :]),
-        "blk",
-        True,
-    )
-    tall = jnp.pad(source_flux, ((0, 0), (REACH, REACH), (0, 0)))
-    window = jnp.stack([tall[:, g * GROUP : g * GROUP + span] for g in range(groups)]).reshape(
-        groups * fields, span * breadth
-    )
-    offset_x = gauss_offset[0]
-    offset_y = gauss_offset[1]
-    slots = lax.broadcasted_iota(jnp.int32, (members, capacity), 1)
-    live = (slots < slot_count[:, None]).astype(jnp.float32)
-    area = jnp.sum(gauss_weight, axis=0)
-    first_x = jnp.sum(gauss_weight * offset_x, axis=0)
-    first_y = jnp.sum(gauss_weight * offset_y, axis=0)
-    second_x = 0.5 * jnp.sum(gauss_weight * offset_x * offset_x, axis=0)
-    second_y = 0.5 * jnp.sum(gauss_weight * offset_y * offset_y, axis=0)
-    centre = area - 2.5 * (second_x + second_y)
-    inverse = 1.0 / (12.0 * centre)
-    taps = []
-    for one, two in ((first_x, second_x), (first_y, second_y)):
-        taps += [
-            (one - two) * inverse,
-            (16.0 * two - 8.0 * one) * inverse,
-            (16.0 * two + 8.0 * one) * inverse,
-            (-one - two) * inverse,
-        ]
-    row = source_cell // breadth
-    col = source_cell - row * breadth
-    terms = [centre * live] + taps + [row.astype(jnp.float32), col.astype(jnp.float32)]
-    terms += [jnp.zeros_like(area)] * (TERMS - len(terms))
-    terms = jnp.stack(terms, axis=1)
+    points = gauss_weight.shape[0]
+    rows = jnp.swapaxes(source_flux, 0, 1)
+    above, below = neighbours(rows[:REACH], rows[height - REACH :], "panel", False)
+    picks = np.zeros((2 * REACH, breadth), np.float32)
+    for i in range(REACH):
+        picks[i, i] = 1.0
+        picks[REACH + i, breadth - REACH + i] = 1.0
+    edges = lax.dot_general(
+        jnp.asarray(picks, jnp.bfloat16),
+        source_flux,
+        (((1,), (2,)), ((), ())),
+        preferred_element_type=jnp.float32,
+    ).astype(jnp.bfloat16)
+    before, after = neighbours(edges[:REACH], edges[REACH:], "blk", True)
     half = capacity // 2
     arrived = []
     for part in range(2):
         records = pl.pallas_call(
-            functools.partial(
-                record_body, fields=fields, height=height, breadth=breadth, start=part * half
-            ),
+            functools.partial(record_body, start=part * half),
             grid_spec=pltpu.PrefetchScalarGridSpec(
                 num_scalar_prefetch=1,
                 grid=(members // OWNERS,),
                 in_specs=[
-                    pl.BlockSpec((groups * fields, span * breadth), lambda i, n: (0, 0)),
-                    pl.BlockSpec((fields, REACH * breadth), lambda i, n: (0, 0)),
-                    pl.BlockSpec((fields, REACH * breadth), lambda i, n: (0, 0)),
-                    pl.BlockSpec((fields, REACH * height), lambda i, n: (0, 0)),
-                    pl.BlockSpec((fields, REACH * height), lambda i, n: (0, 0)),
-                    pl.BlockSpec((OWNERS, TERMS, half), lambda i, n, part=part: (i, 0, part)),
+                    pl.BlockSpec((height, fields, breadth), lambda i, n: (0, 0, 0)),
+                    pl.BlockSpec((REACH, fields, breadth), lambda i, n: (0, 0, 0)),
+                    pl.BlockSpec((REACH, fields, breadth), lambda i, n: (0, 0, 0)),
+                    pl.BlockSpec((REACH, fields, height), lambda i, n: (0, 0, 0)),
+                    pl.BlockSpec((REACH, fields, height), lambda i, n: (0, 0, 0)),
+                    pl.BlockSpec((points, members, half), lambda i, n, part=part: (0, 0, part)),
+                    pl.BlockSpec(
+                        (2, points, members, half), lambda i, n, part=part: (0, 0, 0, part)
+                    ),
+                    pl.BlockSpec((members, half), lambda i, n, part=part: (0, part)),
+                    pl.BlockSpec((members, 1), lambda i, n: (0, 0)),
                 ],
                 out_specs=pl.BlockSpec((OWNERS, fields, half), lambda i, n: (i, 0, 0)),
                 scratch_shapes=[
-                    pltpu.VMEM((groups * fields, span * breadth), jnp.bfloat16)
+                    pltpu.VMEM((groups * fields, span * breadth), jnp.bfloat16),
+                    pltpu.VMEM((fields, 2 * REACH * height), jnp.bfloat16),
+                    pltpu.VMEM((TERMS, members, half), jnp.float32),
                 ],
             ),
             out_shape=jax.ShapeDtypeStruct((members, fields, half), jnp.bfloat16),
             name=f"records_{part}",
-        )(slot_count, window, above, below, before, after, terms)
+        )(
+            slot_count,
+            rows,
+            above,
+            below,
+            before,
+            after,
+            gauss_weight,
+            gauss_offset,
+            source_cell,
+            slot_count.reshape(members, 1),
+        )
         arrived.append(lax.all_to_all(records, "blk", split_axis=0, concat_axis=0, tiled=True))
     highs = cells // LOW
     padded = -(-fields // 16) * 16

time: 78.2 us -> 76.4 us (0.977)
  waiting for transfers between devices: 6.97 us -> 16.7 us
  local copies, waits for them, and re-layouts: 14.4 us -> 5.63 us
  Pallas kernels: 36.3 us -> 33.3 us
  matrix products: 0 us -> 0.97 us
    ppermute x4, waiting for transfers between devices: 0.01 us -> 6.94 us  [neighbours(): return (lax.ppermute(last, axis, up), lax.ppermute(first, axis, down))]
    transpose x3 -> x0, local copies, waits for them, and re-layouts: 3.99 us -> none  [on_device(): jnp.swapaxes(part, 1, 2).reshape(fields, REACH * height)]
    pallas_call x2, Pallas kernels: 25.1 us -> 22.2 us  [on_device(): pl.pallas_call(functools.partial(record_body, start=part * half), grid_sp...]
    all_to_all x2, waiting for transfers between devices: 6.96 us -> 9.73 us  [on_device(): lax.all_to_all(records, 'blk', split_axis=0, concat_axis=0, tiled=True)]
    another operation x6 -> x0, local copies, waits for them, and re-layouts: 2.3 us -> none  [the longest x4 2.16 us: on_device(): terms = jnp.stack(terms, axis=1)]
    all_to_all x2, starting transfers between devices: 9.97 us -> 8.74 us  [on_device(): lax.all_to_all(records, 'blk', split_axis=0, concat_axis=0, tiled=True)]
    unnamed x30 -> x23, local copies, waits for them, and re-layouts: 5.27 us -> 4.18 us
    slice x1 -> x2, local copies, waits for them, and re-layouts: 1.05 us -> 0.02 us  [the longest x1 0.01 us: on_device(): before, after = neighbours(edges[:REACH], edges[REACH:], 'blk', True)]
  transfers between devices with their start and end apart: 6 -> 6, of which waited for: 2 -> 4; matrix products, arithmetic and copies ran while one was open for 15% -> 3% of each run, Pallas kernels for 23% -> 19%
where the time goes in v4:
time: 76.4 us; the launch traced here: 76.3 us
  Pallas kernels  33.3 us (44%)
  starting transfers between devices  19.6 us (26%)
  waiting for transfers between devices  16.7 us (22%)
  local copies, waits for them, and re-layouts  5.63 us (7%)
  matrix products  0.97 us (1%)
    pallas_call x2, Pallas kernels, on_device(): pl.pallas_call(functools.partial(record_body, start=part * half), grid_sp...  22.2 us
    ppermute x4, starting transfers between devices, neighbours(): return (lax.ppermute(last, axis, up), lax.ppermute(first, axis, down))  10.8 us
    all_to_all x2, waiting for transfers between devices, on_device(): lax.all_to_all(records, 'blk', split_axis=0, concat_axis=0, tiled=True)  9.73 us
    all_to_all x2, starting transfers between devices, on_device(): lax.all_to_all(records, 'blk', split_axis=0, concat_axis=0, tiled=True)  8.74 us
    ppermute x4, waiting for transfers between devices, neighbours(): return (lax.ppermute(last, axis, up), lax.ppermute(first, axis, down))  6.94 us
    pallas_call x1, Pallas kernels, on_device(): pl.pallas_call(functools.partial(deposit_last_body, highs=highs, padded=p...  5.77 us
    pallas_call x1, Pallas kernels, on_device(): pl.pallas_call(functools.partial(deposit_first_body, highs=highs, padded=...  5.42 us
    unnamed x23, local copies, waits for them, and re-layouts  4.18 us
  transfers between devices with their start and end apart: 6, of which 4 were waited for; matrix products, arithmetic and copies ran while one was open for 3% of the time, Pallas kernels for 19%

profile of v4, /device:TPU:0, one launch (start us, length us, event | category | flops | bytes accessed | tf_op | source)
XLA Modules:
  0.0 76.3 jit_solution(7997109661352280464)
XLA Ops:
  0.0 0.0 copy-start.10
  0.0 0.0 copy-start.1
  0.0 2.1 %copy.17 = bf16[72,64,128]{2,0,1:T(8,128)(2,1)S(1)} copy(bf16[72,64,128]{2,1,0:T(8,128)(2,1)} %param.8) | data formatting | bytes 2359296 | tf_op args[0]
  2.1 0.0 copy-start
  2.1 0.0 copy-start.9
  2.2 1.4 %collective-permute-start.1 = (bf16[2,72,128]{2,1,0:T(8,128)(2,1)S(1)}, bf16[2,72,128]{2,1,0:T(8,128)(2,1)S(1)}, u32[]{:S(2)}, u32[]{:S(2)}) collective-permute-start(bf16[2,72,128]{2,1,0:T(8,128)(2,1)S(1)} %get-tuple-element.5), channel_id=1, source_target_pairs={{16,0},{32,16},{48,32},{64,48},{80,64},{96,80},{112,96},{17,1},{33... | collective-permute-start | bytes 110600 | tf_op jit(solution)/shard_map/ppermute | solution.py:219
  3.6 3.0 %collective-permute-start = (bf16[2,72,128]{2,1,0:T(8,128)(2,1)S(1)}, bf16[2,72,128]{2,1,0:T(8,128)(2,1)S(1)}, u32[]{:S(2)}, u32[]{:S(2)}) collective-permute-start(bf16[2,72,128]{2,1,0:T(8,128)(2,1)S(1)} %get-tuple-element.6), channel_id=1, source_target_pairs={{0,16},{16,32},{32,48},{48,64},{64,80},{80,96},{96,112},{1,17},{17... | collective-permute-start | bytes 110600 | tf_op jit(solution)/shard_map/ppermute | solution.py:219
  6.6 0.0 copy-done.10
  6.7 0.0 copy-done.1
  6.7 1.0 %fusion = bf16[4,72,64]{1,0,2:T(4,128)(2,1)S(1)} fusion(bf16[4,128,1]{1,0,2:T(4,128)(2,1)S(1)} %copy-done.10, bf16[72,64,128]{2,1,0:T(8,128)(2,1)S(1)} %copy-done.1), kind=kOutput, calls=%fused_computation | convolution fusion | flops 4718592 | bytes 1217536 | tf_op jit(solution)/shard_map/dot_general | solution.py:238
  7.6 0.1 copy.11
  7.8 6.4 %collective-permute-start.3 = (bf16[2,72,64]{2,1,0:T(8,128)(2,1)S(1)}, bf16[2,72,64]{2,1,0:T(8,128)(2,1)S(1)}, u32[]{:S(2)}, u32[]{:S(2)}) collective-permute-start(bf16[2,72,64]{2,1,0:T(8,128)(2,1)S(1)} %get-tuple-element.7), channel_id=1, source_target_pairs={{1,0},{2,1},{3,2},{4,3},{5,4},{6,5},{7,6},{8,7},{9,8},{10,9},{11,1... | collective-permute-start | bytes 55304 | tf_op jit(solution)/shard_map/ppermute | solution.py:219
  14.2 0.0 collective-permute-start.2
  14.2 0.0 copy-done.9
  14.2 0.7 copy.12.counts_ref
  14.9 1.0 %collective-permute-done.3.after_ref = bf16[2,72,64]{2,1,0:T(8,128)(2,1)S(1)} collective-permute-done((bf16[2,72,64]{2,1,0:T(8,128)(2,1)S(1)}, bf16[2,72,64]{2,1,0:T(8,128)(2,1)S(1)}, u32[]{:S(2)}, u32[]{:S(2)}) %collective-permute-start.3) | collective-permute-done | bytes 18464 | tf_op jit(solution)/shard_map/ppermute | solution.py:219
  15.8 0.0 copy-start.6
  15.8 6.0 %collective-permute-done.2.before_ref = bf16[2,72,64]{2,1,0:T(8,128)(2,1)S(1)} collective-permute-done((bf16[2,72,64]{2,1,0:T(8,128)(2,1)S(1)}, bf16[2,72,64]{2,1,0:T(8,128)(2,1)S(1)}, u32[]{:S(2)}, u32[]{:S(2)}) %collective-permute-start.2) | collective-permute-done | bytes 18464 | tf_op jit(solution)/shard_map/ppermute | solution.py:219
  21.8 0.0 copy-start.7
  21.8 0.0 collective-permute-done.1.below_ref
  21.8 0.0 copy-start.4
  21.8 0.0 collective-permute-done.above_ref
  21.8 0.0 copy-done
  21.8 0.0 copy-done.6
  21.8 0.6 copy-done.7
  22.4 0.0 copy-done.4
  22.4 0.0 copy-start.5
  22.4 0.6 copy-done.5
  23.0 12.8 %records_0.1 = bf16[16,72,256]{2,1,0:T(8,128)(2,1)} custom-call(s32[16]{0:T(128)} %count_ref.3, bf16[64,72,128]{2,1,0:T(8,128)(2,1)} %bitcast.8, bf16[2,72,128]{2,1,0:T(8,128)(2,1)} %copy-done.5, bf16[2,72,128]{2,1,0:T(8,128)(2,1)} %copy-done.4, bf16[2,72,64]{2,1,0:T(8,128)(2,1)} %copy-done.7, bf16[2,72,64]{2,1,0:T(8,128)(2,1)} %copy-done.6, ...), custom_call_target="tpu_custom_call" | custom-call | tf_op jit(solution)/shard_map/records_0/pallas_call | solution.py:248
  35.8 3.6 %all-to-all-start.1 = ((bf16[16,72,256]{2,1,0:T(8,128)(2,1)}), bf16[16,72,256]{2,1,0:T(8,128)(2,1)S(1)}, u32[]{:S(2)}, u32[]{:S(2)}) async-start(bf16[16,72,256]{2,1,0:T(8,128)(2,1)} %records_0.1), calls=%async_computation.1 | async-start | bytes 1179648 | tf_op jit(solution)/shard_map/all_to_all | solution.py:287
  39.4 0.0 copy-start.8
  39.4 9.4 %records_1.1 = bf16[16,72,256]{2,1,0:T(8,128)(2,1)} custom-call(s32[16]{0:T(128)} %count_ref.3, bf16[64,72,128]{2,1,0:T(8,128)(2,1)} %bitcast.9, bf16[2,72,128]{2,1,0:T(8,128)(2,1)} %copy-done.5, bf16[2,72,128]{2,1,0:T(8,128)(2,1)} %copy-done.4, bf16[2,72,64]{2,1,0:T(8,128)(2,1)} %copy-done.7, bf16[2,72,64]{2,1,0:T(8,128)(2,1)} %copy-done.6, ...), custom_call_target="tpu_custom_call" | custom-call | tf_op jit(solution)/shard_map/records_1/pallas_call | solution.py:248
  48.8 3.3 %all-to-all-done.1.record_ref = bf16[16,72,256]{2,1,0:T(8,128)(2,1)S(1)} async-done(((bf16[16,72,256]{2,1,0:T(8,128)(2,1)}), bf16[16,72,256]{2,1,0:T(8,128)(2,1)S(1)}, u32[]{:S(2)}, u32[]{:S(2)}) %all-to-all-start.1) | async-done | bytes 589856 | tf_op jit(solution)/shard_map/all_to_all | solution.py:287
  52.1 0.0 copy-start.3
  52.1 5.2 %all-to-all-start = ((bf16[16,72,256]{2,1,0:T(8,128)(2,1)}), bf16[16,72,256]{2,1,0:T(8,128)(2,1)S(1)}, u32[]{:S(2)}, u32[]{:S(2)}) async-start(bf16[16,72,256]{2,1,0:T(8,128)(2,1)} %records_1.1), calls=%async_computation | async-start | bytes 1179648 | tf_op jit(solution)/shard_map/all_to_all | solution.py:287
  57.3 0.0 copy-done.8
  57.3 0.6 reshape.11.target_ref
  57.9 0.0 copy-done.3
  57.9 5.4 %deposit_0.1.before_ref = f32[1280,256]{1,0:T(8,128)} custom-call(bf16[16,72,256]{2,1,0:T(8,128)(2,1)} %copy-done.3, s32[16,1,512]{2,1,0:T(1,128)} %reshape.11.target_ref), custom_call_target="tpu_custom_call" | custom-call | tf_op jit(solution)/shard_map/deposit_0/pallas_call | solution.py:293
  63.4 6.4 %all-to-all-done.record_ref = bf16[16,72,256]{2,1,0:T(8,128)(2,1)S(1)} async-done(((bf16[16,72,256]{2,1,0:T(8,128)(2,1)}), bf16[16,72,256]{2,1,0:T(8,128)(2,1)S(1)}, u32[]{:S(2)}, u32[]{:S(2)}) %all-to-all-start) | async-done | bytes 589856 | tf_op jit(solution)/shard_map/all_to_all | solution.py:287
  69.8 0.0 copy-start.2
  69.8 0.8 %copy-done.2 = bf16[16,72,256]{2,1,0:T(8,128)(2,1)} copy-done((bf16[16,72,256]{2,1,0:T(8,128)(2,1)}, bf16[16,72,256]{2,1,0:T(8,128)(2,1)S(1)}, u32[]{:S(2)}) %copy-start.2) | copy-done | bytes 589848
  70.6 5.8 %deposit_1.1 = bf16[72,4096]{1,0:T(8,128)(2,1)} custom-call(bf16[16,72,256]{2,1,0:T(8,128)(2,1)} %copy-done.2, s32[16,1,512]{2,1,0:T(1,128)} %reshape.11.target_ref, f32[1280,256]{1,0:T(8,128)} %deposit_0.1.before_ref, f32[1,4096]{1,0:T(1,128)} %bitcast.10), custom_call_target="tpu_custom_call" | custom-call | tf_op jit(solution)/shard_map/deposit_1/pallas_call | solution.py:301
  (2 shorter events, 0.0 us)
Async XLA Ops:
  0.0 6.6 %copy-start.10 = (bf16[4,128,1]{1,0,2:T(4,128)(2,1)S(1)}, bf16[4,128,1]{1,0,2:T(4,128)(2,1)}, u32[]{:S(2)}) copy-start(bf16[4,128,1]{1,0,2:T(4,128)(2,1)} %constant.8) | copy-start | bytes 3076
  0.0 6.7 %copy-start.1 = (bf16[72,64,128]{2,1,0:T(8,128)(2,1)S(1)}, bf16[72,64,128]{2,1,0:T(8,128)(2,1)}, u32[]{:S(2)}) copy-start(bf16[72,64,128]{2,1,0:T(8,128)(2,1)} %param.8) | copy-start | bytes 3538948
  2.1 19.7 %copy-start = (bf16[72,64,128]{2,0,1:T(8,128)(2,1)}, bf16[72,64,128]{2,0,1:T(8,128)(2,1)S(1)}, u32[]{:S(2)}) copy-start(bf16[72,64,128]{2,0,1:T(8,128)(2,1)S(1)} %copy.17) | copy-start | bytes 3538948
  2.1 12.0 %copy-start.9 = (s32[16]{0:T(128)S(1)}, s32[16]{0:T(128)}, u32[]{:S(2)}) copy-start(s32[16]{0:T(128)} %count_ref.3) | copy-start | bytes 196
  2.2 19.6 %collective-permute-start.1 = (bf16[2,72,128]{2,1,0:T(8,128)(2,1)S(1)}, bf16[2,72,128]{2,1,0:T(8,128)(2,1)S(1)}, u32[]{:S(2)}, u32[]{:S(2)}) collective-permute-start(bf16[2,72,128]{2,1,0:T(8,128)(2,1)S(1)} %get-tuple-element.5), channel_id=1, source_target_pairs={{16,0},{32,16},{48,32},{64,48},{80,64},{96,80},{112,96},{17,1},{33... | collective-permute-start | bytes 110600 | tf_op jit(solution)/shard_map/ppermute | solution.py:219
  3.6 18.2 %collective-permute-start = (bf16[2,72,128]{2,1,0:T(8,128)(2,1)S(1)}, bf16[2,72,128]{2,1,0:T(8,128)(2,1)S(1)}, u32[]{:S(2)}, u32[]{:S(2)}) collective-permute-start(bf16[2,72,128]{2,1,0:T(8,128)(2,1)S(1)} %get-tuple-element.6), channel_id=1, source_target_pairs={{0,16},{16,32},{32,48},{48,64},{64,80},{80,96},{96,112},{1,17},{17... | collective-permute-start | bytes 110600 | tf_op jit(solution)/shard_map/ppermute | solution.py:219
  7.8 8.0 %collective-permute-start.3 = (bf16[2,72,64]{2,1,0:T(8,128)(2,1)S(1)}, bf16[2,72,64]{2,1,0:T(8,128)(2,1)S(1)}, u32[]{:S(2)}, u32[]{:S(2)}) collective-permute-start(bf16[2,72,64]{2,1,0:T(8,128)(2,1)S(1)} %get-tuple-element.7), channel_id=1, source_target_pairs={{1,0},{2,1},{3,2},{4,3},{5,4},{6,5},{7,6},{8,7},{9,8},{10,9},{11,1... | collective-permute-start | bytes 55304 | tf_op jit(solution)/shard_map/ppermute | solution.py:219
  14.2 7.6 %collective-permute-start.2 = (bf16[2,72,64]{2,1,0:T(8,128)(2,1)S(1)}, bf16[2,72,64]{2,1,0:T(8,128)(2,1)S(1)}, u32[]{:S(2)}, u32[]{:S(2)}) collective-permute-start(bf16[2,72,64]{2,1,0:T(8,128)(2,1)S(1)} %get-tuple-element.8), channel_id=1, source_target_pairs={{0,1},{1,2},{2,3},{3,4},{4,5},{5,6},{6,7},{7,8},{8,9},{9,10},{10,1... | collective-permute-start | bytes 55304 | tf_op jit(solution)/shard_map/ppermute | solution.py:219
  15.8 6.0 %copy-start.6 = (bf16[2,72,64]{2,1,0:T(8,128)(2,1)}, bf16[2,72,64]{2,1,0:T(8,128)(2,1)S(1)}, u32[]{:S(2)}) copy-start(bf16[2,72,64]{2,1,0:T(8,128)(2,1)S(1)} %collective-permute-done.3.after_ref) | copy-start | bytes 55300
  21.8 0.6 copy-start.7
  21.8 0.6 copy-start.4
  22.4 0.6 copy-start.5
  35.8 16.3 %all-to-all-start.1 = ((bf16[16,72,256]{2,1,0:T(8,128)(2,1)}), bf16[16,72,256]{2,1,0:T(8,128)(2,1)S(1)}, u32[]{:S(2)}, u32[]{:S(2)}) async-start(bf16[16,72,256]{2,1,0:T(8,128)(2,1)} %records_0.1), calls=%async_computation.1 | async-start | bytes 1179648 | tf_op jit(solution)/shard_map/all_to_all | solution.py:287
  39.4 17.9 %copy-start.8 = (s32[16,512]{1,0:T(8,128)S(1)}, s32[16,512]{1,0:T(8,128)}, u32[]{:S(2)}) copy-start(s32[16,512]{1,0:T(8,128)} %param.13) | copy-start | bytes 98308
  52.1 5.8 %copy-start.3 = (bf16[16,72,256]{2,1,0:T(8,128)(2,1)}, bf16[16,72,256]{2,1,0:T(8,128)(2,1)S(1)}, u32[]{:S(2)}) copy-start(bf16[16,72,256]{2,1,0:T(8,128)(2,1)S(1)} %all-to-all-done.1.record_ref) | copy-start | bytes 1769476
  52.1 17.6 %all-to-all-start = ((bf16[16,72,256]{2,1,0:T(8,128)(2,1)}), bf16[16,72,256]{2,1,0:T(8,128)(2,1)S(1)}, u32[]{:S(2)}, u32[]{:S(2)}) async-start(bf16[16,72,256]{2,1,0:T(8,128)(2,1)} %records_1.1), calls=%async_computation | async-start | bytes 1179648 | tf_op jit(solution)/shard_map/all_to_all | solution.py:287
  69.8 0.8 %copy-start.2 = (bf16[16,72,256]{2,1,0:T(8,128)(2,1)}, bf16[16,72,256]{2,1,0:T(8,128)(2,1)S(1)}, u32[]{:S(2)}) copy-start(bf16[16,72,256]{2,1,0:T(8,128)(2,1)S(1)} %all-to-all-done.record_ref) | copy-start | bytes 1769476

commit v5 on v4

--- a/solution.py
+++ b/solution.py
@@ -13,7 +13,7 @@
 LOW = 256
 TERMS = 11
 BATCH = 8
-OWNERS = 4
+OWNERS = (8, 4)
 
 
 def slot_records(terms, window_ref, rim, *, fields, height, breadth):
@@ -28,30 +28,35 @@
     shifts = (-2, -1, 1, 2)
     group = row // GROUP
     local = row - group * GROUP + REACH
-    gap = lax.broadcasted_iota(jnp.int32, (breadth, slots), 0) - col
-    here = jnp.where(gap == 0, 1.0, 0.0).astype(jnp.bfloat16)
-    beside = jnp.zeros((breadth, slots), jnp.float32)
+    one = jnp.ones((), jnp.bfloat16)
+    zero = jnp.zeros((), jnp.bfloat16)
+    place = lax.broadcasted_iota(jnp.int32, (breadth, slots), 0).astype(jnp.float32)
+    gap = place.astype(jnp.bfloat16) - terms[10].astype(jnp.bfloat16)
+    here = jnp.where(gap == 0, one, zero)
+    beside = jnp.zeros((breadth, slots), jnp.bfloat16)
     for shift, tap in zip(shifts, col_taps):
-        beside = jnp.where(gap == shift, tap, beside)
-    beside = beside.astype(jnp.bfloat16)
+        beside = jnp.where(gap == shift, tap.astype(jnp.bfloat16), beside)
+    away = lax.broadcasted_iota(jnp.int32, (2 * GROUP, slots), 0) - local
+    centres = jnp.where(away == 0, 1.0, 0.0)
+    weights = centres
+    for shift, tap in zip(shifts, row_taps):
+        weights = jnp.where(away == shift, tap, weights)
     pieces = []
     for j in range(span):
-        centre = jnp.where(local == j, 1.0, 0.0)
-        weight = centre
-        for shift, tap in zip(shifts, row_taps):
-            weight = jnp.where(local + shift == j, tap, weight)
-        pieces.append(here * weight.astype(jnp.bfloat16) + beside * centre.astype(jnp.bfloat16))
+        weight = weights[j : j + 1].astype(jnp.bfloat16)
+        centre = centres[j : j + 1].astype(jnp.bfloat16)
+        pieces.append(here * weight + beside * centre)
     table = jnp.concatenate(pieces, axis=0)
     product = jnp.dot(window_ref[...], table, preferred_element_type=jnp.float32)
     same_row = jnp.where(
-        lax.broadcasted_iota(jnp.int32, (height, slots), 0) == row, 1.0, 0.0
-    ).astype(jnp.bfloat16)
-    rim_pieces = []
-    for place in (-2, -1, breadth, breadth + 1):
-        weight = jnp.zeros((1, slots), jnp.float32)
-        for shift, tap in zip(shifts, col_taps):
-            weight = jnp.where(col + shift == place, tap, weight)
-        rim_pieces.append(same_row * weight.astype(jnp.bfloat16))
+        place[:height].astype(jnp.bfloat16) == terms[9].astype(jnp.bfloat16), one, zero
+    )
+    side = lax.broadcasted_iota(jnp.int32, (GROUP, slots), 0)
+    reach = jnp.where(side < REACH, side - REACH, side + (breadth - REACH)) - col
+    outer = jnp.zeros((GROUP, slots), jnp.float32)
+    for shift, tap in zip(shifts, col_taps):
+        outer = jnp.where(reach == shift, tap, outer)
+    rim_pieces = [same_row * outer[i : i + 1].astype(jnp.bfloat16) for i in range(2 * REACH)]
     total = jnp.dot(rim, jnp.concatenate(rim_pieces, axis=0), preferred_element_type=jnp.float32)
     for g in range(groups):
         total = total + jnp.where(group == g, product[g * fields : (g + 1) * fields], 0.0)
@@ -154,30 +159,35 @@
                 out_ref[b] = jnp.zeros((fields, slots), out_ref.dtype)
 
 
-def deposit_part(record_ref, target_ref, *, highs, padded):
-    batch, fields, _ = record_ref.shape
-    target = jnp.concatenate([target_ref[b] for b in range(batch)], axis=1)
-    values = jnp.concatenate([record_ref[b] for b in range(batch)], axis=1).astype(jnp.float32)
+def deposit_part(record_ref, target_ref, *, highs, padded, start):
+    step = pl.program_id(0)
+    _, fields, half = record_ref.shape
+    sources = [step * BATCH + b for b in range(BATCH)]
+    target = jnp.concatenate(
+        [target_ref[pl.ds(k, 1), start : start + half] for k in sources], axis=1
+    )
+    values = jnp.concatenate([record_ref[k] for k in sources], axis=1).astype(jnp.float32)
     slots = target.shape[1]
     values = jnp.concatenate(
         [values, jnp.zeros((padded - fields, slots), jnp.float32)], axis=0
     ).astype(jnp.bfloat16)
     high = target // LOW
-    low = target - high * LOW
+    low = (target - high * LOW).astype(jnp.float32).astype(jnp.bfloat16)
     spread = jnp.concatenate(
         [values * jnp.where(high == h, 1.0, 0.0).astype(jnp.bfloat16) for h in range(highs)],
         axis=0,
     )
+    lane = lax.broadcasted_iota(jnp.int32, (LOW, slots), 0).astype(jnp.float32)
     place = jnp.where(
-        lax.broadcasted_iota(jnp.int32, (LOW, slots), 0) == low, 1.0, 0.0
-    ).astype(jnp.bfloat16)
+        lane.astype(jnp.bfloat16) == low, jnp.ones((), jnp.bfloat16), jnp.zeros((), jnp.bfloat16)
+    )
     return lax.dot_general(
         spread, place, (((1,), (1,)), ((), ())), preferred_element_type=jnp.float32
     )
 
 
 def deposit_first_body(record_ref, target_ref, total_ref, *, highs, padded):
-    part = deposit_part(record_ref, target_ref, highs=highs, padded=padded)
+    part = deposit_part(record_ref, target_ref, highs=highs, padded=padded, start=0)
 
     @pl.when(pl.program_id(0) == 0)
     def first():
@@ -192,23 +202,27 @@
     record_ref, target_ref, before_ref, area_ref, out_ref, total_ref, *, highs, padded
 ):
     step = pl.program_id(0)
+    last = pl.num_programs(0) - 1
     fields = out_ref.shape[0]
-    part = deposit_part(record_ref, target_ref, highs=highs, padded=padded)
+    part = deposit_part(
+        record_ref, target_ref, highs=highs, padded=padded, start=record_ref.shape[2]
+    )
 
     @pl.when(step == 0)
     def first():
         total_ref[...] = before_ref[...] + part
 
-    @pl.when(step > 0)
+    @pl.when(jnp.logical_and(step > 0, step < last))
     def later():
         total_ref[...] = total_ref[...] + part
 
-    @pl.when(step == pl.num_programs(0) - 1)
+    @pl.when(step == last)
     def finish():
         for h in range(highs):
-            area = area_ref[:, h * LOW : (h + 1) * LOW]
+            cut = slice(h * padded, h * padded + fields)
+            inverse = 1.0 / area_ref[:, h * LOW : (h + 1) * LOW]
             out_ref[:, h * LOW : (h + 1) * LOW] = (
-                total_ref[h * padded : h * padded + fields, :] / area
+                (total_ref[cut, :] + part[cut]) * inverse
             ).astype(jnp.bfloat16)
 
 
@@ -244,12 +258,12 @@
     before, after = neighbours(edges[:REACH], edges[REACH:], "blk", True)
     half = capacity // 2
     arrived = []
-    for part in range(2):
+    for part, owners in enumerate(OWNERS):
         records = pl.pallas_call(
             functools.partial(record_body, start=part * half),
             grid_spec=pltpu.PrefetchScalarGridSpec(
                 num_scalar_prefetch=1,
-                grid=(members // OWNERS,),
+                grid=(members // owners,),
                 in_specs=[
                     pl.BlockSpec((height, fields, breadth), lambda i, n: (0, 0, 0)),
                     pl.BlockSpec((REACH, fields, breadth), lambda i, n: (0, 0, 0)),
@@ -263,7 +277,7 @@
                     pl.BlockSpec((members, half), lambda i, n, part=part: (0, part)),
                     pl.BlockSpec((members, 1), lambda i, n: (0, 0)),
                 ],
-                out_specs=pl.BlockSpec((OWNERS, fields, half), lambda i, n: (i, 0, 0)),
+                out_specs=pl.BlockSpec((owners, fields, half), lambda i, n: (i, 0, 0)),
                 scratch_shapes=[
                     pltpu.VMEM((groups * fields, span * breadth), jnp.bfloat16),
                     pltpu.VMEM((fields, 2 * REACH * height), jnp.bfloat16),
@@ -287,23 +301,23 @@
         arrived.append(lax.all_to_all(records, "blk", split_axis=0, concat_axis=0, tiled=True))
     highs = cells // LOW
     padded = -(-fields // 16) * 16
-    targets = target_cell.reshape(members, 1, capacity)
-    record_spec = pl.BlockSpec((BATCH, fields, half), lambda i: (i, 0, 0))
+    record_spec = pl.BlockSpec(memory_space=pltpu.VMEM)
+    target_spec = pl.BlockSpec((members, capacity), lambda i: (0, 0))
     total_spec = pl.BlockSpec((highs * padded, LOW), lambda i: (0, 0))
     before = pl.pallas_call(
         functools.partial(deposit_first_body, highs=highs, padded=padded),
         grid=(members // BATCH,),
-        in_specs=[record_spec, pl.BlockSpec((BATCH, 1, half), lambda i: (i, 0, 0))],
+        in_specs=[record_spec, target_spec],
         out_specs=total_spec,
         out_shape=jax.ShapeDtypeStruct((highs * padded, LOW), jnp.float32),
         name="deposit_0",
-    )(arrived[0], targets)
+    )(arrived[0], target_cell)
     return pl.pallas_call(
         functools.partial(deposit_last_body, highs=highs, padded=padded),
         grid=(members // BATCH,),
         in_specs=[
             record_spec,
-            pl.BlockSpec((BATCH, 1, half), lambda i: (i, 0, 1)),
+            target_spec,
             total_spec,
             pl.BlockSpec((1, cells), lambda i: (0, 0)),
         ],
@@ -311,7 +325,7 @@
         out_shape=jax.ShapeDtypeStruct((fields, cells), jnp.bfloat16),
         scratch_shapes=[pltpu.VMEM((highs * padded, LOW), jnp.float32)],
         name="deposit_1",
-    )(arrived[1], targets, before, target_area.reshape(1, cells))
+    )(arrived[1], target_cell, before, target_area.reshape(1, cells))
 
 
 def solution(mesh):

time: 76.4 us -> 74.7 us (0.978)
  the two profiles are of different devices: /device:TPU:0 before, /device:TPU:8 now
where the time goes in v5:
time: 74.7 us; the launch traced here: 74.4 us
  Pallas kernels  32.1 us (43%)
  starting transfers between devices  18.4 us (25%)
  waiting for transfers between devices  17.7 us (24%)
  local copies, waits for them, and re-layouts  5.03 us (7%)
  matrix products  0.97 us (1%)
    pallas_call x2, Pallas kernels, on_device(): pl.pallas_call(functools.partial(record_body, start=part * half), grid_sp...  20.8 us
    all_to_all x2, waiting for transfers between devices, on_device(): lax.all_to_all(records, 'blk', split_axis=0, concat_axis=0, tiled=True)  10.8 us
    ppermute x4, starting transfers between devices, neighbours(): return (lax.ppermute(last, axis, up), lax.ppermute(first, axis, down))  10.8 us
    all_to_all x2, starting transfers between devices, on_device(): lax.all_to_all(records, 'blk', split_axis=0, concat_axis=0, tiled=True)  7.69 us
    ppermute x4, waiting for transfers between devices, neighbours(): return (lax.ppermute(last, axis, up), lax.ppermute(first, axis, down))  6.94 us
    pallas_call x1, Pallas kernels, on_device(): pl.pallas_call(functools.partial(deposit_last_body, highs=highs, padded=p...  5.77 us
    pallas_call x1, Pallas kernels, on_device(): pl.pallas_call(functools.partial(deposit_first_body, highs=highs, padded=...  5.54 us
    unnamed x21, local copies, waits for them, and re-layouts  4.22 us
  transfers between devices with their start and end apart: 6, of which 4 were waited for; matrix products, arithmetic and copies ran while one was open for 2% of the time, Pallas kernels for 19%

profile of v5, /device:TPU:8, one launch (start us, length us, event | category | flops | bytes accessed | tf_op | source)
XLA Modules:
  0.0 74.4 jit_solution(1825647150548412606)
XLA Ops:
  0.0 0.0 copy-start.9
  0.0 0.0 copy-start.1
  0.0 2.1 %copy.17 = bf16[72,64,128]{2,0,1:T(8,128)(2,1)S(1)} copy(bf16[72,64,128]{2,1,0:T(8,128)(2,1)} %param.8) | data formatting | bytes 2359296 | tf_op args[0]
  2.1 0.0 copy-start
  2.1 0.0 copy-start.8
  2.2 2.1 %collective-permute-start.1 = (bf16[2,72,128]{2,1,0:T(8,128)(2,1)S(1)}, bf16[2,72,128]{2,1,0:T(8,128)(2,1)S(1)}, u32[]{:S(2)}, u32[]{:S(2)}) collective-permute-start(bf16[2,72,128]{2,1,0:T(8,128)(2,1)S(1)} %get-tuple-element.5), channel_id=1, source_target_pairs={{16,0},{32,16},{48,32},{64,48},{80,64},{96,80},{112,96},{17,1},{33... | collective-permute-start | bytes 110600 | tf_op jit(solution)/shard_map/ppermute | solution.py:233
  4.2 2.4 %collective-permute-start = (bf16[2,72,128]{2,1,0:T(8,128)(2,1)S(1)}, bf16[2,72,128]{2,1,0:T(8,128)(2,1)S(1)}, u32[]{:S(2)}, u32[]{:S(2)}) collective-permute-start(bf16[2,72,128]{2,1,0:T(8,128)(2,1)S(1)} %get-tuple-element.6), channel_id=1, source_target_pairs={{0,16},{16,32},{32,48},{48,64},{64,80},{80,96},{96,112},{1,17},{17... | collective-permute-start | bytes 110600 | tf_op jit(solution)/shard_map/ppermute | solution.py:233
  6.6 0.0 copy-done.9
  6.7 0.0 copy-done.1
  6.7 1.0 %fusion = bf16[4,72,64]{1,0,2:T(4,128)(2,1)S(1)} fusion(bf16[4,128,1]{1,0,2:T(4,128)(2,1)S(1)} %copy-done.9, bf16[72,64,128]{2,1,0:T(8,128)(2,1)S(1)} %copy-done.1), kind=kOutput, calls=%fused_computation | convolution fusion | flops 4718592 | bytes 1217536 | tf_op jit(solution)/shard_map/dot_general | solution.py:252
  7.6 0.1 copy.11
  7.8 6.3 %collective-permute-start.3 = (bf16[2,72,64]{2,1,0:T(8,128)(2,1)S(1)}, bf16[2,72,64]{2,1,0:T(8,128)(2,1)S(1)}, u32[]{:S(2)}, u32[]{:S(2)}) collective-permute-start(bf16[2,72,64]{2,1,0:T(8,128)(2,1)S(1)} %get-tuple-element.7), channel_id=1, source_target_pairs={{1,0},{2,1},{3,2},{4,3},{5,4},{6,5},{7,6},{8,7},{9,8},{10,9},{11,1... | collective-permute-start | bytes 55304 | tf_op jit(solution)/shard_map/ppermute | solution.py:233
  14.1 0.0 collective-permute-start.2
  14.1 0.0 copy-done.8
  14.1 0.7 copy.12.counts_ref
  14.8 1.0 %collective-permute-done.3.after_ref = bf16[2,72,64]{2,1,0:T(8,128)(2,1)S(1)} collective-permute-done((bf16[2,72,64]{2,1,0:T(8,128)(2,1)S(1)}, bf16[2,72,64]{2,1,0:T(8,128)(2,1)S(1)}, u32[]{:S(2)}, u32[]{:S(2)}) %collective-permute-start.3) | collective-permute-done | bytes 18464 | tf_op jit(solution)/shard_map/ppermute | solution.py:233
  15.7 0.0 copy-start.6
  15.7 6.0 %collective-permute-done.2.before_ref = bf16[2,72,64]{2,1,0:T(8,128)(2,1)S(1)} collective-permute-done((bf16[2,72,64]{2,1,0:T(8,128)(2,1)S(1)}, bf16[2,72,64]{2,1,0:T(8,128)(2,1)S(1)}, u32[]{:S(2)}, u32[]{:S(2)}) %collective-permute-start.2) | collective-permute-done | bytes 18464 | tf_op jit(solution)/shard_map/ppermute | solution.py:233
  21.7 0.0 copy-start.7
  21.7 0.0 collective-permute-done.1.below_ref
  21.7 0.0 copy-start.4
  21.7 0.0 collective-permute-done.above_ref
  21.7 0.0 copy-done
  21.7 0.0 copy-done.6
  21.7 0.6 copy-done.7
  22.3 0.0 copy-done.4
  22.4 0.0 copy-start.5
  22.4 0.6 copy-done.5
  23.0 11.9 %records_0.1 = bf16[16,72,256]{2,1,0:T(8,128)(2,1)} custom-call(s32[16]{0:T(128)} %count_ref.3, bf16[64,72,128]{2,1,0:T(8,128)(2,1)} %bitcast.8, bf16[2,72,128]{2,1,0:T(8,128)(2,1)} %copy-done.5, bf16[2,72,128]{2,1,0:T(8,128)(2,1)} %copy-done.4, bf16[2,72,64]{2,1,0:T(8,128)(2,1)} %copy-done.7, bf16[2,72,64]{2,1,0:T(8,128)(2,1)} %copy-done.6, ...), custom_call_target="tpu_custom_call" | custom-call | tf_op jit(solution)/shard_map/records_0/pallas_call | solution.py:262
  34.8 3.6 %all-to-all-start.1 = ((bf16[16,72,256]{2,1,0:T(8,128)(2,1)}), bf16[16,72,256]{2,1,0:T(8,128)(2,1)S(1)}, u32[]{:S(2)}, u32[]{:S(2)}) async-start(bf16[16,72,256]{2,1,0:T(8,128)(2,1)} %records_0.1), calls=%async_computation.1 | async-start | bytes 1179648 | tf_op jit(solution)/shard_map/all_to_all | solution.py:301
  38.4 8.9 %records_1.1 = bf16[16,72,256]{2,1,0:T(8,128)(2,1)} custom-call(s32[16]{0:T(128)} %count_ref.3, bf16[64,72,128]{2,1,0:T(8,128)(2,1)} %bitcast.9, bf16[2,72,128]{2,1,0:T(8,128)(2,1)} %copy-done.5, bf16[2,72,128]{2,1,0:T(8,128)(2,1)} %copy-done.4, bf16[2,72,64]{2,1,0:T(8,128)(2,1)} %copy-done.7, bf16[2,72,64]{2,1,0:T(8,128)(2,1)} %copy-done.6, ...), custom_call_target="tpu_custom_call" | custom-call | tf_op jit(solution)/shard_map/records_1/pallas_call | solution.py:262
  47.3 3.8 %all-to-all-done.1.record_ref = bf16[16,72,256]{2,1,0:T(8,128)(2,1)S(1)} async-done(((bf16[16,72,256]{2,1,0:T(8,128)(2,1)}), bf16[16,72,256]{2,1,0:T(8,128)(2,1)S(1)}, u32[]{:S(2)}, u32[]{:S(2)}) %all-to-all-start.1) | async-done | bytes 589856 | tf_op jit(solution)/shard_map/all_to_all | solution.py:301
  51.1 0.0 copy-start.3
  51.1 4.1 %all-to-all-start = ((bf16[16,72,256]{2,1,0:T(8,128)(2,1)}), bf16[16,72,256]{2,1,0:T(8,128)(2,1)S(1)}, u32[]{:S(2)}, u32[]{:S(2)}) async-start(bf16[16,72,256]{2,1,0:T(8,128)(2,1)} %records_1.1), calls=%async_computation | async-start | bytes 1179648 | tf_op jit(solution)/shard_map/all_to_all | solution.py:301
  55.2 0.0 copy-done.3
  55.3 5.5 %deposit_0.1.before_ref = f32[1280,256]{1,0:T(8,128)} custom-call(bf16[16,72,256]{2,1,0:T(8,128)(2,1)} %copy-done.3, s32[16,512]{1,0:T(8,128)} %target_ref.3), custom_call_target="tpu_custom_call" | custom-call | tf_op jit(solution)/shard_map/deposit_0/pallas_call | solution.py:307
  60.8 7.0 %all-to-all-done.record_ref = bf16[16,72,256]{2,1,0:T(8,128)(2,1)S(1)} async-done(((bf16[16,72,256]{2,1,0:T(8,128)(2,1)}), bf16[16,72,256]{2,1,0:T(8,128)(2,1)S(1)}, u32[]{:S(2)}, u32[]{:S(2)}) %all-to-all-start) | async-done | bytes 589856 | tf_op jit(solution)/shard_map/all_to_all | solution.py:301
  67.8 0.0 copy-start.2
  67.8 0.8 %copy-done.2 = bf16[16,72,256]{2,1,0:T(8,128)(2,1)} copy-done((bf16[16,72,256]{2,1,0:T(8,128)(2,1)}, bf16[16,72,256]{2,1,0:T(8,128)(2,1)S(1)}, u32[]{:S(2)}) %copy-start.2) | copy-done | bytes 589848
  68.6 5.8 %deposit_1.1 = bf16[72,4096]{1,0:T(8,128)(2,1)} custom-call(bf16[16,72,256]{2,1,0:T(8,128)(2,1)} %copy-done.2, s32[16,512]{1,0:T(8,128)} %target_ref.3, f32[1280,256]{1,0:T(8,128)} %deposit_0.1.before_ref, f32[1,4096]{1,0:T(1,128)} %bitcast.10), custom_call_target="tpu_custom_call" | custom-call | tf_op jit(solution)/shard_map/deposit_1/pallas_call | solution.py:315
  (2 shorter events, 0.0 us)
Async XLA Ops:
  0.0 6.7 %copy-start.9 = (bf16[4,128,1]{1,0,2:T(4,128)(2,1)S(1)}, bf16[4,128,1]{1,0,2:T(4,128)(2,1)}, u32[]{:S(2)}) copy-start(bf16[4,128,1]{1,0,2:T(4,128)(2,1)} %constant.8) | copy-start | bytes 3076
  0.0 6.7 %copy-start.1 = (bf16[72,64,128]{2,1,0:T(8,128)(2,1)S(1)}, bf16[72,64,128]{2,1,0:T(8,128)(2,1)}, u32[]{:S(2)}) copy-start(bf16[72,64,128]{2,1,0:T(8,128)(2,1)} %param.8) | copy-start | bytes 3538948
  2.1 19.6 %copy-start = (bf16[72,64,128]{2,0,1:T(8,128)(2,1)}, bf16[72,64,128]{2,0,1:T(8,128)(2,1)S(1)}, u32[]{:S(2)}) copy-start(bf16[72,64,128]{2,0,1:T(8,128)(2,1)S(1)} %copy.17) | copy-start | bytes 3538948
  2.1 12.0 %copy-start.8 = (s32[16]{0:T(128)S(1)}, s32[16]{0:T(128)}, u32[]{:S(2)}) copy-start(s32[16]{0:T(128)} %count_ref.3) | copy-start | bytes 196
  2.2 19.5 %collective-permute-start.1 = (bf16[2,72,128]{2,1,0:T(8,128)(2,1)S(1)}, bf16[2,72,128]{2,1,0:T(8,128)(2,1)S(1)}, u32[]{:S(2)}, u32[]{:S(2)}) collective-permute-start(bf16[2,72,128]{2,1,0:T(8,128)(2,1)S(1)} %get-tuple-element.5), channel_id=1, source_target_pairs={{16,0},{32,16},{48,32},{64,48},{80,64},{96,80},{112,96},{17,1},{33... | collective-permute-start | bytes 110600 | tf_op jit(solution)/shard_map/ppermute | solution.py:233
  4.2 17.5 %collective-permute-start = (bf16[2,72,128]{2,1,0:T(8,128)(2,1)S(1)}, bf16[2,72,128]{2,1,0:T(8,128)(2,1)S(1)}, u32[]{:S(2)}, u32[]{:S(2)}) collective-permute-start(bf16[2,72,128]{2,1,0:T(8,128)(2,1)S(1)} %get-tuple-element.6), channel_id=1, source_target_pairs={{0,16},{16,32},{32,48},{48,64},{64,80},{80,96},{96,112},{1,17},{17... | collective-permute-start | bytes 110600 | tf_op jit(solution)/shard_map/ppermute | solution.py:233
  7.8 7.9 %collective-permute-start.3 = (bf16[2,72,64]{2,1,0:T(8,128)(2,1)S(1)}, bf16[2,72,64]{2,1,0:T(8,128)(2,1)S(1)}, u32[]{:S(2)}, u32[]{:S(2)}) collective-permute-start(bf16[2,72,64]{2,1,0:T(8,128)(2,1)S(1)} %get-tuple-element.7), channel_id=1, source_target_pairs={{1,0},{2,1},{3,2},{4,3},{5,4},{6,5},{7,6},{8,7},{9,8},{10,9},{11,1... | collective-permute-start | bytes 55304 | tf_op jit(solution)/shard_map/ppermute | solution.py:233
  14.1 7.6 %collective-permute-start.2 = (bf16[2,72,64]{2,1,0:T(8,128)(2,1)S(1)}, bf16[2,72,64]{2,1,0:T(8,128)(2,1)S(1)}, u32[]{:S(2)}, u32[]{:S(2)}) collective-permute-start(bf16[2,72,64]{2,1,0:T(8,128)(2,1)S(1)} %get-tuple-element.8), channel_id=1, source_target_pairs={{0,1},{1,2},{2,3},{3,4},{4,5},{5,6},{6,7},{7,8},{8,9},{9,10},{10,1... | collective-permute-start | bytes 55304 | tf_op jit(solution)/shard_map/ppermute | solution.py:233
  15.7 6.0 %copy-start.6 = (bf16[2,72,64]{2,1,0:T(8,128)(2,1)}, bf16[2,72,64]{2,1,0:T(8,128)(2,1)S(1)}, u32[]{:S(2)}) copy-start(bf16[2,72,64]{2,1,0:T(8,128)(2,1)S(1)} %collective-permute-done.3.after_ref) | copy-start | bytes 55300
  21.7 0.6 copy-start.7
  21.7 0.6 copy-start.4
  22.4 0.6 copy-start.5
  34.8 16.3 %all-to-all-start.1 = ((bf16[16,72,256]{2,1,0:T(8,128)(2,1)}), bf16[16,72,256]{2,1,0:T(8,128)(2,1)S(1)}, u32[]{:S(2)}, u32[]{:S(2)}) async-start(bf16[16,72,256]{2,1,0:T(8,128)(2,1)} %records_0.1), calls=%async_computation.1 | async-start | bytes 1179648 | tf_op jit(solution)/shard_map/all_to_all | solution.py:301
  51.1 4.1 %copy-start.3 = (bf16[16,72,256]{2,1,0:T(8,128)(2,1)}, bf16[16,72,256]{2,1,0:T(8,128)(2,1)S(1)}, u32[]{:S(2)}) copy-start(bf16[16,72,256]{2,1,0:T(8,128)(2,1)S(1)} %all-to-all-done.1.record_ref) | copy-start | bytes 1769476
  51.1 16.7 %all-to-all-start = ((bf16[16,72,256]{2,1,0:T(8,128)(2,1)}), bf16[16,72,256]{2,1,0:T(8,128)(2,1)S(1)}, u32[]{:S(2)}, u32[]{:S(2)}) async-start(bf16[16,72,256]{2,1,0:T(8,128)(2,1)} %records_1.1), calls=%async_computation | async-start | bytes 1179648 | tf_op jit(solution)/shard_map/all_to_all | solution.py:301
  67.8 0.8 %copy-start.2 = (bf16[16,72,256]{2,1,0:T(8,128)(2,1)}, bf16[16,72,256]{2,1,0:T(8,128)(2,1)S(1)}, u32[]{:S(2)}) copy-start(bf16[16,72,256]{2,1,0:T(8,128)(2,1)S(1)} %all-to-all-done.record_ref) | copy-start | bytes 1769476

commit v6 on v5

--- a/solution.py
+++ b/solution.py
@@ -11,6 +11,7 @@
 GROUP = 8
 REACH = 2
 LOW = 256
+INNER = 4
 TERMS = 11
 BATCH = 8
 OWNERS = (8, 4)
@@ -98,7 +99,6 @@
     weight_ref,
     offset_ref,
     cell_ref,
-    counts_ref,
     out_ref,
     full_ref,
     rim_ref,
@@ -125,11 +125,15 @@
         rim_ref[...] = jnp.concatenate(
             [side[i] for side in (before_ref, after_ref) for i in range(REACH)], axis=1
         )
+        member = lax.broadcasted_iota(jnp.int32, cell_ref.shape, 0)
+        count = jnp.zeros(cell_ref.shape, jnp.int32)
+        for m in range(cell_ref.shape[0]):
+            count = jnp.where(member == m, count_ref[m], count)
         terms = slot_terms(
             weight_ref[...],
             offset_ref[...],
             cell_ref[...],
-            counts_ref[...],
+            count,
             start=start,
             breadth=breadth,
         )
@@ -231,6 +235,25 @@
     up = [(i, (i + 1) % size) for i in range(size if wrap else size - 1)]
     down = [(j, i) for i, j in up]
     return (lax.ppermute(last, axis, up), lax.ppermute(first, axis, down))
+
+
+def ring_neighbours(first, last, axis):
+    size = lax.axis_size(axis)
+    inner = INNER if size % INNER == 0 and size > INNER else 1
+    if inner == 1:
+        return neighbours(first, last, axis, True)
+    up = [(i, i // inner * inner + (i + 1) % inner) for i in range(size)]
+    down = [(j, i) for i, j in up]
+    before = lax.ppermute(last, axis, up)
+    after = lax.ppermute(first, axis, down)
+    head = [(i, (i + inner) % size) for i in range(0, size, inner)]
+    tail = [(i, (i - inner) % size) for i in range(inner - 1, size, inner)]
+    spot = lax.axis_index(axis) % inner
+    turned = lax.ppermute(jnp.where(spot == 0, before, after), axis, head + tail)
+    return (
+        jnp.where(spot == 0, turned, before),
+        jnp.where(spot == inner - 1, turned, after),
+    )
 
 
 def on_device(
@@ -255,7 +278,7 @@
         (((1,), (2,)), ((), ())),
         preferred_element_type=jnp.float32,
     ).astype(jnp.bfloat16)
-    before, after = neighbours(edges[:REACH], edges[REACH:], "blk", True)
+    before, after = ring_neighbours(edges[:REACH], edges[REACH:], "blk")
     half = capacity // 2
     arrived = []
     for part, owners in enumerate(OWNERS):
@@ -275,7 +298,6 @@
                         (2, points, members, half), lambda i, n, part=part: (0, 0, 0, part)
                     ),
                     pl.BlockSpec((members, half), lambda i, n, part=part: (0, part)),
-                    pl.BlockSpec((members, 1), lambda i, n: (0, 0)),
                 ],
                 out_specs=pl.BlockSpec((owners, fields, half), lambda i, n: (i, 0, 0)),
                 scratch_shapes=[
@@ -296,7 +318,6 @@
             gauss_weight,
             gauss_offset,
             source_cell,
-            slot_count.reshape(members, 1),
         )
         arrived.append(lax.all_to_all(records, "blk", split_axis=0, concat_axis=0, tiled=True))
     highs = cells // LOW

time: 74.7 us -> 74.6 us (level)
  the two profiles are of different devices: /device:TPU:8 before, /device:TPU:0 now
where the time goes in v6:
time: 74.6 us; the launch traced here: 74.1 us
  Pallas kernels  32.2 us (43%)
  starting transfers between devices  19.8 us (27%)
  waiting for transfers between devices  16.5 us (22%)
  matrix products  2.36 us (3%)
  local copies, waits for them, and re-layouts  2.34 us (3%)
    pallas_call x2, Pallas kernels, on_device(): pl.pallas_call(functools.partial(record_body, start=part * half), grid_sp...  20.9 us
    all_to_all x2, waiting for transfers between devices, on_device(): lax.all_to_all(records, 'blk', split_axis=0, concat_axis=0, tiled=True)  12 us
    all_to_all x2, starting transfers between devices, on_device(): lax.all_to_all(records, 'blk', split_axis=0, concat_axis=0, tiled=True)  8.74 us
    pallas_call x1, Pallas kernels, on_device(): pl.pallas_call(functools.partial(deposit_last_body, highs=highs, padded=p...  5.77 us
    pallas_call x1, Pallas kernels, on_device(): pl.pallas_call(functools.partial(deposit_first_body, highs=highs, padded=...  5.53 us
    ppermute x2, starting transfers between devices, neighbours(): return (lax.ppermute(last, axis, up), lax.ppermute(first, axis, down))  4.32 us
    ppermute x1, starting transfers between devices, ring_neighbours(): lax.ppermute(jnp.where(spot == 0, before, after), axis, head + tail)  3.83 us
    ppermute x1, waiting for transfers between devices, ring_neighbours(): before = lax.ppermute(last, axis, up)  3.53 us
  transfers between devices with their start and end apart: 7, of which 5 were waited for; matrix products, arithmetic and copies ran while one was open for 2% of the time, Pallas kernels for 20%

profile of v6, /device:TPU:0, one launch (start us, length us, event | category | flops | bytes accessed | tf_op | source)
XLA Modules:
  0.0 74.1 jit_solution(4823527150922085663)
XLA Ops:
  0.0 0.0 copy-start.1
  0.0 2.4 %fusion = bf16[4,72,64]{1,0,2:T(4,128)(2,1)S(1)} fusion(bf16[4,128,1]{1,0,2:T(4,128)(2,1)} %constant.27, bf16[72,64,128]{2,1,0:T(8,128)(2,1)} %param.8), kind=kOutput, calls=%fused_computation | convolution fusion | flops 4718592 | bytes 1217536 | tf_op jit(solution)/shard_map/dot_general | solution.py:275
  2.4 0.1 copy.11
  2.5 2.9 %collective-permute-start.3 = (bf16[2,72,64]{2,1,0:T(8,128)(2,1)S(1)}, bf16[2,72,64]{2,1,0:T(8,128)(2,1)S(1)}, u32[]{:S(2)}, u32[]{:S(2)}) collective-permute-start(bf16[2,72,64]{2,1,0:T(8,128)(2,1)S(1)} %get-tuple-element.7), channel_id=1, source_target_pairs={{1,0},{2,1},{3,2},{0,3},{5,4},{6,5},{7,6},{4,7},{9,8},{10,9},{11,1... | collective-permute-start | bytes 55304 | tf_op jit(solution)/shard_map/ppermute | solution.py:248
  5.4 0.0 collective-permute-start.2
  5.4 0.0 copy-done.1
  5.4 0.8 %copy.15 = bf16[72,64,128]{2,0,1:T(8,128)(2,1)S(1)} copy(bf16[72,64,128]{2,1,0:T(8,128)(2,1)S(1)} %copy-done.1) | data formatting | bytes 2359296 | tf_op args[0]
  6.2 0.0 copy-start
  6.2 0.8 %collective-permute-done.3 = bf16[2,72,64]{2,1,0:T(8,128)(2,1)S(1)} collective-permute-done((bf16[2,72,64]{2,1,0:T(8,128)(2,1)S(1)}, bf16[2,72,64]{2,1,0:T(8,128)(2,1)S(1)}, u32[]{:S(2)}, u32[]{:S(2)}) %collective-permute-start.3) | collective-permute-done | bytes 18464 | tf_op jit(solution)/shard_map/ppermute | solution.py:248
  7.1 3.5 %collective-permute-done.2 = bf16[2,72,64]{2,1,0:T(8,128)(2,1)S(1)} collective-permute-done((bf16[2,72,64]{2,1,0:T(8,128)(2,1)S(1)}, bf16[2,72,64]{2,1,0:T(8,128)(2,1)S(1)}, u32[]{:S(2)}, u32[]{:S(2)}) %collective-permute-start.2) | collective-permute-done | bytes 18464 | tf_op jit(solution)/shard_map/ppermute | solution.py:247
  10.6 3.8 %collective-permute-start.4 = (bf16[2,72,64]{2,1,0:T(8,128)(2,1)S(1)}, bf16[2,72,64]{2,1,0:T(8,128)(2,1)S(1)}, u32[]{:S(2)}, u32[]{:S(2)}) collective-permute-start(bf16[2,72,64]{2,1,0:T(8,128)(2,1)S(1)} %broadcast_select_fusion.2), channel_id=1, source_target_pairs={{0,4},{4,8},{8,12},{12,0},{3,15},{7,3},{11,7},{15,11},{16,20},{20,... | collective-permute-start | bytes 55304 | tf_op jit(solution)/shard_map/ppermute | solution.py:252
  14.4 1.3 %collective-permute-start.1 = (bf16[2,72,128]{2,1,0:T(8,128)(2,1)S(1)}, bf16[2,72,128]{2,1,0:T(8,128)(2,1)S(1)}, u32[]{:S(2)}, u32[]{:S(2)}) collective-permute-start(bf16[2,72,128]{2,1,0:T(8,128)(2,1)S(1)} %get-tuple-element.5), channel_id=1, source_target_pairs={{16,0},{32,16},{48,32},{64,48},{80,64},{96,80},{112,96},{17,1},{33... | collective-permute-start | bytes 110600 | tf_op jit(solution)/shard_map/ppermute | solution.py:237
  15.7 3.0 %collective-permute-start = (bf16[2,72,128]{2,1,0:T(8,128)(2,1)S(1)}, bf16[2,72,128]{2,1,0:T(8,128)(2,1)S(1)}, u32[]{:S(2)}, u32[]{:S(2)}) collective-permute-start(bf16[2,72,128]{2,1,0:T(8,128)(2,1)S(1)} %get-tuple-element.6), channel_id=1, source_target_pairs={{0,16},{16,32},{32,48},{48,64},{64,80},{80,96},{96,112},{1,17},{17... | collective-permute-start | bytes 110600 | tf_op jit(solution)/shard_map/ppermute | solution.py:237
  18.8 0.0 collective-permute-done.4
  18.8 0.6 broadcast_select_fusion
  19.4 0.0 collective-permute-done.1.below_ref
  19.5 0.0 copy-start.4
  19.5 0.2 collective-permute-done.above_ref
  19.6 0.0 copy-start.5
  19.6 0.0 copy-done
  19.6 0.4 copy-done.4
  20.1 0.2 copy-done.5
  20.2 11.8 %records_0.1 = bf16[16,72,256]{2,1,0:T(8,128)(2,1)} custom-call(s32[16]{0:T(128)} %count_ref.3, bf16[64,72,128]{2,1,0:T(8,128)(2,1)} %bitcast.7, bf16[2,72,128]{2,1,0:T(8,128)(2,1)} %copy-done.5, bf16[2,72,128]{2,1,0:T(8,128)(2,1)} %copy-done.4, bf16[2,72,64]{2,1,0:T(8,128)(2,1)} %get-tuple-element.10.before_ref, ...), custom_call_target="tpu_custom_call" | custom-call | tf_op jit(solution)/shard_map/records_0/pallas_call | solution.py:285
  32.1 5.0 %all-to-all-start.1 = ((bf16[16,72,256]{2,1,0:T(8,128)(2,1)}), bf16[16,72,256]{2,1,0:T(8,128)(2,1)S(1)}, u32[]{:S(2)}, u32[]{:S(2)}) async-start(bf16[16,72,256]{2,1,0:T(8,128)(2,1)} %records_0.1), calls=%async_computation.1 | async-start | bytes 1179648 | tf_op jit(solution)/shard_map/all_to_all | solution.py:322
  37.1 9.1 %records_1.1 = bf16[16,72,256]{2,1,0:T(8,128)(2,1)} custom-call(s32[16]{0:T(128)} %count_ref.3, bf16[64,72,128]{2,1,0:T(8,128)(2,1)} %bitcast.8, bf16[2,72,128]{2,1,0:T(8,128)(2,1)} %copy-done.5, bf16[2,72,128]{2,1,0:T(8,128)(2,1)} %copy-done.4, bf16[2,72,64]{2,1,0:T(8,128)(2,1)} %get-tuple-element.10.before_ref, ...), custom_call_target="tpu_custom_call" | custom-call | tf_op jit(solution)/shard_map/records_1/pallas_call | solution.py:285
  46.2 4.8 %all-to-all-done.1.record_ref = bf16[16,72,256]{2,1,0:T(8,128)(2,1)S(1)} async-done(((bf16[16,72,256]{2,1,0:T(8,128)(2,1)}), bf16[16,72,256]{2,1,0:T(8,128)(2,1)S(1)}, u32[]{:S(2)}, u32[]{:S(2)}) %all-to-all-start.1) | async-done | bytes 589856 | tf_op jit(solution)/shard_map/all_to_all | solution.py:322
  51.0 0.0 copy-start.3
  51.0 3.8 %all-to-all-start = ((bf16[16,72,256]{2,1,0:T(8,128)(2,1)}), bf16[16,72,256]{2,1,0:T(8,128)(2,1)S(1)}, u32[]{:S(2)}, u32[]{:S(2)}) async-start(bf16[16,72,256]{2,1,0:T(8,128)(2,1)} %records_1.1), calls=%async_computation | async-start | bytes 1179648 | tf_op jit(solution)/shard_map/all_to_all | solution.py:322
  54.8 0.0 copy-done.3
  54.8 5.5 %deposit_0.1.before_ref = f32[1280,256]{1,0:T(8,128)} custom-call(bf16[16,72,256]{2,1,0:T(8,128)(2,1)} %copy-done.3, s32[16,512]{1,0:T(8,128)} %target_ref.3), custom_call_target="tpu_custom_call" | custom-call | tf_op jit(solution)/shard_map/deposit_0/pallas_call | solution.py:328
  60.3 7.1 %all-to-all-done.record_ref = bf16[16,72,256]{2,1,0:T(8,128)(2,1)S(1)} async-done(((bf16[16,72,256]{2,1,0:T(8,128)(2,1)}), bf16[16,72,256]{2,1,0:T(8,128)(2,1)S(1)}, u32[]{:S(2)}, u32[]{:S(2)}) %all-to-all-start) | async-done | bytes 589856 | tf_op jit(solution)/shard_map/all_to_all | solution.py:322
  67.5 0.0 copy-start.2
  67.5 0.8 %copy-done.2 = bf16[16,72,256]{2,1,0:T(8,128)(2,1)} copy-done((bf16[16,72,256]{2,1,0:T(8,128)(2,1)}, bf16[16,72,256]{2,1,0:T(8,128)(2,1)S(1)}, u32[]{:S(2)}) %copy-start.2) | copy-done | bytes 589848
  68.3 5.8 %deposit_1.1 = bf16[72,4096]{1,0:T(8,128)(2,1)} custom-call(bf16[16,72,256]{2,1,0:T(8,128)(2,1)} %copy-done.2, s32[16,512]{1,0:T(8,128)} %target_ref.3, f32[1280,256]{1,0:T(8,128)} %deposit_0.1.before_ref, f32[1,4096]{1,0:T(1,128)} %bitcast.9), custom_call_target="tpu_custom_call" | custom-call | tf_op jit(solution)/shard_map/deposit_1/pallas_call | solution.py:336
  (3 shorter events, 0.0 us)
Async XLA Ops:
  0.0 5.4 %copy-start.1 = (bf16[72,64,128]{2,1,0:T(8,128)(2,1)S(1)}, bf16[72,64,128]{2,1,0:T(8,128)(2,1)}, u32[]{:S(2)}) copy-start(bf16[72,64,128]{2,1,0:T(8,128)(2,1)} %param.8) | copy-start | bytes 3538948
  2.5 4.5 %collective-permute-start.3 = (bf16[2,72,64]{2,1,0:T(8,128)(2,1)S(1)}, bf16[2,72,64]{2,1,0:T(8,128)(2,1)S(1)}, u32[]{:S(2)}, u32[]{:S(2)}) collective-permute-start(bf16[2,72,64]{2,1,0:T(8,128)(2,1)S(1)} %get-tuple-element.7), channel_id=1, source_target_pairs={{1,0},{2,1},{3,2},{0,3},{5,4},{6,5},{7,6},{4,7},{9,8},{10,9},{11,1... | collective-permute-start | bytes 55304 | tf_op jit(solution)/shard_map/ppermute | solution.py:248
  5.4 5.2 %collective-permute-start.2 = (bf16[2,72,64]{2,1,0:T(8,128)(2,1)S(1)}, bf16[2,72,64]{2,1,0:T(8,128)(2,1)S(1)}, u32[]{:S(2)}, u32[]{:S(2)}) collective-permute-start(bf16[2,72,64]{2,1,0:T(8,128)(2,1)S(1)} %get-tuple-element.8), channel_id=1, source_target_pairs={{0,1},{1,2},{2,3},{3,0},{4,5},{5,6},{6,7},{7,4},{8,9},{9,10},{10,1... | collective-permute-start | bytes 55304 | tf_op jit(solution)/shard_map/ppermute | solution.py:247
  6.2 13.4 %copy-start = (bf16[72,64,128]{2,0,1:T(8,128)(2,1)}, bf16[72,64,128]{2,0,1:T(8,128)(2,1)S(1)}, u32[]{:S(2)}) copy-start(bf16[72,64,128]{2,0,1:T(8,128)(2,1)S(1)} %copy.15) | copy-start | bytes 3538948
  10.6 8.2 %collective-permute-start.4 = (bf16[2,72,64]{2,1,0:T(8,128)(2,1)S(1)}, bf16[2,72,64]{2,1,0:T(8,128)(2,1)S(1)}, u32[]{:S(2)}, u32[]{:S(2)}) collective-permute-start(bf16[2,72,64]{2,1,0:T(8,128)(2,1)S(1)} %broadcast_select_fusion.2), channel_id=1, source_target_pairs={{0,4},{4,8},{8,12},{12,0},{3,15},{7,3},{11,7},{15,11},{16,20},{20,... | collective-permute-start | bytes 55304 | tf_op jit(solution)/shard_map/ppermute | solution.py:252
  14.4 5.0 %collective-permute-start.1 = (bf16[2,72,128]{2,1,0:T(8,128)(2,1)S(1)}, bf16[2,72,128]{2,1,0:T(8,128)(2,1)S(1)}, u32[]{:S(2)}, u32[]{:S(2)}) collective-permute-start(bf16[2,72,128]{2,1,0:T(8,128)(2,1)S(1)} %get-tuple-element.5), channel_id=1, source_target_pairs={{16,0},{32,16},{48,32},{64,48},{80,64},{96,80},{112,96},{17,1},{33... | collective-permute-start | bytes 110600 | tf_op jit(solution)/shard_map/ppermute | solution.py:237
  15.7 3.9 %collective-permute-start = (bf16[2,72,128]{2,1,0:T(8,128)(2,1)S(1)}, bf16[2,72,128]{2,1,0:T(8,128)(2,1)S(1)}, u32[]{:S(2)}, u32[]{:S(2)}) collective-permute-start(bf16[2,72,128]{2,1,0:T(8,128)(2,1)S(1)} %get-tuple-element.6), channel_id=1, source_target_pairs={{0,16},{16,32},{32,48},{48,64},{64,80},{80,96},{96,112},{1,17},{17... | collective-permute-start | bytes 110600 | tf_op jit(solution)/shard_map/ppermute | solution.py:237
  19.5 0.6 copy-start.4
  19.6 0.6 copy-start.5
  32.1 18.9 %all-to-all-start.1 = ((bf16[16,72,256]{2,1,0:T(8,128)(2,1)}), bf16[16,72,256]{2,1,0:T(8,128)(2,1)S(1)}, u32[]{:S(2)}, u32[]{:S(2)}) async-start(bf16[16,72,256]{2,1,0:T(8,128)(2,1)} %records_0.1), calls=%async_computation.1 | async-start | bytes 1179648 | tf_op jit(solution)/shard_map/all_to_all | solution.py:322
  51.0 3.8 %copy-start.3 = (bf16[16,72,256]{2,1,0:T(8,128)(2,1)}, bf16[16,72,256]{2,1,0:T(8,128)(2,1)S(1)}, u32[]{:S(2)}) copy-start(bf16[16,72,256]{2,1,0:T(8,128)(2,1)S(1)} %all-to-all-done.1.record_ref) | copy-start | bytes 1769476
  51.0 16.5 %all-to-all-start = ((bf16[16,72,256]{2,1,0:T(8,128)(2,1)}), bf16[16,72,256]{2,1,0:T(8,128)(2,1)S(1)}, u32[]{:S(2)}, u32[]{:S(2)}) async-start(bf16[16,72,256]{2,1,0:T(8,128)(2,1)} %records_1.1), calls=%async_computation | async-start | bytes 1179648 | tf_op jit(solution)/shard_map/all_to_all | solution.py:322
  67.5 0.8 %copy-start.2 = (bf16[16,72,256]{2,1,0:T(8,128)(2,1)}, bf16[16,72,256]{2,1,0:T(8,128)(2,1)S(1)}, u32[]{:S(2)}) copy-start(bf16[16,72,256]{2,1,0:T(8,128)(2,1)S(1)} %all-to-all-done.record_ref) | copy-start | bytes 1769476

commit v7 on v5

--- a/solution.py
+++ b/solution.py
@@ -13,19 +13,13 @@
 LOW = 256
 TERMS = 11
 BATCH = 8
-OWNERS = (8, 4)
-
-
-def slot_records(terms, window_ref, rim, *, fields, height, breadth):
-    groups = height // GROUP
+SHIFTS = (-2, -1, 1, 2)
+
+
+def window_sum(terms, window_ref, *, fields, breadth):
     span = GROUP + 2 * REACH
     slots = terms[0].shape[1]
-    scale = terms[0]
-    row_taps = terms[1:5]
-    col_taps = terms[5:9]
     row = terms[9].astype(jnp.int32)
-    col = terms[10].astype(jnp.int32)
-    shifts = (-2, -1, 1, 2)
     group = row // GROUP
     local = row - group * GROUP + REACH
     one = jnp.ones((), jnp.bfloat16)
@@ -34,12 +28,12 @@
     gap = place.astype(jnp.bfloat16) - terms[10].astype(jnp.bfloat16)
     here = jnp.where(gap == 0, one, zero)
     beside = jnp.zeros((breadth, slots), jnp.bfloat16)
-    for shift, tap in zip(shifts, col_taps):
+    for shift, tap in zip(SHIFTS, terms[5:9]):
         beside = jnp.where(gap == shift, tap.astype(jnp.bfloat16), beside)
     away = lax.broadcasted_iota(jnp.int32, (2 * GROUP, slots), 0) - local
     centres = jnp.where(away == 0, 1.0, 0.0)
     weights = centres
-    for shift, tap in zip(shifts, row_taps):
+    for shift, tap in zip(SHIFTS, terms[1:5]):
         weights = jnp.where(away == shift, tap, weights)
     pieces = []
     for j in range(span):
@@ -48,19 +42,28 @@
         pieces.append(here * weight + beside * centre)
     table = jnp.concatenate(pieces, axis=0)
     product = jnp.dot(window_ref[...], table, preferred_element_type=jnp.float32)
+    total = jnp.where(group == 0, product[:fields], 0.0)
+    for g in range(1, product.shape[0] // fields):
+        total = total + jnp.where(group == g, product[g * fields : (g + 1) * fields], 0.0)
+    return total
+
+
+def rim_sum(terms, rim, *, height, breadth):
+    slots = terms[0].shape[1]
+    col = terms[10].astype(jnp.int32)
+    place = lax.broadcasted_iota(jnp.int32, (height, slots), 0).astype(jnp.float32)
     same_row = jnp.where(
-        place[:height].astype(jnp.bfloat16) == terms[9].astype(jnp.bfloat16), one, zero
+        place.astype(jnp.bfloat16) == terms[9].astype(jnp.bfloat16),
+        jnp.ones((), jnp.bfloat16),
+        jnp.zeros((), jnp.bfloat16),
     )
     side = lax.broadcasted_iota(jnp.int32, (GROUP, slots), 0)
     reach = jnp.where(side < REACH, side - REACH, side + (breadth - REACH)) - col
     outer = jnp.zeros((GROUP, slots), jnp.float32)
-    for shift, tap in zip(shifts, col_taps):
+    for shift, tap in zip(SHIFTS, terms[5:9]):
         outer = jnp.where(reach == shift, tap, outer)
-    rim_pieces = [same_row * outer[i : i + 1].astype(jnp.bfloat16) for i in range(2 * REACH)]
-    total = jnp.dot(rim, jnp.concatenate(rim_pieces, axis=0), preferred_element_type=jnp.float32)
-    for g in range(groups):
-        total = total + jnp.where(group == g, product[g * fields : (g + 1) * fields], 0.0)
-    return (total * scale).astype(jnp.bfloat16)
+    pieces = [same_row * outer[i : i + 1].astype(jnp.bfloat16) for i in range(2 * REACH)]
+    return jnp.dot(rim, jnp.concatenate(pieces, axis=0), preferred_element_type=jnp.float32)
 
 
 def slot_terms(weight, offset, cell, count, *, start, breadth):
@@ -88,6 +91,107 @@
     return terms + [row.astype(jnp.float32), col.astype(jnp.float32)]
 
 
+def fill_window(rows_ref, above_ref, below_ref, full_ref):
+    height, fields, breadth = rows_ref.shape
+    for g in range(height // GROUP):
+        for j in range(GROUP + 2 * REACH):
+            r = g * GROUP + j - REACH
+            if r < 0:
+                part = above_ref[r + REACH]
+            elif r >= height:
+                part = below_ref[r - height]
+            else:
+                part = rows_ref[r]
+            full_ref[g * fields : (g + 1) * fields, j * breadth : (j + 1) * breadth] = part
+
+
+def fill_rim(before_ref, after_ref, rim_ref):
+    rim_ref[...] = jnp.concatenate(
+        [side[i] for side in (before_ref, after_ref) for i in range(REACH)], axis=1
+    )
+
+
+def fill_terms(count_ref, weight_ref, offset_ref, cell_ref, term_ref, *, start, breadth):
+    member = lax.broadcasted_iota(jnp.int32, cell_ref.shape, 0)
+    count = jnp.zeros(cell_ref.shape, jnp.int32)
+    for m in range(cell_ref.shape[0]):
+        count = jnp.where(member == m, count_ref[m], count)
+    terms = slot_terms(
+        weight_ref[...], offset_ref[...], cell_ref[...], count, start=start, breadth=breadth
+    )
+    for k, term in enumerate(terms):
+        term_ref[k] = term
+
+
+def row_terms(term_ref, first, batch):
+    return [
+        jnp.concatenate([term_ref[k, pl.ds(first + b, 1), :] for b in range(batch)], axis=1)
+        for k in range(TERMS)
+    ]
+
+
+def inner_body(
+    count_ref,
+    rows_ref,
+    above_ref,
+    below_ref,
+    weight_ref,
+    offset_ref,
+    cell_ref,
+    out_ref,
+    full_ref,
+    term_ref,
+):
+    step = pl.program_id(0)
+    _, fields, breadth = rows_ref.shape
+    batch, _, slots = out_ref.shape
+
+    @pl.when(step == 0)
+    def fill():
+        fill_window(rows_ref, above_ref, below_ref, full_ref)
+        fill_terms(
+            count_ref, weight_ref, offset_ref, cell_ref, term_ref, start=0, breadth=breadth
+        )
+
+    made = window_sum(
+        row_terms(term_ref, step * batch, batch), full_ref, fields=fields, breadth=breadth
+    )
+    for b in range(batch):
+        out_ref[b] = made[:, b * slots : (b + 1) * slots]
+
+
+def outer_body(
+    count_ref,
+    inner_ref,
+    before_ref,
+    after_ref,
+    weight_ref,
+    offset_ref,
+    cell_ref,
+    out_ref,
+    rim_ref,
+    term_ref,
+    *,
+    height,
+    breadth,
+):
+    step = pl.program_id(0)
+    batch, _, slots = out_ref.shape
+
+    @pl.when(step == 0)
+    def fill():
+        fill_rim(before_ref, after_ref, rim_ref)
+        fill_terms(
+            count_ref, weight_ref, offset_ref, cell_ref, term_ref, start=0, breadth=breadth
+        )
+
+    terms = row_terms(term_ref, step * batch, batch)
+    made = rim_sum(terms, rim_ref[...], height=height, breadth=breadth)
+    for b in range(batch):
+        cut = slice(b * slots, (b + 1) * slots)
+        out_ref[b] = ((inner_ref[b] + made[:, cut]) * terms[0][:, cut]).astype(jnp.bfloat16)
+
+
 def record_body(
     count_ref,
     rows_ref,
@@ -98,7 +202,6 @@
     weight_ref,
     offset_ref,
     cell_ref,
-    counts_ref,
     out_ref,
     full_ref,
     rim_ref,
@@ -112,51 +215,25 @@
 
     @pl.when(step == 0)
     def fill():
-        for g in range(height // GROUP):
-            for j in range(GROUP + 2 * REACH):
-                r = g * GROUP + j - REACH
-                if r < 0:
-                    part = above_ref[r + REACH]
-                elif r >= height:
-                    part = below_ref[r - height]
-                else:
-                    part = rows_ref[r]
-                full_ref[g * fields : (g + 1) * fields, j * breadth : (j + 1) * breadth] = part
-        rim_ref[...] = jnp.concatenate(
-            [side[i] for side in (before_ref, after_ref) for i in range(REACH)], axis=1
+        fill_window(rows_ref, above_ref, below_ref, full_ref)
+        fill_rim(before_ref, after_ref, rim_ref)
+        fill_terms(
+            count_ref, weight_ref, offset_ref, cell_ref, term_ref, start=start, breadth=breadth
         )
-        terms = slot_terms(
-            weight_ref[...],
-            offset_ref[...],
-            cell_ref[...],
-            counts_ref[...],
-            start=start,
-            breadth=breadth,
-        )
-        for k, term in enumerate(terms):
-            term_ref[k] = term
-
-    rim = rim_ref[...]
-    make = functools.partial(slot_records, fields=fields, height=height, breadth=breadth)
-    take = lambda k, b: term_ref[k, pl.ds(step * batch + b, 1), :]
-    if start == 0:
-        terms = [
-            jnp.concatenate([take(k, b) for b in range(batch)], axis=1) for k in range(TERMS)
-        ]
-        made = make(terms, full_ref, rim)
-        for b in range(batch):
-            out_ref[b] = made[:, b * slots : (b + 1) * slots]
-    else:
-        for b in range(batch):
-            alive = count_ref[step * batch + b] > start
-
-            @pl.when(alive)
-            def compute():
-                out_ref[b] = make([take(k, b) for k in range(TERMS)], full_ref, rim)
-
-            @pl.when(jnp.logical_not(alive))
-            def clear():
-                out_ref[b] = jnp.zeros((fields, slots), out_ref.dtype)
+
+    for b in range(batch):
+        alive = count_ref[step * batch + b] > start
+
+        @pl.when(alive)
+        def compute():
+            terms = row_terms(term_ref, step * batch + b, 1)
+            total = window_sum(terms, full_ref, fields=fields, breadth=breadth)
+            total = total + rim_sum(terms, rim_ref[...], height=height, breadth=breadth)
+            out_ref[b] = (total * terms[0]).astype(jnp.bfloat16)
+
+        @pl.when(jnp.logical_not(alive))
+        def clear():
+            out_ref[b] = jnp.zeros((fields, slots), out_ref.dtype)
 
 
 def deposit_part(record_ref, target_ref, *, highs, padded, start):
@@ -257,48 +334,60 @@
     ).astype(jnp.bfloat16)
     before, after = neighbours(edges[:REACH], edges[REACH:], "blk", True)
     half = capacity // 2
-    arrived = []
-    for part, owners in enumerate(OWNERS):
-        records = pl.pallas_call(
-            functools.partial(record_body, start=part * half),
+    whole = lambda *shape: pl.BlockSpec(shape, lambda i, n: (0,) * len(shape))
+    strip = lambda owners: pl.BlockSpec((owners, fields, half), lambda i, n: (i, 0, 0))
+    row_specs = [whole(height, fields, breadth)] + [whole(REACH, fields, breadth)] * 2
+    rim_specs = [whole(REACH, fields, height)] * 2
+
+    def slot_specs(part):
+        return [
+            pl.BlockSpec((points, members, half), lambda i, n: (0, 0, part)),
+            pl.BlockSpec((2, points, members, half), lambda i, n: (0, 0, 0, part)),
+            pl.BlockSpec((members, half), lambda i, n: (0, part)),
+        ]
+
+    full = pltpu.VMEM((groups * fields, span * breadth), jnp.bfloat16)
+    rim = pltpu.VMEM((fields, 2 * REACH * height), jnp.bfloat16)
+    held = pltpu.VMEM((TERMS, members, half), jnp.float32)
+
+    def call(body, owners, specs, scratch, dtype, name):
+        return pl.pallas_call(
+            body,
             grid_spec=pltpu.PrefetchScalarGridSpec(
                 num_scalar_prefetch=1,
                 grid=(members // owners,),
-                in_specs=[
-                    pl.BlockSpec((height, fields, breadth), lambda i, n: (0, 0, 0)),
-                    pl.BlockSpec((REACH, fields, breadth), lambda i, n: (0, 0, 0)),
-                    pl.BlockSpec((REACH, fields, breadth), lambda i, n: (0, 0, 0)),
-                    pl.BlockSpec((REACH, fields, height), lambda i, n: (0, 0, 0)),
-                    pl.BlockSpec((REACH, fields, height), lambda i, n: (0, 0, 0)),
-                    pl.BlockSpec((points, members, half), lambda i, n, part=part: (0, 0, part)),
-                    pl.BlockSpec(
-                        (2, points, members, half), lambda i, n, part=part: (0, 0, 0, part)
-                    ),
-                    pl.BlockSpec((members, half), lambda i, n, part=part: (0, part)),
-                    pl.BlockSpec((members, 1), lambda i, n: (0, 0)),
-                ],
-                out_specs=pl.BlockSpec((owners, fields, half), lambda i, n: (i, 0, 0)),
-                scratch_shapes=[
-                    pltpu.VMEM((groups * fields, span * breadth), jnp.bfloat16),
-                    pltpu.VMEM((fields, 2 * REACH * height), jnp.bfloat16),
-                    pltpu.VMEM((TERMS, members, half), jnp.float32),
-                ],
+                in_specs=specs,
+                out_specs=strip(owners),
+                scratch_shapes=scratch,
             ),
-            out_shape=jax.ShapeDtypeStruct((members, fields, half), jnp.bfloat16),
-            name=f"records_{part}",
-        )(
-            slot_count,
-            rows,
-            above,
-            below,
-            before,
-            after,
-            gauss_weight,
-            gauss_offset,
-            source_cell,
-            slot_count.reshape(members, 1),
+            out_shape=jax.ShapeDtypeStruct((members, fields, half), dtype),
+            name=name,
         )
-        arrived.append(lax.all_to_all(records, "blk", split_axis=0, concat_axis=0, tiled=True))
+
+    slot_inputs = (gauss_weight, gauss_offset, source_cell)
+    inner = call(
+        inner_body, 8, row_specs + slot_specs(0), [full, held], jnp.float32, "records_inner"
+    )(slot_count, rows, above, below, *slot_inputs)
+    early = call(
+        functools.partial(outer_body, height=height, breadth=breadth),
+        4,
+        [strip(4)] + rim_specs + slot_specs(0),
+        [rim, held],
+        jnp.bfloat16,
+        "records_outer",
+    )(slot_count, inner, before, after, *slot_inputs)
+    late = call(
+        functools.partial(record_body, start=half),
+        4,
+        row_specs + rim_specs + slot_specs(1),
+        [full, rim, held],
+        jnp.bfloat16,
+        "records_late",
+    )(slot_count, rows, above, below, before, after, *slot_inputs)
+    arrived = [
+        lax.all_to_all(part, "blk", split_axis=0, concat_axis=0, tiled=True)
+        for part in (early, late)
+    ]
     highs = cells // LOW
     padded = -(-fields // 16) * 16
     record_spec = pl.BlockSpec(memory_space=pltpu.VMEM)

time: 74.7 us -> 76.3 us (1.021)
  the two profiles are of different devices: /device:TPU:8 before, /device:TPU:0 now
where the time goes in v7:
time: 76.3 us; the launch traced here: 75 us
  Pallas kernels  34.6 us (45%)
  starting transfers between devices  21.2 us (28%)
  waiting for transfers between devices  12.6 us (17%)
  local copies, waits for them, and re-layouts  5.51 us (7%)
  matrix products  0.97 us (1%)
    all_to_all x2, waiting for transfers between devices, on_device(): lax.all_to_all(part, 'blk', split_axis=0, concat_axis=0, tiled=True)  12.6 us
    pallas_call x1, Pallas kernels, on_device(): call(inner_body, 8, row_specs + slot_specs(0), [full, held], jnp.float32,...  11 us
    ppermute x4, starting transfers between devices, neighbours(): return (lax.ppermute(last, axis, up), lax.ppermute(first, axis, down))  10.7 us
    all_to_all x2, starting transfers between devices, on_device(): lax.all_to_all(part, 'blk', split_axis=0, concat_axis=0, tiled=True)  10.5 us
    pallas_call x1, Pallas kernels, on_device(): call(functools.partial(record_body, start=half), 4, row_specs + rim_specs...  7.66 us
    pallas_call x1, Pallas kernels, on_device(): pl.pallas_call(functools.partial(deposit_last_body, highs=highs, padded=p...  5.77 us
    pallas_call x1, Pallas kernels, on_device(): pl.pallas_call(functools.partial(deposit_first_body, highs=highs, padded=...  5.55 us
    unnamed x19, local copies, waits for them, and re-layouts  5.37 us
  transfers between devices with their start and end apart: 6, of which 2 were waited for; matrix products, arithmetic and copies ran while one was open for 1% of the time, Pallas kernels for 32%

profile of v7, /device:TPU:0, one launch (start us, length us, event | category | flops | bytes accessed | tf_op | source)
XLA Modules:
  0.0 75.0 jit_solution(11541101869592549823)
XLA Ops:
  0.0 0.0 copy-start.8
  0.0 0.0 copy-start.1
  0.0 2.1 %copy.15 = bf16[72,64,128]{2,0,1:T(8,128)(2,1)S(1)} copy(bf16[72,64,128]{2,1,0:T(8,128)(2,1)} %param.8) | data formatting | bytes 2359296 | tf_op args[0]
  2.1 0.0 copy-start
  2.2 1.3 %collective-permute-start.1 = (bf16[2,72,128]{2,1,0:T(8,128)(2,1)S(1)}, bf16[2,72,128]{2,1,0:T(8,128)(2,1)S(1)}, u32[]{:S(2)}, u32[]{:S(2)}) collective-permute-start(bf16[2,72,128]{2,1,0:T(8,128)(2,1)S(1)} %get-tuple-element.5), channel_id=1, source_target_pairs={{16,0},{32,16},{48,32},{64,48},{80,64},{96,80},{112,96},{17,1},{33... | collective-permute-start | bytes 110600 | tf_op jit(solution)/shard_map/ppermute | solution.py:310
  3.5 3.0 %collective-permute-start = (bf16[2,72,128]{2,1,0:T(8,128)(2,1)S(1)}, bf16[2,72,128]{2,1,0:T(8,128)(2,1)S(1)}, u32[]{:S(2)}, u32[]{:S(2)}) collective-permute-start(bf16[2,72,128]{2,1,0:T(8,128)(2,1)S(1)} %get-tuple-element.6), channel_id=1, source_target_pairs={{0,16},{16,32},{32,48},{48,64},{64,80},{80,96},{96,112},{1,17},{17... | collective-permute-start | bytes 110600 | tf_op jit(solution)/shard_map/ppermute | solution.py:310
  6.5 0.0 copy-done.8
  6.5 0.0 copy-done.1
  6.5 1.0 %fusion = bf16[4,72,64]{1,0,2:T(4,128)(2,1)S(1)} fusion(bf16[4,128,1]{1,0,2:T(4,128)(2,1)S(1)} %copy-done.8, bf16[72,64,128]{2,1,0:T(8,128)(2,1)S(1)} %copy-done.1), kind=kOutput, calls=%fused_computation | convolution fusion | flops 4718592 | bytes 1217536 | tf_op jit(solution)/shard_map/dot_general | solution.py:329
  7.5 0.1 copy.11
  7.6 6.4 %collective-permute-start.3 = (bf16[2,72,64]{2,1,0:T(8,128)(2,1)S(1)}, bf16[2,72,64]{2,1,0:T(8,128)(2,1)S(1)}, u32[]{:S(2)}, u32[]{:S(2)}) collective-permute-start(bf16[2,72,64]{2,1,0:T(8,128)(2,1)S(1)} %get-tuple-element.7), channel_id=1, source_target_pairs={{1,0},{2,1},{3,2},{4,3},{5,4},{6,5},{7,6},{8,7},{9,8},{10,9},{11,1... | collective-permute-start | bytes 55304 | tf_op jit(solution)/shard_map/ppermute | solution.py:310
  14.0 0.0 collective-permute-start.2
  14.0 0.0 collective-permute-done.1.below_ref
  14.0 0.0 copy-start.4
  14.0 0.0 collective-permute-done.above_ref
  14.1 0.0 copy-done
  14.1 0.6 copy-done.4
  14.6 0.0 copy-start.5
  14.6 0.6 copy-done.5
  15.2 11.0 %records_inner.1.inner_ref = f32[16,72,256]{2,1,0:T(8,128)} custom-call(s32[16]{0:T(128)} %count_ref.5, bf16[64,72,128]{2,1,0:T(8,128)(2,1)} %bitcast.7, bf16[2,72,128]{2,1,0:T(8,128)(2,1)} %copy-done.5, bf16[2,72,128]{2,1,0:T(8,128)(2,1)} %copy-done.4, f32[4,16,512]{2,1,0:T(8,128)} %weight_ref.5, f32[2,4,16,512]{3,2,1,0:T(8,128)} %offset_ref.5, ...), custom_call_target="tpu_custom_call" | custom-call | tf_op jit(solution)/shard_map/records_inner/pallas_call | solution.py:368
  26.3 0.0 collective-permute-done.3.after_ref
  26.3 0.0 copy-start.6
  26.3 0.0 collective-permute-done.2.before_ref
  26.3 0.6 copy-done.6
  26.9 0.0 copy-start.7
  26.9 0.6 copy-done.7
  27.5 4.6 %records_outer.1 = bf16[16,72,256]{2,1,0:T(8,128)(2,1)} custom-call(s32[16]{0:T(128)} %count_ref.5, f32[16,72,256]{2,1,0:T(8,128)} %records_inner.1.inner_ref, bf16[2,72,64]{2,1,0:T(8,128)(2,1)} %copy-done.7, bf16[2,72,64]{2,1,0:T(8,128)(2,1)} %copy-done.6, f32[4,16,512]{2,1,0:T(8,128)} %weight_ref.5, f32[2,4,16,512]{3,2,1,0:T(8,128)} %offset_ref.5, ...), custom_call_target="tpu_custom_call" | custom-call | tf_op jit(solution)/shard_map/records_outer/pallas_call | solution.py:371
  32.1 6.7 %all-to-all-start.1 = ((bf16[16,72,256]{2,1,0:T(8,128)(2,1)}), bf16[16,72,256]{2,1,0:T(8,128)(2,1)S(1)}, u32[]{:S(2)}, u32[]{:S(2)}) async-start(bf16[16,72,256]{2,1,0:T(8,128)(2,1)} %records_outer.1), calls=%async_computation.1 | async-start | bytes 1179648 | tf_op jit(solution)/shard_map/all_to_all | solution.py:388
  38.8 7.7 %records_late.1 = bf16[16,72,256]{2,1,0:T(8,128)(2,1)} custom-call(s32[16]{0:T(128)} %count_ref.5, bf16[64,72,128]{2,1,0:T(8,128)(2,1)} %bitcast.8, bf16[2,72,128]{2,1,0:T(8,128)(2,1)} %copy-done.5, bf16[2,72,128]{2,1,0:T(8,128)(2,1)} %copy-done.4, bf16[2,72,64]{2,1,0:T(8,128)(2,1)} %copy-done.7, bf16[2,72,64]{2,1,0:T(8,128)(2,1)} %copy-done.6, ...), custom_call_target="tpu_custom_call" | custom-call | tf_op jit(solution)/shard_map/records_late/pallas_call | solution.py:379
  46.5 5.4 %all-to-all-done.1.record_ref = bf16[16,72,256]{2,1,0:T(8,128)(2,1)S(1)} async-done(((bf16[16,72,256]{2,1,0:T(8,128)(2,1)}), bf16[16,72,256]{2,1,0:T(8,128)(2,1)S(1)}, u32[]{:S(2)}, u32[]{:S(2)}) %all-to-all-start.1) | async-done | bytes 589856 | tf_op jit(solution)/shard_map/all_to_all | solution.py:388
  51.9 0.0 copy-start.3
  51.9 3.8 %all-to-all-start = ((bf16[16,72,256]{2,1,0:T(8,128)(2,1)}), bf16[16,72,256]{2,1,0:T(8,128)(2,1)S(1)}, u32[]{:S(2)}, u32[]{:S(2)}) async-start(bf16[16,72,256]{2,1,0:T(8,128)(2,1)} %records_late.1), calls=%async_computation | async-start | bytes 1179648 | tf_op jit(solution)/shard_map/all_to_all | solution.py:388
  55.6 0.0 copy-done.3
  55.6 5.5 %deposit_0.1.before_ref = f32[1280,256]{1,0:T(8,128)} custom-call(bf16[16,72,256]{2,1,0:T(8,128)(2,1)} %copy-done.3, s32[16,512]{1,0:T(8,128)} %target_ref.3), custom_call_target="tpu_custom_call" | custom-call | tf_op jit(solution)/shard_map/deposit_0/pallas_call | solution.py:396
  61.2 7.3 %all-to-all-done.record_ref = bf16[16,72,256]{2,1,0:T(8,128)(2,1)S(1)} async-done(((bf16[16,72,256]{2,1,0:T(8,128)(2,1)}), bf16[16,72,256]{2,1,0:T(8,128)(2,1)S(1)}, u32[]{:S(2)}, u32[]{:S(2)}) %all-to-all-start) | async-done | bytes 589856 | tf_op jit(solution)/shard_map/all_to_all | solution.py:388
  68.4 0.0 copy-start.2
  68.4 0.8 %copy-done.2 = bf16[16,72,256]{2,1,0:T(8,128)(2,1)} copy-done((bf16[16,72,256]{2,1,0:T(8,128)(2,1)}, bf16[16,72,256]{2,1,0:T(8,128)(2,1)S(1)}, u32[]{:S(2)}) %copy-start.2) | copy-done | bytes 589848
  69.3 5.8 %deposit_1.1 = bf16[72,4096]{1,0:T(8,128)(2,1)} custom-call(bf16[16,72,256]{2,1,0:T(8,128)(2,1)} %copy-done.2, s32[16,512]{1,0:T(8,128)} %target_ref.3, f32[1280,256]{1,0:T(8,128)} %deposit_0.1.before_ref, f32[1,4096]{1,0:T(1,128)} %bitcast.9), custom_call_target="tpu_custom_call" | custom-call | tf_op jit(solution)/shard_map/deposit_1/pallas_call | solution.py:404
  (2 shorter events, 0.0 us)
Async XLA Ops:
  0.0 6.5 %copy-start.8 = (bf16[4,128,1]{1,0,2:T(4,128)(2,1)S(1)}, bf16[4,128,1]{1,0,2:T(4,128)(2,1)}, u32[]{:S(2)}) copy-start(bf16[4,128,1]{1,0,2:T(4,128)(2,1)} %constant.8) | copy-start | bytes 3076
  0.0 6.5 %copy-start.1 = (bf16[72,64,128]{2,1,0:T(8,128)(2,1)S(1)}, bf16[72,64,128]{2,1,0:T(8,128)(2,1)}, u32[]{:S(2)}) copy-start(bf16[72,64,128]{2,1,0:T(8,128)(2,1)} %param.8) | copy-start | bytes 3538948
  2.1 11.9 %copy-start = (bf16[72,64,128]{2,0,1:T(8,128)(2,1)}, bf16[72,64,128]{2,0,1:T(8,128)(2,1)S(1)}, u32[]{:S(2)}) copy-start(bf16[72,64,128]{2,0,1:T(8,128)(2,1)S(1)} %copy.15) | copy-start | bytes 3538948
  2.2 11.9 %collective-permute-start.1 = (bf16[2,72,128]{2,1,0:T(8,128)(2,1)S(1)}, bf16[2,72,128]{2,1,0:T(8,128)(2,1)S(1)}, u32[]{:S(2)}, u32[]{:S(2)}) collective-permute-start(bf16[2,72,128]{2,1,0:T(8,128)(2,1)S(1)} %get-tuple-element.5), channel_id=1, source_target_pairs={{16,0},{32,16},{48,32},{64,48},{80,64},{96,80},{112,96},{17,1},{33... | collective-permute-start | bytes 110600 | tf_op jit(solution)/shard_map/ppermute | solution.py:310
  3.5 10.6 %collective-permute-start = (bf16[2,72,128]{2,1,0:T(8,128)(2,1)S(1)}, bf16[2,72,128]{2,1,0:T(8,128)(2,1)S(1)}, u32[]{:S(2)}, u32[]{:S(2)}) collective-permute-start(bf16[2,72,128]{2,1,0:T(8,128)(2,1)S(1)} %get-tuple-element.6), channel_id=1, source_target_pairs={{0,16},{16,32},{32,48},{48,64},{64,80},{80,96},{96,112},{1,17},{17... | collective-permute-start | bytes 110600 | tf_op jit(solution)/shard_map/ppermute | solution.py:310
  7.6 18.6 %collective-permute-start.3 = (bf16[2,72,64]{2,1,0:T(8,128)(2,1)S(1)}, bf16[2,72,64]{2,1,0:T(8,128)(2,1)S(1)}, u32[]{:S(2)}, u32[]{:S(2)}) collective-permute-start(bf16[2,72,64]{2,1,0:T(8,128)(2,1)S(1)} %get-tuple-element.7), channel_id=1, source_target_pairs={{1,0},{2,1},{3,2},{4,3},{5,4},{6,5},{7,6},{8,7},{9,8},{10,9},{11,1... | collective-permute-start | bytes 55304 | tf_op jit(solution)/shard_map/ppermute | solution.py:310
  14.0 12.3 %collective-permute-start.2 = (bf16[2,72,64]{2,1,0:T(8,128)(2,1)S(1)}, bf16[2,72,64]{2,1,0:T(8,128)(2,1)S(1)}, u32[]{:S(2)}, u32[]{:S(2)}) collective-permute-start(bf16[2,72,64]{2,1,0:T(8,128)(2,1)S(1)} %get-tuple-element.8), channel_id=1, source_target_pairs={{0,1},{1,2},{2,3},{3,4},{4,5},{5,6},{6,7},{7,8},{8,9},{9,10},{10,1... | collective-permute-start | bytes 55304 | tf_op jit(solution)/shard_map/ppermute | solution.py:310
  14.0 0.6 copy-start.4
  14.6 0.6 copy-start.5
  26.3 0.6 copy-start.6
  26.9 0.6 copy-start.7
  32.1 19.8 %all-to-all-start.1 = ((bf16[16,72,256]{2,1,0:T(8,128)(2,1)}), bf16[16,72,256]{2,1,0:T(8,128)(2,1)S(1)}, u32[]{:S(2)}, u32[]{:S(2)}) async-start(bf16[16,72,256]{2,1,0:T(8,128)(2,1)} %records_outer.1), calls=%async_computation.1 | async-start | bytes 1179648 | tf_op jit(solution)/shard_map/all_to_all | solution.py:388
  51.9 3.8 %copy-start.3 = (bf16[16,72,256]{2,1,0:T(8,128)(2,1)}, bf16[16,72,256]{2,1,0:T(8,128)(2,1)S(1)}, u32[]{:S(2)}) copy-start(bf16[16,72,256]{2,1,0:T(8,128)(2,1)S(1)} %all-to-all-done.1.record_ref) | copy-start | bytes 1769476
  51.9 16.6 %all-to-all-start = ((bf16[16,72,256]{2,1,0:T(8,128)(2,1)}), bf16[16,72,256]{2,1,0:T(8,128)(2,1)S(1)}, u32[]{:S(2)}, u32[]{:S(2)}) async-start(bf16[16,72,256]{2,1,0:T(8,128)(2,1)} %records_late.1), calls=%async_computation | async-start | bytes 1179648 | tf_op jit(solution)/shard_map/all_to_all | solution.py:388
  68.4 0.8 %copy-start.2 = (bf16[16,72,256]{2,1,0:T(8,128)(2,1)}, bf16[16,72,256]{2,1,0:T(8,128)(2,1)S(1)}, u32[]{:S(2)}) copy-start(bf16[16,72,256]{2,1,0:T(8,128)(2,1)S(1)} %all-to-all-done.record_ref) | copy-start | bytes 1769476

commit v8 on v5

--- a/solution.py
+++ b/solution.py
@@ -93,12 +93,10 @@
     rows_ref,
     above_ref,
     below_ref,
-    before_ref,
-    after_ref,
+    beside_ref,
     weight_ref,
     offset_ref,
     cell_ref,
-    counts_ref,
     out_ref,
     full_ref,
     rim_ref,
@@ -123,13 +121,17 @@
                     part = rows_ref[r]
                 full_ref[g * fields : (g + 1) * fields, j * breadth : (j + 1) * breadth] = part
         rim_ref[...] = jnp.concatenate(
-            [side[i] for side in (before_ref, after_ref) for i in range(REACH)], axis=1
+            [beside_ref[i] for i in range(2 * REACH)], axis=1
         )
+        member = lax.broadcasted_iota(jnp.int32, cell_ref.shape, 0)
+        count = jnp.zeros(cell_ref.shape, jnp.int32)
+        for m in range(cell_ref.shape[0]):
+            count = jnp.where(member == m, count_ref[m], count)
         terms = slot_terms(
             weight_ref[...],
             offset_ref[...],
             cell_ref[...],
-            counts_ref[...],
+            count,
             start=start,
             breadth=breadth,
         )
@@ -243,8 +245,6 @@
     groups = height // GROUP
     span = GROUP + 2 * REACH
     points = gauss_weight.shape[0]
-    rows = jnp.swapaxes(source_flux, 0, 1)
-    above, below = neighbours(rows[:REACH], rows[height - REACH :], "panel", False)
     picks = np.zeros((2 * REACH, breadth), np.float32)
     for i in range(REACH):
         picks[i, i] = 1.0
@@ -255,7 +255,9 @@
         (((1,), (2,)), ((), ())),
         preferred_element_type=jnp.float32,
     ).astype(jnp.bfloat16)
-    before, after = neighbours(edges[:REACH], edges[REACH:], "blk", True)
+    beside = jnp.concatenate(neighbours(edges[:REACH], edges[REACH:], "blk", True), axis=0)
+    rows = jnp.swapaxes(source_flux, 0, 1)
+    above, below = neighbours(rows[:REACH], rows[height - REACH :], "panel", False)
     half = capacity // 2
     arrived = []
     for part, owners in enumerate(OWNERS):
@@ -268,14 +270,12 @@
                     pl.BlockSpec((height, fields, breadth), lambda i, n: (0, 0, 0)),
                     pl.BlockSpec((REACH, fields, breadth), lambda i, n: (0, 0, 0)),
                     pl.BlockSpec((REACH, fields, breadth), lambda i, n: (0, 0, 0)),
-                    pl.BlockSpec((REACH, fields, height), lambda i, n: (0, 0, 0)),
-                    pl.BlockSpec((REACH, fields, height), lambda i, n: (0, 0, 0)),
+                    pl.BlockSpec((2 * REACH, fields, height), lambda i, n: (0, 0, 0)),
                     pl.BlockSpec((points, members, half), lambda i, n, part=part: (0, 0, part)),
                     pl.BlockSpec(
                         (2, points, members, half), lambda i, n, part=part: (0, 0, 0, part)
                     ),
                     pl.BlockSpec((members, half), lambda i, n, part=part: (0, part)),
-                    pl.BlockSpec((members, 1), lambda i, n: (0, 0)),
                 ],
                 out_specs=pl.BlockSpec((owners, fields, half), lambda i, n: (i, 0, 0)),
                 scratch_shapes=[
@@ -291,12 +291,10 @@
             rows,
             above,
             below,
-            before,
-            after,
+            beside,
             gauss_weight,
             gauss_offset,
             source_cell,
-            slot_count.reshape(members, 1),
         )
         arrived.append(lax.all_to_all(records, "blk", split_axis=0, concat_axis=0, tiled=True))
     highs = cells // LOW

time: 74.7 us -> 71.7 us (0.960)
  the two profiles are of different devices: /device:TPU:8 before, /device:TPU:0 now
where the time goes in v8:
time: 71.7 us; the launch traced here: 71 us
  Pallas kernels  31.6 us (44%)
  starting transfers between devices  19.2 us (27%)
  waiting for transfers between devices  14.7 us (21%)
  local copies, waits for them, and re-layouts  2.97 us (4%)
  matrix products  2.36 us (3%)
    pallas_call x2, Pallas kernels, on_device(): pl.pallas_call(functools.partial(record_body, start=part * half), grid_sp...  20.3 us
    all_to_all x2, waiting for transfers between devices, on_device(): lax.all_to_all(records, 'blk', split_axis=0, concat_axis=0, tiled=True)  12.6 us
    ppermute x4, starting transfers between devices, neighbours(): return (lax.ppermute(last, axis, up), lax.ppermute(first, axis, down))  10.7 us
    all_to_all x2, starting transfers between devices, on_device(): lax.all_to_all(records, 'blk', split_axis=0, concat_axis=0, tiled=True)  8.53 us
    pallas_call x1, Pallas kernels, on_device(): pl.pallas_call(functools.partial(deposit_last_body, highs=highs, padded=p...  5.77 us
    pallas_call x1, Pallas kernels, on_device(): pl.pallas_call(functools.partial(deposit_first_body, highs=highs, padded=...  5.52 us
    unnamed x16, local copies, waits for them, and re-layouts  2.82 us
    dot_general x1, matrix products, on_device(): lax.dot_general(jnp.asarray(picks, jnp.bfloat16), source_flux, (((1,), (2...  2.36 us
  transfers between devices with their start and end apart: 6, of which 3 were waited for; matrix products, arithmetic and copies ran while one was open for 1% of the time, Pallas kernels for 20%

profile of v8, /device:TPU:0, one launch (start us, length us, event | category | flops | bytes accessed | tf_op | source)
XLA Modules:
  0.0 71.0 jit_solution(16220388869604182389)
XLA Ops:
  0.0 0.0 copy-start.1
  0.0 2.4 %fusion = bf16[4,72,64]{1,0,2:T(4,128)(2,1)S(1)} fusion(bf16[4,128,1]{1,0,2:T(4,128)(2,1)} %constant.8, bf16[72,64,128]{2,1,0:T(8,128)(2,1)} %param.8), kind=kOutput, calls=%fused_computation | convolution fusion | flops 4718592 | bytes 1217536 | tf_op jit(solution)/shard_map/dot_general | solution.py:252
  2.4 0.1 copy.11
  2.5 6.4 %collective-permute-start.3 = (bf16[2,72,64]{2,1,0:T(8,128)(2,1)S(1)}, bf16[2,72,64]{2,1,0:T(8,128)(2,1)S(1)}, u32[]{:S(2)}, u32[]{:S(2)}) collective-permute-start(bf16[2,72,64]{2,1,0:T(8,128)(2,1)S(1)} %get-tuple-element.7), channel_id=1, source_target_pairs={{1,0},{2,1},{3,2},{4,3},{5,4},{6,5},{7,6},{8,7},{9,8},{10,9},{11,1... | collective-permute-start | bytes 55304 | tf_op jit(solution)/shard_map/ppermute | solution.py:235
  8.9 0.0 collective-permute-start.2
  8.9 0.0 copy-done.1
  8.9 0.8 %copy.15 = bf16[72,64,128]{2,0,1:T(8,128)(2,1)S(1)} copy(bf16[72,64,128]{2,1,0:T(8,128)(2,1)S(1)} %copy-done.1) | data formatting | bytes 2359296 | tf_op args[0]
  9.7 0.0 copy-start
  9.7 1.3 %collective-permute-start.1 = (bf16[2,72,128]{2,1,0:T(8,128)(2,1)S(1)}, bf16[2,72,128]{2,1,0:T(8,128)(2,1)S(1)}, u32[]{:S(2)}, u32[]{:S(2)}) collective-permute-start(bf16[2,72,128]{2,1,0:T(8,128)(2,1)S(1)} %get-tuple-element.5), channel_id=1, source_target_pairs={{16,0},{32,16},{48,32},{64,48},{80,64},{96,80},{112,96},{17,1},{33... | collective-permute-start | bytes 110600 | tf_op jit(solution)/shard_map/ppermute | solution.py:235
  11.0 3.0 %collective-permute-start = (bf16[2,72,128]{2,1,0:T(8,128)(2,1)S(1)}, bf16[2,72,128]{2,1,0:T(8,128)(2,1)S(1)}, u32[]{:S(2)}, u32[]{:S(2)}) collective-permute-start(bf16[2,72,128]{2,1,0:T(8,128)(2,1)S(1)} %get-tuple-element.6), channel_id=1, source_target_pairs={{0,16},{16,32},{32,48},{48,64},{64,80},{80,96},{96,112},{1,17},{17... | collective-permute-start | bytes 110600 | tf_op jit(solution)/shard_map/ppermute | solution.py:235
  14.0 2.1 %collective-permute-done.2 = bf16[2,72,64]{2,1,0:T(8,128)(2,1)S(1)} collective-permute-done((bf16[2,72,64]{2,1,0:T(8,128)(2,1)S(1)}, bf16[2,72,64]{2,1,0:T(8,128)(2,1)S(1)}, u32[]{:S(2)}, u32[]{:S(2)}) %collective-permute-start.2) | collective-permute-done | bytes 18464 | tf_op jit(solution)/shard_map/ppermute | solution.py:235
  16.2 0.0 collective-permute-done.3
  16.2 0.0 copy-start.4
  16.2 0.0 collective-permute-done.1.below_ref
  16.2 0.0 copy-start.5
  16.2 0.0 collective-permute-done.above_ref
  16.2 0.0 copy-done
  16.2 0.6 copy-done.4
  16.8 0.0 copy-done.5
  16.8 0.0 copy-start.6
  16.8 0.6 copy-done.6
  17.5 11.9 %records_0.1 = bf16[16,72,256]{2,1,0:T(8,128)(2,1)} custom-call(s32[16]{0:T(128)} %count_ref.3, bf16[64,72,128]{2,1,0:T(8,128)(2,1)} %bitcast.7, bf16[2,72,128]{2,1,0:T(8,128)(2,1)} %copy-done.6, bf16[2,72,128]{2,1,0:T(8,128)(2,1)} %copy-done.5, bf16[4,72,64]{2,1,0:T(8,128)(2,1)} %copy-done.4, f32[4,16,512]{2,1,0:T(8,128)} %weight_ref.3, ...), custom_call_target="tpu_custom_call" | custom-call | tf_op jit(solution)/shard_map/records_0/pallas_call | solution.py:264
  29.3 4.8 %all-to-all-start.1 = ((bf16[16,72,256]{2,1,0:T(8,128)(2,1)}), bf16[16,72,256]{2,1,0:T(8,128)(2,1)S(1)}, u32[]{:S(2)}, u32[]{:S(2)}) async-start(bf16[16,72,256]{2,1,0:T(8,128)(2,1)} %records_0.1), calls=%async_computation.1 | async-start | bytes 1179648 | tf_op jit(solution)/shard_map/all_to_all | solution.py:299
  34.1 8.4 %records_1.1 = bf16[16,72,256]{2,1,0:T(8,128)(2,1)} custom-call(s32[16]{0:T(128)} %count_ref.3, bf16[64,72,128]{2,1,0:T(8,128)(2,1)} %bitcast.8, bf16[2,72,128]{2,1,0:T(8,128)(2,1)} %copy-done.6, bf16[2,72,128]{2,1,0:T(8,128)(2,1)} %copy-done.5, bf16[4,72,64]{2,1,0:T(8,128)(2,1)} %copy-done.4, f32[4,16,512]{2,1,0:T(8,128)} %weight_ref.3, ...), custom_call_target="tpu_custom_call" | custom-call | tf_op jit(solution)/shard_map/records_1/pallas_call | solution.py:264
  42.5 5.5 %all-to-all-done.1.record_ref = bf16[16,72,256]{2,1,0:T(8,128)(2,1)S(1)} async-done(((bf16[16,72,256]{2,1,0:T(8,128)(2,1)}), bf16[16,72,256]{2,1,0:T(8,128)(2,1)S(1)}, u32[]{:S(2)}, u32[]{:S(2)}) %all-to-all-start.1) | async-done | bytes 589856 | tf_op jit(solution)/shard_map/all_to_all | solution.py:299
  48.1 0.0 copy-start.3
  48.1 3.8 %all-to-all-start = ((bf16[16,72,256]{2,1,0:T(8,128)(2,1)}), bf16[16,72,256]{2,1,0:T(8,128)(2,1)S(1)}, u32[]{:S(2)}, u32[]{:S(2)}) async-start(bf16[16,72,256]{2,1,0:T(8,128)(2,1)} %records_1.1), calls=%async_computation | async-start | bytes 1179648 | tf_op jit(solution)/shard_map/all_to_all | solution.py:299
  51.8 0.0 copy-done.3
  51.8 5.5 %deposit_0.1.before_ref = f32[1280,256]{1,0:T(8,128)} custom-call(bf16[16,72,256]{2,1,0:T(8,128)(2,1)} %copy-done.3, s32[16,512]{1,0:T(8,128)} %target_ref.3), custom_call_target="tpu_custom_call" | custom-call | tf_op jit(solution)/shard_map/deposit_0/pallas_call | solution.py:305
  57.4 7.0 %all-to-all-done.record_ref = bf16[16,72,256]{2,1,0:T(8,128)(2,1)S(1)} async-done(((bf16[16,72,256]{2,1,0:T(8,128)(2,1)}), bf16[16,72,256]{2,1,0:T(8,128)(2,1)S(1)}, u32[]{:S(2)}, u32[]{:S(2)}) %all-to-all-start) | async-done | bytes 589856 | tf_op jit(solution)/shard_map/all_to_all | solution.py:299
  64.4 0.0 copy-start.2
  64.4 0.8 %copy-done.2 = bf16[16,72,256]{2,1,0:T(8,128)(2,1)} copy-done((bf16[16,72,256]{2,1,0:T(8,128)(2,1)}, bf16[16,72,256]{2,1,0:T(8,128)(2,1)S(1)}, u32[]{:S(2)}) %copy-start.2) | copy-done | bytes 589848
  65.2 5.8 %deposit_1.1 = bf16[72,4096]{1,0:T(8,128)(2,1)} custom-call(bf16[16,72,256]{2,1,0:T(8,128)(2,1)} %copy-done.2, s32[16,512]{1,0:T(8,128)} %target_ref.3, f32[1280,256]{1,0:T(8,128)} %deposit_0.1.before_ref, f32[1,4096]{1,0:T(1,128)} %bitcast.9), custom_call_target="tpu_custom_call" | custom-call | tf_op jit(solution)/shard_map/deposit_1/pallas_call | solution.py:313
  (4 shorter events, 0.0 us)
Async XLA Ops:
  0.0 8.9 %copy-start.1 = (bf16[72,64,128]{2,1,0:T(8,128)(2,1)S(1)}, bf16[72,64,128]{2,1,0:T(8,128)(2,1)}, u32[]{:S(2)}) copy-start(bf16[72,64,128]{2,1,0:T(8,128)(2,1)} %param.8) | copy-start | bytes 3538948
  2.5 13.7 %collective-permute-start.3 = (bf16[2,72,64]{2,1,0:T(8,128)(2,1)S(1)}, bf16[2,72,64]{2,1,0:T(8,128)(2,1)S(1)}, u32[]{:S(2)}, u32[]{:S(2)}) collective-permute-start(bf16[2,72,64]{2,1,0:T(8,128)(2,1)S(1)} %get-tuple-element.7), channel_id=1, source_target_pairs={{1,0},{2,1},{3,2},{4,3},{5,4},{6,5},{7,6},{8,7},{9,8},{10,9},{11,1... | collective-permute-start | bytes 55304 | tf_op jit(solution)/shard_map/ppermute | solution.py:235
  8.9 7.3 %collective-permute-start.2 = (bf16[2,72,64]{2,1,0:T(8,128)(2,1)S(1)}, bf16[2,72,64]{2,1,0:T(8,128)(2,1)S(1)}, u32[]{:S(2)}, u32[]{:S(2)}) collective-permute-start(bf16[2,72,64]{2,1,0:T(8,128)(2,1)S(1)} %get-tuple-element.8), channel_id=1, source_target_pairs={{0,1},{1,2},{2,3},{3,4},{4,5},{5,6},{6,7},{7,8},{8,9},{9,10},{10,1... | collective-permute-start | bytes 55304 | tf_op jit(solution)/shard_map/ppermute | solution.py:235
  9.7 6.6 %copy-start = (bf16[72,64,128]{2,0,1:T(8,128)(2,1)}, bf16[72,64,128]{2,0,1:T(8,128)(2,1)S(1)}, u32[]{:S(2)}) copy-start(bf16[72,64,128]{2,0,1:T(8,128)(2,1)S(1)} %copy.15) | copy-start | bytes 3538948
  9.7 6.5 %collective-permute-start.1 = (bf16[2,72,128]{2,1,0:T(8,128)(2,1)S(1)}, bf16[2,72,128]{2,1,0:T(8,128)(2,1)S(1)}, u32[]{:S(2)}, u32[]{:S(2)}) collective-permute-start(bf16[2,72,128]{2,1,0:T(8,128)(2,1)S(1)} %get-tuple-element.5), channel_id=1, source_target_pairs={{16,0},{32,16},{48,32},{64,48},{80,64},{96,80},{112,96},{17,1},{33... | collective-permute-start | bytes 110600 | tf_op jit(solution)/shard_map/ppermute | solution.py:235
  11.0 5.2 %collective-permute-start = (bf16[2,72,128]{2,1,0:T(8,128)(2,1)S(1)}, bf16[2,72,128]{2,1,0:T(8,128)(2,1)S(1)}, u32[]{:S(2)}, u32[]{:S(2)}) collective-permute-start(bf16[2,72,128]{2,1,0:T(8,128)(2,1)S(1)} %get-tuple-element.6), channel_id=1, source_target_pairs={{0,16},{16,32},{32,48},{48,64},{64,80},{80,96},{96,112},{1,17},{17... | collective-permute-start | bytes 110600 | tf_op jit(solution)/shard_map/ppermute | solution.py:235
  16.2 0.6 copy-start.4
  16.2 0.6 copy-start.5
  16.8 0.6 copy-start.6
  29.3 18.7 %all-to-all-start.1 = ((bf16[16,72,256]{2,1,0:T(8,128)(2,1)}), bf16[16,72,256]{2,1,0:T(8,128)(2,1)S(1)}, u32[]{:S(2)}, u32[]{:S(2)}) async-start(bf16[16,72,256]{2,1,0:T(8,128)(2,1)} %records_0.1), calls=%async_computation.1 | async-start | bytes 1179648 | tf_op jit(solution)/shard_map/all_to_all | solution.py:299
  48.1 3.8 %copy-start.3 = (bf16[16,72,256]{2,1,0:T(8,128)(2,1)}, bf16[16,72,256]{2,1,0:T(8,128)(2,1)S(1)}, u32[]{:S(2)}) copy-start(bf16[16,72,256]{2,1,0:T(8,128)(2,1)S(1)} %all-to-all-done.1.record_ref) | copy-start | bytes 1769476
  48.1 16.4 %all-to-all-start = ((bf16[16,72,256]{2,1,0:T(8,128)(2,1)}), bf16[16,72,256]{2,1,0:T(8,128)(2,1)S(1)}, u32[]{:S(2)}, u32[]{:S(2)}) async-start(bf16[16,72,256]{2,1,0:T(8,128)(2,1)} %records_1.1), calls=%async_computation | async-start | bytes 1179648 | tf_op jit(solution)/shard_map/all_to_all | solution.py:299
  64.4 0.8 %copy-start.2 = (bf16[16,72,256]{2,1,0:T(8,128)(2,1)}, bf16[16,72,256]{2,1,0:T(8,128)(2,1)S(1)}, u32[]{:S(2)}) copy-start(bf16[16,72,256]{2,1,0:T(8,128)(2,1)S(1)} %all-to-all-done.record_ref) | copy-start | bytes 1769476

commit v9 on v8

--- a/solution.py
+++ b/solution.py
@@ -12,7 +12,6 @@
 REACH = 2
 LOW = 256
 TERMS = 11
-BATCH = 8
 OWNERS = (8, 4)
 
 
@@ -162,11 +161,10 @@
 
 
 def deposit_part(record_ref, target_ref, *, highs, padded, start):
-    step = pl.program_id(0)
-    _, fields, half = record_ref.shape
-    sources = [step * BATCH + b for b in range(BATCH)]
+    members, fields, half = record_ref.shape
+    sources = range(members)
     target = jnp.concatenate(
-        [target_ref[pl.ds(k, 1), start : start + half] for k in sources], axis=1
+        [target_ref[k : k + 1, start : start + half] for k in sources], axis=1
     )
     values = jnp.concatenate([record_ref[k] for k in sources], axis=1).astype(jnp.float32)
     slots = target.shape[1]
@@ -189,43 +187,20 @@
 
 
 def deposit_first_body(record_ref, target_ref, total_ref, *, highs, padded):
-    part = deposit_part(record_ref, target_ref, highs=highs, padded=padded, start=0)
-
-    @pl.when(pl.program_id(0) == 0)
-    def first():
-        total_ref[...] = part
-
-    @pl.when(pl.program_id(0) > 0)
-    def later():
-        total_ref[...] = total_ref[...] + part
-
-
-def deposit_last_body(
-    record_ref, target_ref, before_ref, area_ref, out_ref, total_ref, *, highs, padded
-):
-    step = pl.program_id(0)
-    last = pl.num_programs(0) - 1
+    total_ref[...] = deposit_part(record_ref, target_ref, highs=highs, padded=padded, start=0)
+
+
+def deposit_last_body(record_ref, target_ref, before_ref, area_ref, out_ref, *, highs, padded):
     fields = out_ref.shape[0]
     part = deposit_part(
         record_ref, target_ref, highs=highs, padded=padded, start=record_ref.shape[2]
     )
-
-    @pl.when(step == 0)
-    def first():
-        total_ref[...] = before_ref[...] + part
-
-    @pl.when(jnp.logical_and(step > 0, step < last))
-    def later():
-        total_ref[...] = total_ref[...] + part
-
-    @pl.when(step == last)
-    def finish():
-        for h in range(highs):
-            cut = slice(h * padded, h * padded + fields)
-            inverse = 1.0 / area_ref[:, h * LOW : (h + 1) * LOW]
-            out_ref[:, h * LOW : (h + 1) * LOW] = (
-                (total_ref[cut, :] + part[cut]) * inverse
-            ).astype(jnp.bfloat16)
+    for h in range(highs):
+        cut = slice(h * padded, h * padded + fields)
+        inverse = 1.0 / area_ref[:, h * LOW : (h + 1) * LOW]
+        out_ref[:, h * LOW : (h + 1) * LOW] = (
+            (before_ref[cut, :] + part[cut]) * inverse
+        ).astype(jnp.bfloat16)
 
 
 def neighbours(first, last, axis, wrap):
@@ -304,7 +279,7 @@
     total_spec = pl.BlockSpec((highs * padded, LOW), lambda i: (0, 0))
     before = pl.pallas_call(
         functools.partial(deposit_first_body, highs=highs, padded=padded),
-        grid=(members // BATCH,),
+        grid=(1,),
         in_specs=[record_spec, target_spec],
         out_specs=total_spec,
         out_shape=jax.ShapeDtypeStruct((highs * padded, LOW), jnp.float32),
@@ -312,7 +287,7 @@
     )(arrived[0], target_cell)
     return pl.pallas_call(
         functools.partial(deposit_last_body, highs=highs, padded=padded),
-        grid=(members // BATCH,),
+        grid=(1,),
         in_specs=[
             record_spec,
             target_spec,
@@ -321,7 +296,6 @@
         ],
         out_specs=pl.BlockSpec((fields, cells), lambda i: (0, 0)),
         out_shape=jax.ShapeDtypeStruct((fields, cells), jnp.bfloat16),
-        scratch_shapes=[pltpu.VMEM((highs * padded, LOW), jnp.float32)],
         name="deposit_1",
     )(arrived[1], target_cell, before, target_area.reshape(1, cells))
 

time: 71.7 us -> 71.3 us (level)
  Pallas kernels: 31.6 us -> 30.6 us
  transfers between devices with their start and end apart: 6 -> 6, of which waited for: 3 -> 3; matrix products, arithmetic and copies ran while one was open for 1% -> 1% of each run, Pallas kernels for 20% -> 19%
where the time goes in v9:
time: 71.3 us; the launch traced here: 70.5 us
  Pallas kernels  30.6 us (43%)
  starting transfers between devices  19.2 us (27%)
  waiting for transfers between devices  15.2 us (21%)
  local copies, waits for them, and re-layouts  2.97 us (4%)
  matrix products  2.36 us (3%)
    pallas_call x2, Pallas kernels, on_device(): pl.pallas_call(functools.partial(record_body, start=part * half), grid_sp...  20.3 us
    all_to_all x2, waiting for transfers between devices, on_device(): lax.all_to_all(records, 'blk', split_axis=0, concat_axis=0, tiled=True)  13 us
    ppermute x4, starting transfers between devices, neighbours(): return (lax.ppermute(last, axis, up), lax.ppermute(first, axis, down))  10.7 us
    all_to_all x2, starting transfers between devices, on_device(): lax.all_to_all(records, 'blk', split_axis=0, concat_axis=0, tiled=True)  8.53 us
    pallas_call x1, Pallas kernels, on_device(): pl.pallas_call(functools.partial(deposit_last_body, highs=highs, padded=p...  5.29 us
    pallas_call x1, Pallas kernels, on_device(): pl.pallas_call(functools.partial(deposit_first_body, highs=highs, padded=...  5.07 us
    unnamed x16, local copies, waits for them, and re-layouts  2.82 us
    dot_general x1, matrix products, on_device(): lax.dot_general(jnp.asarray(picks, jnp.bfloat16), source_flux, (((1,), (2...  2.36 us
  transfers between devices with their start and end apart: 6, of which 3 were waited for; matrix products, arithmetic and copies ran while one was open for 1% of the time, Pallas kernels for 19%

profile of v9, /device:TPU:0, one launch (start us, length us, event | category | flops | bytes accessed | tf_op | source)
XLA Modules:
  0.0 70.5 jit_solution(10630266603367057818)
XLA Ops:
  0.0 0.0 copy-start.1
  0.0 2.4 %fusion = bf16[4,72,64]{1,0,2:T(4,128)(2,1)S(1)} fusion(bf16[4,128,1]{1,0,2:T(4,128)(2,1)} %constant.8, bf16[72,64,128]{2,1,0:T(8,128)(2,1)} %param.8), kind=kOutput, calls=%fused_computation | convolution fusion | flops 4718592 | bytes 1217536 | tf_op jit(solution)/shard_map/dot_general | solution.py:227
  2.4 0.1 copy.11
  2.5 6.4 %collective-permute-start.3 = (bf16[2,72,64]{2,1,0:T(8,128)(2,1)S(1)}, bf16[2,72,64]{2,1,0:T(8,128)(2,1)S(1)}, u32[]{:S(2)}, u32[]{:S(2)}) collective-permute-start(bf16[2,72,64]{2,1,0:T(8,128)(2,1)S(1)} %get-tuple-element.7), channel_id=1, source_target_pairs={{1,0},{2,1},{3,2},{4,3},{5,4},{6,5},{7,6},{8,7},{9,8},{10,9},{11,1... | collective-permute-start | bytes 55304 | tf_op jit(solution)/shard_map/ppermute | solution.py:210
  8.9 0.0 collective-permute-start.2
  8.9 0.0 copy-done.1
  8.9 0.8 %copy.15 = bf16[72,64,128]{2,0,1:T(8,128)(2,1)S(1)} copy(bf16[72,64,128]{2,1,0:T(8,128)(2,1)S(1)} %copy-done.1) | data formatting | bytes 2359296 | tf_op args[0]
  9.7 0.0 copy-start
  9.7 1.3 %collective-permute-start.1 = (bf16[2,72,128]{2,1,0:T(8,128)(2,1)S(1)}, bf16[2,72,128]{2,1,0:T(8,128)(2,1)S(1)}, u32[]{:S(2)}, u32[]{:S(2)}) collective-permute-start(bf16[2,72,128]{2,1,0:T(8,128)(2,1)S(1)} %get-tuple-element.5), channel_id=1, source_target_pairs={{16,0},{32,16},{48,32},{64,48},{80,64},{96,80},{112,96},{17,1},{33... | collective-permute-start | bytes 110600 | tf_op jit(solution)/shard_map/ppermute | solution.py:210
  11.0 3.0 %collective-permute-start = (bf16[2,72,128]{2,1,0:T(8,128)(2,1)S(1)}, bf16[2,72,128]{2,1,0:T(8,128)(2,1)S(1)}, u32[]{:S(2)}, u32[]{:S(2)}) collective-permute-start(bf16[2,72,128]{2,1,0:T(8,128)(2,1)S(1)} %get-tuple-element.6), channel_id=1, source_target_pairs={{0,16},{16,32},{32,48},{48,64},{64,80},{80,96},{96,112},{1,17},{17... | collective-permute-start | bytes 110600 | tf_op jit(solution)/shard_map/ppermute | solution.py:210
  14.0 2.1 %collective-permute-done.2 = bf16[2,72,64]{2,1,0:T(8,128)(2,1)S(1)} collective-permute-done((bf16[2,72,64]{2,1,0:T(8,128)(2,1)S(1)}, bf16[2,72,64]{2,1,0:T(8,128)(2,1)S(1)}, u32[]{:S(2)}, u32[]{:S(2)}) %collective-permute-start.2) | collective-permute-done | bytes 18464 | tf_op jit(solution)/shard_map/ppermute | solution.py:210
  16.2 0.0 collective-permute-done.3
  16.2 0.0 copy-start.4
  16.2 0.0 collective-permute-done.1.below_ref
  16.2 0.0 copy-start.5
  16.2 0.0 collective-permute-done.above_ref
  16.2 0.0 copy-done
  16.2 0.6 copy-done.4
  16.8 0.0 copy-done.5
  16.8 0.0 copy-start.6
  16.8 0.6 copy-done.6
  17.5 11.9 %records_0.1 = bf16[16,72,256]{2,1,0:T(8,128)(2,1)} custom-call(s32[16]{0:T(128)} %count_ref.3, bf16[64,72,128]{2,1,0:T(8,128)(2,1)} %bitcast.7, bf16[2,72,128]{2,1,0:T(8,128)(2,1)} %copy-done.6, bf16[2,72,128]{2,1,0:T(8,128)(2,1)} %copy-done.5, bf16[4,72,64]{2,1,0:T(8,128)(2,1)} %copy-done.4, f32[4,16,512]{2,1,0:T(8,128)} %weight_ref.3, ...), custom_call_target="tpu_custom_call" | custom-call | tf_op jit(solution)/shard_map/records_0/pallas_call | solution.py:239
  29.3 4.8 %all-to-all-start.1 = ((bf16[16,72,256]{2,1,0:T(8,128)(2,1)}), bf16[16,72,256]{2,1,0:T(8,128)(2,1)S(1)}, u32[]{:S(2)}, u32[]{:S(2)}) async-start(bf16[16,72,256]{2,1,0:T(8,128)(2,1)} %records_0.1), calls=%async_computation.1 | async-start | bytes 1179648 | tf_op jit(solution)/shard_map/all_to_all | solution.py:274
  34.1 8.4 %records_1.1 = bf16[16,72,256]{2,1,0:T(8,128)(2,1)} custom-call(s32[16]{0:T(128)} %count_ref.3, bf16[64,72,128]{2,1,0:T(8,128)(2,1)} %bitcast.8, bf16[2,72,128]{2,1,0:T(8,128)(2,1)} %copy-done.6, bf16[2,72,128]{2,1,0:T(8,128)(2,1)} %copy-done.5, bf16[4,72,64]{2,1,0:T(8,128)(2,1)} %copy-done.4, f32[4,16,512]{2,1,0:T(8,128)} %weight_ref.3, ...), custom_call_target="tpu_custom_call" | custom-call | tf_op jit(solution)/shard_map/records_1/pallas_call | solution.py:239
  42.5 5.5 %all-to-all-done.1.record_ref = bf16[16,72,256]{2,1,0:T(8,128)(2,1)S(1)} async-done(((bf16[16,72,256]{2,1,0:T(8,128)(2,1)}), bf16[16,72,256]{2,1,0:T(8,128)(2,1)S(1)}, u32[]{:S(2)}, u32[]{:S(2)}) %all-to-all-start.1) | async-done | bytes 589856 | tf_op jit(solution)/shard_map/all_to_all | solution.py:274
  48.1 0.0 copy-start.3
  48.1 3.8 %all-to-all-start = ((bf16[16,72,256]{2,1,0:T(8,128)(2,1)}), bf16[16,72,256]{2,1,0:T(8,128)(2,1)S(1)}, u32[]{:S(2)}, u32[]{:S(2)}) async-start(bf16[16,72,256]{2,1,0:T(8,128)(2,1)} %records_1.1), calls=%async_computation | async-start | bytes 1179648 | tf_op jit(solution)/shard_map/all_to_all | solution.py:274
  51.8 0.0 copy-done.3
  51.8 5.1 %deposit_0.1.before_ref = f32[1280,256]{1,0:T(8,128)} custom-call(bf16[16,72,256]{2,1,0:T(8,128)(2,1)} %copy-done.3, s32[16,512]{1,0:T(8,128)} %target_ref.3), custom_call_target="tpu_custom_call" | custom-call | tf_op jit(solution)/shard_map/deposit_0/pallas_call | solution.py:280
  56.9 7.5 %all-to-all-done.record_ref = bf16[16,72,256]{2,1,0:T(8,128)(2,1)S(1)} async-done(((bf16[16,72,256]{2,1,0:T(8,128)(2,1)}), bf16[16,72,256]{2,1,0:T(8,128)(2,1)S(1)}, u32[]{:S(2)}, u32[]{:S(2)}) %all-to-all-start) | async-done | bytes 589856 | tf_op jit(solution)/shard_map/all_to_all | solution.py:274
  64.4 0.0 copy-start.2
  64.4 0.8 %copy-done.2 = bf16[16,72,256]{2,1,0:T(8,128)(2,1)} copy-done((bf16[16,72,256]{2,1,0:T(8,128)(2,1)}, bf16[16,72,256]{2,1,0:T(8,128)(2,1)S(1)}, u32[]{:S(2)}) %copy-start.2) | copy-done | bytes 589848
  65.2 5.3 %deposit_1.1 = bf16[72,4096]{1,0:T(8,128)(2,1)} custom-call(bf16[16,72,256]{2,1,0:T(8,128)(2,1)} %copy-done.2, s32[16,512]{1,0:T(8,128)} %target_ref.3, f32[1280,256]{1,0:T(8,128)} %deposit_0.1.before_ref, f32[1,4096]{1,0:T(1,128)} %bitcast.9), custom_call_target="tpu_custom_call" | custom-call | tf_op jit(solution)/shard_map/deposit_1/pallas_call | solution.py:288
  (4 shorter events, 0.0 us)
Async XLA Ops:
  0.0 8.9 %copy-start.1 = (bf16[72,64,128]{2,1,0:T(8,128)(2,1)S(1)}, bf16[72,64,128]{2,1,0:T(8,128)(2,1)}, u32[]{:S(2)}) copy-start(bf16[72,64,128]{2,1,0:T(8,128)(2,1)} %param.8) | copy-start | bytes 3538948
  2.5 13.7 %collective-permute-start.3 = (bf16[2,72,64]{2,1,0:T(8,128)(2,1)S(1)}, bf16[2,72,64]{2,1,0:T(8,128)(2,1)S(1)}, u32[]{:S(2)}, u32[]{:S(2)}) collective-permute-start(bf16[2,72,64]{2,1,0:T(8,128)(2,1)S(1)} %get-tuple-element.7), channel_id=1, source_target_pairs={{1,0},{2,1},{3,2},{4,3},{5,4},{6,5},{7,6},{8,7},{9,8},{10,9},{11,1... | collective-permute-start | bytes 55304 | tf_op jit(solution)/shard_map/ppermute | solution.py:210
  8.9 7.3 %collective-permute-start.2 = (bf16[2,72,64]{2,1,0:T(8,128)(2,1)S(1)}, bf16[2,72,64]{2,1,0:T(8,128)(2,1)S(1)}, u32[]{:S(2)}, u32[]{:S(2)}) collective-permute-start(bf16[2,72,64]{2,1,0:T(8,128)(2,1)S(1)} %get-tuple-element.8), channel_id=1, source_target_pairs={{0,1},{1,2},{2,3},{3,4},{4,5},{5,6},{6,7},{7,8},{8,9},{9,10},{10,1... | collective-permute-start | bytes 55304 | tf_op jit(solution)/shard_map/ppermute | solution.py:210
  9.7 6.6 %copy-start = (bf16[72,64,128]{2,0,1:T(8,128)(2,1)}, bf16[72,64,128]{2,0,1:T(8,128)(2,1)S(1)}, u32[]{:S(2)}) copy-start(bf16[72,64,128]{2,0,1:T(8,128)(2,1)S(1)} %copy.15) | copy-start | bytes 3538948
  9.7 6.5 %collective-permute-start.1 = (bf16[2,72,128]{2,1,0:T(8,128)(2,1)S(1)}, bf16[2,72,128]{2,1,0:T(8,128)(2,1)S(1)}, u32[]{:S(2)}, u32[]{:S(2)}) collective-permute-start(bf16[2,72,128]{2,1,0:T(8,128)(2,1)S(1)} %get-tuple-element.5), channel_id=1, source_target_pairs={{16,0},{32,16},{48,32},{64,48},{80,64},{96,80},{112,96},{17,1},{33... | collective-permute-start | bytes 110600 | tf_op jit(solution)/shard_map/ppermute | solution.py:210
  11.0 5.2 %collective-permute-start = (bf16[2,72,128]{2,1,0:T(8,128)(2,1)S(1)}, bf16[2,72,128]{2,1,0:T(8,128)(2,1)S(1)}, u32[]{:S(2)}, u32[]{:S(2)}) collective-permute-start(bf16[2,72,128]{2,1,0:T(8,128)(2,1)S(1)} %get-tuple-element.6), channel_id=1, source_target_pairs={{0,16},{16,32},{32,48},{48,64},{64,80},{80,96},{96,112},{1,17},{17... | collective-permute-start | bytes 110600 | tf_op jit(solution)/shard_map/ppermute | solution.py:210
  16.2 0.6 copy-start.4
  16.2 0.6 copy-start.5
  16.8 0.6 copy-start.6
  29.3 18.7 %all-to-all-start.1 = ((bf16[16,72,256]{2,1,0:T(8,128)(2,1)}), bf16[16,72,256]{2,1,0:T(8,128)(2,1)S(1)}, u32[]{:S(2)}, u32[]{:S(2)}) async-start(bf16[16,72,256]{2,1,0:T(8,128)(2,1)} %records_0.1), calls=%async_computation.1 | async-start | bytes 1179648 | tf_op jit(solution)/shard_map/all_to_all | solution.py:274
  48.1 3.8 %copy-start.3 = (bf16[16,72,256]{2,1,0:T(8,128)(2,1)}, bf16[16,72,256]{2,1,0:T(8,128)(2,1)S(1)}, u32[]{:S(2)}) copy-start(bf16[16,72,256]{2,1,0:T(8,128)(2,1)S(1)} %all-to-all-done.1.record_ref) | copy-start | bytes 1769476
  48.1 16.4 %all-to-all-start = ((bf16[16,72,256]{2,1,0:T(8,128)(2,1)}), bf16[16,72,256]{2,1,0:T(8,128)(2,1)S(1)}, u32[]{:S(2)}, u32[]{:S(2)}) async-start(bf16[16,72,256]{2,1,0:T(8,128)(2,1)} %records_1.1), calls=%async_computation | async-start | bytes 1179648 | tf_op jit(solution)/shard_map/all_to_all | solution.py:274
  64.4 0.8 %copy-start.2 = (bf16[16,72,256]{2,1,0:T(8,128)(2,1)}, bf16[16,72,256]{2,1,0:T(8,128)(2,1)S(1)}, u32[]{:S(2)}) copy-start(bf16[16,72,256]{2,1,0:T(8,128)(2,1)S(1)} %all-to-all-done.record_ref) | copy-start | bytes 1769476

commit v10 on v9

--- a/solution.py
+++ b/solution.py
@@ -12,7 +12,7 @@
 REACH = 2
 LOW = 256
 TERMS = 11
-OWNERS = (8, 4)
+OWNERS = (16, 4)
 
 
 def slot_records(terms, window_ref, rim, *, fields, height, breadth):

time: 71.3 us -> 71.5 us (level)
  Pallas kernels: 30.6 us -> 28.9 us
  waiting for transfers between devices: 15.2 us -> 16.8 us
    pallas_call x2, Pallas kernels: 20.3 us -> 18.5 us  [on_device(): pl.pallas_call(functools.partial(record_body, start=part * half), grid_sp...]
    all_to_all x2, waiting for transfers between devices: 13 us -> 14.6 us  [on_device(): lax.all_to_all(records, 'blk', split_axis=0, concat_axis=0, tiled=True)]
  transfers between devices with their start and end apart: 6 -> 6, of which waited for: 3 -> 3; matrix products, arithmetic and copies ran while one was open for 1% -> 1% of each run, Pallas kernels for 19% -> 17%
where the time goes in v10:
time: 71.5 us; the launch traced here: 70.2 us
  Pallas kernels  28.9 us (40%)
  starting transfers between devices  19.1 us (27%)
  waiting for transfers between devices  16.8 us (23%)
  local copies, waits for them, and re-layouts  2.97 us (4%)
  matrix products  2.36 us (3%)
    pallas_call x2, Pallas kernels, on_device(): pl.pallas_call(functools.partial(record_body, start=part * half), grid_sp...  18.5 us
    all_to_all x2, waiting for transfers between devices, on_device(): lax.all_to_all(records, 'blk', split_axis=0, concat_axis=0, tiled=True)  14.6 us
    ppermute x4, starting transfers between devices, neighbours(): return (lax.ppermute(last, axis, up), lax.ppermute(first, axis, down))  10.7 us
    all_to_all x2, starting transfers between devices, on_device(): lax.all_to_all(records, 'blk', split_axis=0, concat_axis=0, tiled=True)  8.36 us
    pallas_call x1, Pallas kernels, on_device(): pl.pallas_call(functools.partial(deposit_last_body, highs=highs, padded=p...  5.29 us
    pallas_call x1, Pallas kernels, on_device(): pl.pallas_call(functools.partial(deposit_first_body, highs=highs, padded=...  5.07 us
    unnamed x16, local copies, waits for them, and re-layouts  2.82 us
    dot_general x1, matrix products, on_device(): lax.dot_general(jnp.asarray(picks, jnp.bfloat16), source_flux, (((1,), (2...  2.36 us
  transfers between devices with their start and end apart: 6, of which 3 were waited for; matrix products, arithmetic and copies ran while one was open for 1% of the time, Pallas kernels for 17%

profile of v10, /device:TPU:0, one launch (start us, length us, event | category | flops | bytes accessed | tf_op | source)
XLA Modules:
  0.0 70.2 jit_solution(8512414782353925365)
XLA Ops:
  0.0 0.0 copy-start.1
  0.0 2.4 %fusion = bf16[4,72,64]{1,0,2:T(4,128)(2,1)S(1)} fusion(bf16[4,128,1]{1,0,2:T(4,128)(2,1)} %constant.8, bf16[72,64,128]{2,1,0:T(8,128)(2,1)} %param.8), kind=kOutput, calls=%fused_computation | convolution fusion | flops 4718592 | bytes 1217536 | tf_op jit(solution)/shard_map/dot_general | solution.py:227
  2.4 0.1 copy.11
  2.5 6.4 %collective-permute-start.3 = (bf16[2,72,64]{2,1,0:T(8,128)(2,1)S(1)}, bf16[2,72,64]{2,1,0:T(8,128)(2,1)S(1)}, u32[]{:S(2)}, u32[]{:S(2)}) collective-permute-start(bf16[2,72,64]{2,1,0:T(8,128)(2,1)S(1)} %get-tuple-element.7), channel_id=1, source_target_pairs={{1,0},{2,1},{3,2},{4,3},{5,4},{6,5},{7,6},{8,7},{9,8},{10,9},{11,1... | collective-permute-start | bytes 55304 | tf_op jit(solution)/shard_map/ppermute | solution.py:210
  8.9 0.0 collective-permute-start.2
  8.9 0.0 copy-done.1
  8.9 0.8 %copy.15 = bf16[72,64,128]{2,0,1:T(8,128)(2,1)S(1)} copy(bf16[72,64,128]{2,1,0:T(8,128)(2,1)S(1)} %copy-done.1) | data formatting | bytes 2359296 | tf_op args[0]
  9.7 0.0 copy-start
  9.7 1.3 %collective-permute-start.1 = (bf16[2,72,128]{2,1,0:T(8,128)(2,1)S(1)}, bf16[2,72,128]{2,1,0:T(8,128)(2,1)S(1)}, u32[]{:S(2)}, u32[]{:S(2)}) collective-permute-start(bf16[2,72,128]{2,1,0:T(8,128)(2,1)S(1)} %get-tuple-element.5), channel_id=1, source_target_pairs={{16,0},{32,16},{48,32},{64,48},{80,64},{96,80},{112,96},{17,1},{33... | collective-permute-start | bytes 110600 | tf_op jit(solution)/shard_map/ppermute | solution.py:210
  11.0 3.0 %collective-permute-start = (bf16[2,72,128]{2,1,0:T(8,128)(2,1)S(1)}, bf16[2,72,128]{2,1,0:T(8,128)(2,1)S(1)}, u32[]{:S(2)}, u32[]{:S(2)}) collective-permute-start(bf16[2,72,128]{2,1,0:T(8,128)(2,1)S(1)} %get-tuple-element.6), channel_id=1, source_target_pairs={{0,16},{16,32},{32,48},{48,64},{64,80},{80,96},{96,112},{1,17},{17... | collective-permute-start | bytes 110600 | tf_op jit(solution)/shard_map/ppermute | solution.py:210
  14.0 2.1 %collective-permute-done.2 = bf16[2,72,64]{2,1,0:T(8,128)(2,1)S(1)} collective-permute-done((bf16[2,72,64]{2,1,0:T(8,128)(2,1)S(1)}, bf16[2,72,64]{2,1,0:T(8,128)(2,1)S(1)}, u32[]{:S(2)}, u32[]{:S(2)}) %collective-permute-start.2) | collective-permute-done | bytes 18464 | tf_op jit(solution)/shard_map/ppermute | solution.py:210
  16.2 0.0 collective-permute-done.3
  16.2 0.0 copy-start.4
  16.2 0.0 collective-permute-done.1.below_ref
  16.2 0.0 copy-start.5
  16.2 0.0 collective-permute-done.above_ref
  16.2 0.0 copy-done
  16.2 0.6 copy-done.4
  16.8 0.0 copy-done.5
  16.8 0.0 copy-start.6
  16.8 0.6 copy-done.6
  17.5 11.5 %records_0.1 = bf16[16,72,256]{2,1,0:T(8,128)(2,1)} custom-call(s32[16]{0:T(128)} %count_ref.3, bf16[64,72,128]{2,1,0:T(8,128)(2,1)} %bitcast.7, bf16[2,72,128]{2,1,0:T(8,128)(2,1)} %copy-done.6, bf16[2,72,128]{2,1,0:T(8,128)(2,1)} %copy-done.5, bf16[4,72,64]{2,1,0:T(8,128)(2,1)} %copy-done.4, f32[4,16,512]{2,1,0:T(8,128)} %weight_ref.3, ...), custom_call_target="tpu_custom_call" | custom-call | tf_op jit(solution)/shard_map/records_0/pallas_call | solution.py:239
  29.0 4.8 %all-to-all-start.1 = ((bf16[16,72,256]{2,1,0:T(8,128)(2,1)}), bf16[16,72,256]{2,1,0:T(8,128)(2,1)S(1)}, u32[]{:S(2)}, u32[]{:S(2)}) async-start(bf16[16,72,256]{2,1,0:T(8,128)(2,1)} %records_0.1), calls=%async_computation.1 | async-start | bytes 1179648 | tf_op jit(solution)/shard_map/all_to_all | solution.py:274
  33.8 7.0 %records_1.1 = bf16[16,72,256]{2,1,0:T(8,128)(2,1)} custom-call(s32[16]{0:T(128)} %count_ref.3, bf16[64,72,128]{2,1,0:T(8,128)(2,1)} %bitcast.8, bf16[2,72,128]{2,1,0:T(8,128)(2,1)} %copy-done.6, bf16[2,72,128]{2,1,0:T(8,128)(2,1)} %copy-done.5, bf16[4,72,64]{2,1,0:T(8,128)(2,1)} %copy-done.4, f32[4,16,512]{2,1,0:T(8,128)} %weight_ref.3, ...), custom_call_target="tpu_custom_call" | custom-call | tf_op jit(solution)/shard_map/records_1/pallas_call | solution.py:239
  40.8 7.0 %all-to-all-done.1.record_ref = bf16[16,72,256]{2,1,0:T(8,128)(2,1)S(1)} async-done(((bf16[16,72,256]{2,1,0:T(8,128)(2,1)}), bf16[16,72,256]{2,1,0:T(8,128)(2,1)S(1)}, u32[]{:S(2)}, u32[]{:S(2)}) %all-to-all-start.1) | async-done | bytes 589856 | tf_op jit(solution)/shard_map/all_to_all | solution.py:274
  47.7 0.0 copy-start.3
  47.7 3.6 %all-to-all-start = ((bf16[16,72,256]{2,1,0:T(8,128)(2,1)}), bf16[16,72,256]{2,1,0:T(8,128)(2,1)S(1)}, u32[]{:S(2)}, u32[]{:S(2)}) async-start(bf16[16,72,256]{2,1,0:T(8,128)(2,1)} %records_1.1), calls=%async_computation | async-start | bytes 1179648 | tf_op jit(solution)/shard_map/all_to_all | solution.py:274
  51.3 0.0 copy-done.3
  51.3 5.1 %deposit_0.1.before_ref = f32[1280,256]{1,0:T(8,128)} custom-call(bf16[16,72,256]{2,1,0:T(8,128)(2,1)} %copy-done.3, s32[16,512]{1,0:T(8,128)} %target_ref.3), custom_call_target="tpu_custom_call" | custom-call | tf_op jit(solution)/shard_map/deposit_0/pallas_call | solution.py:280
  56.4 7.7 %all-to-all-done.record_ref = bf16[16,72,256]{2,1,0:T(8,128)(2,1)S(1)} async-done(((bf16[16,72,256]{2,1,0:T(8,128)(2,1)}), bf16[16,72,256]{2,1,0:T(8,128)(2,1)S(1)}, u32[]{:S(2)}, u32[]{:S(2)}) %all-to-all-start) | async-done | bytes 589856 | tf_op jit(solution)/shard_map/all_to_all | solution.py:274
  64.1 0.0 copy-start.2
  64.1 0.8 %copy-done.2 = bf16[16,72,256]{2,1,0:T(8,128)(2,1)} copy-done((bf16[16,72,256]{2,1,0:T(8,128)(2,1)}, bf16[16,72,256]{2,1,0:T(8,128)(2,1)S(1)}, u32[]{:S(2)}) %copy-start.2) | copy-done | bytes 589848
  64.9 5.3 %deposit_1.1 = bf16[72,4096]{1,0:T(8,128)(2,1)} custom-call(bf16[16,72,256]{2,1,0:T(8,128)(2,1)} %copy-done.2, s32[16,512]{1,0:T(8,128)} %target_ref.3, f32[1280,256]{1,0:T(8,128)} %deposit_0.1.before_ref, f32[1,4096]{1,0:T(1,128)} %bitcast.9), custom_call_target="tpu_custom_call" | custom-call | tf_op jit(solution)/shard_map/deposit_1/pallas_call | solution.py:288
  (4 shorter events, 0.0 us)
Async XLA Ops:
  0.0 8.9 %copy-start.1 = (bf16[72,64,128]{2,1,0:T(8,128)(2,1)S(1)}, bf16[72,64,128]{2,1,0:T(8,128)(2,1)}, u32[]{:S(2)}) copy-start(bf16[72,64,128]{2,1,0:T(8,128)(2,1)} %param.8) | copy-start | bytes 3538948
  2.5 13.7 %collective-permute-start.3 = (bf16[2,72,64]{2,1,0:T(8,128)(2,1)S(1)}, bf16[2,72,64]{2,1,0:T(8,128)(2,1)S(1)}, u32[]{:S(2)}, u32[]{:S(2)}) collective-permute-start(bf16[2,72,64]{2,1,0:T(8,128)(2,1)S(1)} %get-tuple-element.7), channel_id=1, source_target_pairs={{1,0},{2,1},{3,2},{4,3},{5,4},{6,5},{7,6},{8,7},{9,8},{10,9},{11,1... | collective-permute-start | bytes 55304 | tf_op jit(solution)/shard_map/ppermute | solution.py:210
  8.9 7.3 %collective-permute-start.2 = (bf16[2,72,64]{2,1,0:T(8,128)(2,1)S(1)}, bf16[2,72,64]{2,1,0:T(8,128)(2,1)S(1)}, u32[]{:S(2)}, u32[]{:S(2)}) collective-permute-start(bf16[2,72,64]{2,1,0:T(8,128)(2,1)S(1)} %get-tuple-element.8), channel_id=1, source_target_pairs={{0,1},{1,2},{2,3},{3,4},{4,5},{5,6},{6,7},{7,8},{8,9},{9,10},{10,1... | collective-permute-start | bytes 55304 | tf_op jit(solution)/shard_map/ppermute | solution.py:210
  9.7 6.6 %copy-start = (bf16[72,64,128]{2,0,1:T(8,128)(2,1)}, bf16[72,64,128]{2,0,1:T(8,128)(2,1)S(1)}, u32[]{:S(2)}) copy-start(bf16[72,64,128]{2,0,1:T(8,128)(2,1)S(1)} %copy.15) | copy-start | bytes 3538948
  9.7 6.5 %collective-permute-start.1 = (bf16[2,72,128]{2,1,0:T(8,128)(2,1)S(1)}, bf16[2,72,128]{2,1,0:T(8,128)(2,1)S(1)}, u32[]{:S(2)}, u32[]{:S(2)}) collective-permute-start(bf16[2,72,128]{2,1,0:T(8,128)(2,1)S(1)} %get-tuple-element.5), channel_id=1, source_target_pairs={{16,0},{32,16},{48,32},{64,48},{80,64},{96,80},{112,96},{17,1},{33... | collective-permute-start | bytes 110600 | tf_op jit(solution)/shard_map/ppermute | solution.py:210
  11.0 5.2 %collective-permute-start = (bf16[2,72,128]{2,1,0:T(8,128)(2,1)S(1)}, bf16[2,72,128]{2,1,0:T(8,128)(2,1)S(1)}, u32[]{:S(2)}, u32[]{:S(2)}) collective-permute-start(bf16[2,72,128]{2,1,0:T(8,128)(2,1)S(1)} %get-tuple-element.6), channel_id=1, source_target_pairs={{0,16},{16,32},{32,48},{48,64},{64,80},{80,96},{96,112},{1,17},{17... | collective-permute-start | bytes 110600 | tf_op jit(solution)/shard_map/ppermute | solution.py:210
  16.2 0.6 copy-start.4
  16.2 0.6 copy-start.5
  16.8 0.6 copy-start.6
  29.0 18.7 %all-to-all-start.1 = ((bf16[16,72,256]{2,1,0:T(8,128)(2,1)}), bf16[16,72,256]{2,1,0:T(8,128)(2,1)S(1)}, u32[]{:S(2)}, u32[]{:S(2)}) async-start(bf16[16,72,256]{2,1,0:T(8,128)(2,1)} %records_0.1), calls=%async_computation.1 | async-start | bytes 1179648 | tf_op jit(solution)/shard_map/all_to_all | solution.py:274
  47.7 3.6 %copy-start.3 = (bf16[16,72,256]{2,1,0:T(8,128)(2,1)}, bf16[16,72,256]{2,1,0:T(8,128)(2,1)S(1)}, u32[]{:S(2)}) copy-start(bf16[16,72,256]{2,1,0:T(8,128)(2,1)S(1)} %all-to-all-done.1.record_ref) | copy-start | bytes 1769476
  47.7 16.4 %all-to-all-start = ((bf16[16,72,256]{2,1,0:T(8,128)(2,1)}), bf16[16,72,256]{2,1,0:T(8,128)(2,1)S(1)}, u32[]{:S(2)}, u32[]{:S(2)}) async-start(bf16[16,72,256]{2,1,0:T(8,128)(2,1)} %records_1.1), calls=%async_computation | async-start | bytes 1179648 | tf_op jit(solution)/shard_map/all_to_all | solution.py:274
  64.1 0.8 %copy-start.2 = (bf16[16,72,256]{2,1,0:T(8,128)(2,1)}, bf16[16,72,256]{2,1,0:T(8,128)(2,1)S(1)}, u32[]{:S(2)}) copy-start(bf16[16,72,256]{2,1,0:T(8,128)(2,1)S(1)} %all-to-all-done.record_ref) | copy-start | bytes 1769476

commit v11 on v10

--- a/solution.py
+++ b/solution.py
@@ -12,7 +12,7 @@
 REACH = 2
 LOW = 256
 TERMS = 11
-OWNERS = (16, 4)
+OWNERS = (8, 8)
 
 
 def slot_records(terms, window_ref, rim, *, fields, height, breadth):

time: 71.5 us -> 71.2 us (level)
  waiting for transfers between devices: 16.8 us -> 14.7 us
  Pallas kernels: 28.9 us -> 30.6 us
    all_to_all x2, waiting for transfers between devices: 14.6 us -> 12.6 us  [on_device(): lax.all_to_all(records, 'blk', split_axis=0, concat_axis=0, tiled=True)]
    pallas_call x2, Pallas kernels: 18.5 us -> 20.3 us  [on_device(): pl.pallas_call(functools.partial(record_body, start=part * half), grid_sp...]
  transfers between devices with their start and end apart: 6 -> 6, of which waited for: 3 -> 3; matrix products, arithmetic and copies ran while one was open for 1% -> 1% of each run, Pallas kernels for 17% -> 19%
where the time goes in v11:
time: 71.2 us; the launch traced here: 70.5 us
  Pallas kernels  30.6 us (43%)
  starting transfers between devices  19.7 us (28%)
  waiting for transfers between devices  14.7 us (21%)
  local copies, waits for them, and re-layouts  2.97 us (4%)
  matrix products  2.36 us (3%)
    pallas_call x2, Pallas kernels, on_device(): pl.pallas_call(functools.partial(record_body, start=part * half), grid_sp...  20.3 us
    all_to_all x2, waiting for transfers between devices, on_device(): lax.all_to_all(records, 'blk', split_axis=0, concat_axis=0, tiled=True)  12.6 us
    ppermute x4, starting transfers between devices, neighbours(): return (lax.ppermute(last, axis, up), lax.ppermute(first, axis, down))  10.7 us
    all_to_all x2, starting transfers between devices, on_device(): lax.all_to_all(records, 'blk', split_axis=0, concat_axis=0, tiled=True)  9 us
    pallas_call x1, Pallas kernels, on_device(): pl.pallas_call(functools.partial(deposit_last_body, highs=highs, padded=p...  5.29 us
    pallas_call x1, Pallas kernels, on_device(): pl.pallas_call(functools.partial(deposit_first_body, highs=highs, padded=...  5.07 us
    unnamed x16, local copies, waits for them, and re-layouts  2.82 us
    dot_general x1, matrix products, on_device(): lax.dot_general(jnp.asarray(picks, jnp.bfloat16), source_flux, (((1,), (2...  2.36 us
  transfers between devices with their start and end apart: 6, of which 3 were waited for; matrix products, arithmetic and copies ran while one was open for 1% of the time, Pallas kernels for 19%

profile of v11, /device:TPU:0, one launch (start us, length us, event | category | flops | bytes accessed | tf_op | source)
XLA Modules:
  0.0 70.5 jit_solution(9557363537345162690)
XLA Ops:
  0.0 0.0 copy-start.1
  0.0 2.4 %fusion = bf16[4,72,64]{1,0,2:T(4,128)(2,1)S(1)} fusion(bf16[4,128,1]{1,0,2:T(4,128)(2,1)} %constant.8, bf16[72,64,128]{2,1,0:T(8,128)(2,1)} %param.8), kind=kOutput, calls=%fused_computation | convolution fusion | flops 4718592 | bytes 1217536 | tf_op jit(solution)/shard_map/dot_general | solution.py:227
  2.4 0.1 copy.11
  2.5 6.4 %collective-permute-start.3 = (bf16[2,72,64]{2,1,0:T(8,128)(2,1)S(1)}, bf16[2,72,64]{2,1,0:T(8,128)(2,1)S(1)}, u32[]{:S(2)}, u32[]{:S(2)}) collective-permute-start(bf16[2,72,64]{2,1,0:T(8,128)(2,1)S(1)} %get-tuple-element.7), channel_id=1, source_target_pairs={{1,0},{2,1},{3,2},{4,3},{5,4},{6,5},{7,6},{8,7},{9,8},{10,9},{11,1... | collective-permute-start | bytes 55304 | tf_op jit(solution)/shard_map/ppermute | solution.py:210
  8.9 0.0 collective-permute-start.2
  8.9 0.0 copy-done.1
  8.9 0.8 %copy.15 = bf16[72,64,128]{2,0,1:T(8,128)(2,1)S(1)} copy(bf16[72,64,128]{2,1,0:T(8,128)(2,1)S(1)} %copy-done.1) | data formatting | bytes 2359296 | tf_op args[0]
  9.7 0.0 copy-start
  9.7 1.3 %collective-permute-start.1 = (bf16[2,72,128]{2,1,0:T(8,128)(2,1)S(1)}, bf16[2,72,128]{2,1,0:T(8,128)(2,1)S(1)}, u32[]{:S(2)}, u32[]{:S(2)}) collective-permute-start(bf16[2,72,128]{2,1,0:T(8,128)(2,1)S(1)} %get-tuple-element.5), channel_id=1, source_target_pairs={{16,0},{32,16},{48,32},{64,48},{80,64},{96,80},{112,96},{17,1},{33... | collective-permute-start | bytes 110600 | tf_op jit(solution)/shard_map/ppermute | solution.py:210
  11.0 3.0 %collective-permute-start = (bf16[2,72,128]{2,1,0:T(8,128)(2,1)S(1)}, bf16[2,72,128]{2,1,0:T(8,128)(2,1)S(1)}, u32[]{:S(2)}, u32[]{:S(2)}) collective-permute-start(bf16[2,72,128]{2,1,0:T(8,128)(2,1)S(1)} %get-tuple-element.6), channel_id=1, source_target_pairs={{0,16},{16,32},{32,48},{48,64},{64,80},{80,96},{96,112},{1,17},{17... | collective-permute-start | bytes 110600 | tf_op jit(solution)/shard_map/ppermute | solution.py:210
  14.0 2.1 %collective-permute-done.2 = bf16[2,72,64]{2,1,0:T(8,128)(2,1)S(1)} collective-permute-done((bf16[2,72,64]{2,1,0:T(8,128)(2,1)S(1)}, bf16[2,72,64]{2,1,0:T(8,128)(2,1)S(1)}, u32[]{:S(2)}, u32[]{:S(2)}) %collective-permute-start.2) | collective-permute-done | bytes 18464 | tf_op jit(solution)/shard_map/ppermute | solution.py:210
  16.2 0.0 collective-permute-done.3
  16.2 0.0 copy-start.4
  16.2 0.0 collective-permute-done.1.below_ref
  16.2 0.0 copy-start.5
  16.2 0.0 collective-permute-done.above_ref
  16.2 0.0 copy-done
  16.2 0.6 copy-done.4
  16.8 0.0 copy-done.5
  16.8 0.0 copy-start.6
  16.8 0.6 copy-done.6
  17.5 11.9 %records_0.1 = bf16[16,72,256]{2,1,0:T(8,128)(2,1)} custom-call(s32[16]{0:T(128)} %count_ref.3, bf16[64,72,128]{2,1,0:T(8,128)(2,1)} %bitcast.7, bf16[2,72,128]{2,1,0:T(8,128)(2,1)} %copy-done.6, bf16[2,72,128]{2,1,0:T(8,128)(2,1)} %copy-done.5, bf16[4,72,64]{2,1,0:T(8,128)(2,1)} %copy-done.4, f32[4,16,512]{2,1,0:T(8,128)} %weight_ref.3, ...), custom_call_target="tpu_custom_call" | custom-call | tf_op jit(solution)/shard_map/records_0/pallas_call | solution.py:239
  29.3 4.8 %all-to-all-start.1 = ((bf16[16,72,256]{2,1,0:T(8,128)(2,1)}), bf16[16,72,256]{2,1,0:T(8,128)(2,1)S(1)}, u32[]{:S(2)}, u32[]{:S(2)}) async-start(bf16[16,72,256]{2,1,0:T(8,128)(2,1)} %records_0.1), calls=%async_computation.1 | async-start | bytes 1179648 | tf_op jit(solution)/shard_map/all_to_all | solution.py:274
  34.1 8.4 %records_1.1 = bf16[16,72,256]{2,1,0:T(8,128)(2,1)} custom-call(s32[16]{0:T(128)} %count_ref.3, bf16[64,72,128]{2,1,0:T(8,128)(2,1)} %bitcast.8, bf16[2,72,128]{2,1,0:T(8,128)(2,1)} %copy-done.6, bf16[2,72,128]{2,1,0:T(8,128)(2,1)} %copy-done.5, bf16[4,72,64]{2,1,0:T(8,128)(2,1)} %copy-done.4, f32[4,16,512]{2,1,0:T(8,128)} %weight_ref.3, ...), custom_call_target="tpu_custom_call" | custom-call | tf_op jit(solution)/shard_map/records_1/pallas_call | solution.py:239
  42.5 5.5 %all-to-all-done.1.record_ref = bf16[16,72,256]{2,1,0:T(8,128)(2,1)S(1)} async-done(((bf16[16,72,256]{2,1,0:T(8,128)(2,1)}), bf16[16,72,256]{2,1,0:T(8,128)(2,1)S(1)}, u32[]{:S(2)}, u32[]{:S(2)}) %all-to-all-start.1) | async-done | bytes 589856 | tf_op jit(solution)/shard_map/all_to_all | solution.py:274
  48.1 0.0 copy-start.3
  48.1 4.2 %all-to-all-start = ((bf16[16,72,256]{2,1,0:T(8,128)(2,1)}), bf16[16,72,256]{2,1,0:T(8,128)(2,1)S(1)}, u32[]{:S(2)}, u32[]{:S(2)}) async-start(bf16[16,72,256]{2,1,0:T(8,128)(2,1)} %records_1.1), calls=%async_computation | async-start | bytes 1179648 | tf_op jit(solution)/shard_map/all_to_all | solution.py:274
  52.3 0.0 copy-done.3
  52.3 5.1 %deposit_0.1.before_ref = f32[1280,256]{1,0:T(8,128)} custom-call(bf16[16,72,256]{2,1,0:T(8,128)(2,1)} %copy-done.3, s32[16,512]{1,0:T(8,128)} %target_ref.3), custom_call_target="tpu_custom_call" | custom-call | tf_op jit(solution)/shard_map/deposit_0/pallas_call | solution.py:280
  57.4 7.0 %all-to-all-done.record_ref = bf16[16,72,256]{2,1,0:T(8,128)(2,1)S(1)} async-done(((bf16[16,72,256]{2,1,0:T(8,128)(2,1)}), bf16[16,72,256]{2,1,0:T(8,128)(2,1)S(1)}, u32[]{:S(2)}, u32[]{:S(2)}) %all-to-all-start) | async-done | bytes 589856 | tf_op jit(solution)/shard_map/all_to_all | solution.py:274
  64.4 0.0 copy-start.2
  64.4 0.8 %copy-done.2 = bf16[16,72,256]{2,1,0:T(8,128)(2,1)} copy-done((bf16[16,72,256]{2,1,0:T(8,128)(2,1)}, bf16[16,72,256]{2,1,0:T(8,128)(2,1)S(1)}, u32[]{:S(2)}) %copy-start.2) | copy-done | bytes 589848
  65.2 5.3 %deposit_1.1 = bf16[72,4096]{1,0:T(8,128)(2,1)} custom-call(bf16[16,72,256]{2,1,0:T(8,128)(2,1)} %copy-done.2, s32[16,512]{1,0:T(8,128)} %target_ref.3, f32[1280,256]{1,0:T(8,128)} %deposit_0.1.before_ref, f32[1,4096]{1,0:T(1,128)} %bitcast.9), custom_call_target="tpu_custom_call" | custom-call | tf_op jit(solution)/shard_map/deposit_1/pallas_call | solution.py:288
  (4 shorter events, 0.0 us)
Async XLA Ops:
  0.0 8.9 %copy-start.1 = (bf16[72,64,128]{2,1,0:T(8,128)(2,1)S(1)}, bf16[72,64,128]{2,1,0:T(8,128)(2,1)}, u32[]{:S(2)}) copy-start(bf16[72,64,128]{2,1,0:T(8,128)(2,1)} %param.8) | copy-start | bytes 3538948
  2.5 13.7 %collective-permute-start.3 = (bf16[2,72,64]{2,1,0:T(8,128)(2,1)S(1)}, bf16[2,72,64]{2,1,0:T(8,128)(2,1)S(1)}, u32[]{:S(2)}, u32[]{:S(2)}) collective-permute-start(bf16[2,72,64]{2,1,0:T(8,128)(2,1)S(1)} %get-tuple-element.7), channel_id=1, source_target_pairs={{1,0},{2,1},{3,2},{4,3},{5,4},{6,5},{7,6},{8,7},{9,8},{10,9},{11,1... | collective-permute-start | bytes 55304 | tf_op jit(solution)/shard_map/ppermute | solution.py:210
  8.9 7.3 %collective-permute-start.2 = (bf16[2,72,64]{2,1,0:T(8,128)(2,1)S(1)}, bf16[2,72,64]{2,1,0:T(8,128)(2,1)S(1)}, u32[]{:S(2)}, u32[]{:S(2)}) collective-permute-start(bf16[2,72,64]{2,1,0:T(8,128)(2,1)S(1)} %get-tuple-element.8), channel_id=1, source_target_pairs={{0,1},{1,2},{2,3},{3,4},{4,5},{5,6},{6,7},{7,8},{8,9},{9,10},{10,1... | collective-permute-start | bytes 55304 | tf_op jit(solution)/shard_map/ppermute | solution.py:210
  9.7 6.6 %copy-start = (bf16[72,64,128]{2,0,1:T(8,128)(2,1)}, bf16[72,64,128]{2,0,1:T(8,128)(2,1)S(1)}, u32[]{:S(2)}) copy-start(bf16[72,64,128]{2,0,1:T(8,128)(2,1)S(1)} %copy.15) | copy-start | bytes 3538948
  9.7 6.5 %collective-permute-start.1 = (bf16[2,72,128]{2,1,0:T(8,128)(2,1)S(1)}, bf16[2,72,128]{2,1,0:T(8,128)(2,1)S(1)}, u32[]{:S(2)}, u32[]{:S(2)}) collective-permute-start(bf16[2,72,128]{2,1,0:T(8,128)(2,1)S(1)} %get-tuple-element.5), channel_id=1, source_target_pairs={{16,0},{32,16},{48,32},{64,48},{80,64},{96,80},{112,96},{17,1},{33... | collective-permute-start | bytes 110600 | tf_op jit(solution)/shard_map/ppermute | solution.py:210
  11.0 5.2 %collective-permute-start = (bf16[2,72,128]{2,1,0:T(8,128)(2,1)S(1)}, bf16[2,72,128]{2,1,0:T(8,128)(2,1)S(1)}, u32[]{:S(2)}, u32[]{:S(2)}) collective-permute-start(bf16[2,72,128]{2,1,0:T(8,128)(2,1)S(1)} %get-tuple-element.6), channel_id=1, source_target_pairs={{0,16},{16,32},{32,48},{48,64},{64,80},{80,96},{96,112},{1,17},{17... | collective-permute-start | bytes 110600 | tf_op jit(solution)/shard_map/ppermute | solution.py:210
  16.2 0.6 copy-start.4
  16.2 0.6 copy-start.5
  16.8 0.6 copy-start.6
  29.3 18.7 %all-to-all-start.1 = ((bf16[16,72,256]{2,1,0:T(8,128)(2,1)}), bf16[16,72,256]{2,1,0:T(8,128)(2,1)S(1)}, u32[]{:S(2)}, u32[]{:S(2)}) async-start(bf16[16,72,256]{2,1,0:T(8,128)(2,1)} %records_0.1), calls=%async_computation.1 | async-start | bytes 1179648 | tf_op jit(solution)/shard_map/all_to_all | solution.py:274
  48.1 4.2 %copy-start.3 = (bf16[16,72,256]{2,1,0:T(8,128)(2,1)}, bf16[16,72,256]{2,1,0:T(8,128)(2,1)S(1)}, u32[]{:S(2)}) copy-start(bf16[16,72,256]{2,1,0:T(8,128)(2,1)S(1)} %all-to-all-done.1.record_ref) | copy-start | bytes 1769476
  48.1 16.4 %all-to-all-start = ((bf16[16,72,256]{2,1,0:T(8,128)(2,1)}), bf16[16,72,256]{2,1,0:T(8,128)(2,1)S(1)}, u32[]{:S(2)}, u32[]{:S(2)}) async-start(bf16[16,72,256]{2,1,0:T(8,128)(2,1)} %records_1.1), calls=%async_computation | async-start | bytes 1179648 | tf_op jit(solution)/shard_map/all_to_all | solution.py:274
  64.4 0.8 %copy-start.2 = (bf16[16,72,256]{2,1,0:T(8,128)(2,1)}, bf16[16,72,256]{2,1,0:T(8,128)(2,1)S(1)}, u32[]{:S(2)}) copy-start(bf16[16,72,256]{2,1,0:T(8,128)(2,1)S(1)} %all-to-all-done.record_ref) | copy-start | bytes 1769476
